TPU v7x, 32 devices: a whole 2x2x4 slice. The times are simulated.
32 devices in a mesh: dp: 16 (over z, y, core), mp: 2 (over x).
Axes of the slice: x: 2, y: 2, z: 4, core: 2. Of those that a mesh axis runs over, the one named last changes fastest.
Arguments:
- hidden_in: bfloat16 [32768, 1024], P(('dp', 'mp')), may hold values from -6 to 6
- out_grad: bfloat16 [32768, 1024], P(('dp', 'mp')), may hold values from -6 to 6
- ln1_gain: float32 [1024], replicated, may hold values from 0.5 to 1.5
- ln1_bias: float32 [1024], replicated, may hold values from -3 to 3
- w_query: bfloat16 [1024, 1024], P(None, 'mp'), may hold values from -0.1875 to 0.1875
- w_key: bfloat16 [1024, 1024], P(None, 'mp'), may hold values from -0.1875 to 0.1875
- w_value: bfloat16 [1024, 1024], P(None, 'mp'), may hold values from -0.1875 to 0.1875
- w_out: bfloat16 [1024, 1024], P('mp'), may hold values from -1.5 to 1.5
- ln2_gain: float32 [1024], replicated, may hold values from 0.5 to 1.5
- ln2_bias: float32 [1024], replicated, may hold values from -3 to 3
- w_up: bfloat16 [1024, 4096], P(None, 'mp'), may hold values from -0.1875 to 0.1875
- b_up: float32 [4096], P('mp'), may hold values from -3 to 3
- w_down: bfloat16 [4096, 1024], P('mp'), may hold values from -0.09375 to 0.09375
- b_down: float32 [1024], replicated, may hold values from -3 to 3
- rand_blocks: int32 [16, 16, 3], P('mp'), may hold values from 0 to 15
Outputs:
- output: bfloat16 [32768, 1024], P(('dp', 'mp'))
- input_grad: float32 [32768, 1024], P(('dp', 'mp'))
- grad_ln1_gain: float32 [1024], replicated
- grad_ln1_bias: float32 [1024], replicated
- grad_w_query: float32 [1024, 1024], P(None, 'mp')
- grad_w_key: float32 [1024, 1024], P(None, 'mp')
- grad_w_value: float32 [1024, 1024], P(None, 'mp')
- grad_w_out: float32 [1024, 1024], P('mp')
- grad_ln2_gain: float32 [1024], replicated
- grad_ln2_bias: float32 [1024], replicated
- grad_w_up: float32 [1024, 4096], P(None, 'mp')
- grad_b_up: float32 [4096], P('mp')
- grad_w_down: float32 [4096, 1024], P('mp')
- grad_b_down: float32 [1024], replicated
Inputs may be any that keep to these rules, and one draw needn't show every extreme that they name: rand_blocks[h, i, r] is a key block of the same sequence; entries may repeat or fall on window or global blocks, and those of the first and last query blocks have no effect.
All inputs are finite; a program needn't handle non-finite values.
Results may differ from a plain program's by a relative error of at most 0.02.
Values may be sent and summed in bfloat16 or wider, within the bound.
A program may use at most 320 MiB of HBM per device.

v0:
```python
import jax
import jax.numpy as jnp
from jax import lax
from jax.sharding import PartitionSpec as P

HD = 64
BLOCK = 64
SEQ = 1024


def layer_norm(values, norm_gain, norm_bias):
    center = values - jnp.mean(values, axis=-1, keepdims=True)
    spread = jnp.mean(center * center, axis=-1, keepdims=True)
    return center * lax.rsqrt(spread + 1e-05) * norm_gain + norm_bias


def block_mask(rand_blocks):
    blocks = SEQ // BLOCK
    row_ids = jnp.arange(blocks)[:, None]
    col_ids = jnp.arange(blocks)[None, :]
    window = (
        (jnp.abs(row_ids - col_ids) <= 1)
        | (col_ids == 0)
        | (col_ids == blocks - 1)
        | (row_ids == 0)
        | (row_ids == blocks - 1)
    )
    picked = jnp.any(rand_blocks[:, :, :, None] == jnp.arange(blocks)[None, None, None, :], axis=2)
    allowed = window[None] | picked
    return jnp.repeat(jnp.repeat(allowed, BLOCK, axis=1), BLOCK, axis=2)


def attend_forward(joined_seq, allowed, scaling):
    queries = joined_seq[:, 0]
    key_rows = joined_seq[:, 1]
    value_rows = joined_seq[:, 2]
    scores = (
        jnp.einsum("qhd,khd->hqk", queries, key_rows, preferred_element_type=jnp.float32) * scaling
    )
    scores = jnp.where(allowed, scores, -1e30)
    highest = jnp.max(scores, axis=-1, keepdims=True)
    shifted = jnp.exp(scores - highest)
    row_totals = jnp.sum(shifted, axis=-1, keepdims=True)
    attn_probs = (shifted / row_totals).astype(jnp.bfloat16)
    context = jnp.einsum("hqk,khd->qhd", attn_probs, value_rows, preferred_element_type=jnp.float32)
    return (context.astype(jnp.bfloat16), (highest + jnp.log(row_totals))[..., 0])


def attend_backward(seq_items, allowed, scaling):
    joined_seq, grad_context, row_lse = seq_items
    queries = joined_seq[:, 0]
    key_rows = joined_seq[:, 1]
    value_rows = joined_seq[:, 2]
    scores = (
        jnp.einsum("qhd,khd->hqk", queries, key_rows, preferred_element_type=jnp.float32) * scaling
    )
    scores = jnp.where(allowed, scores, -1e30)
    attn_probs = jnp.exp(scores - row_lse[..., None])
    grad_values = jnp.einsum(
        "hqk,qhd->khd",
        attn_probs.astype(jnp.bfloat16),
        grad_context,
        preferred_element_type=jnp.float32,
    ).astype(jnp.bfloat16)
    grad_probs = jnp.einsum(
        "qhd,khd->hqk", grad_context, value_rows, preferred_element_type=jnp.float32
    )
    row_inner = jnp.sum(grad_probs * attn_probs, axis=-1, keepdims=True)
    grad_scores = (attn_probs * (grad_probs - row_inner)).astype(jnp.bfloat16)
    grad_queries = (
        jnp.einsum("hqk,khd->qhd", grad_scores, key_rows, preferred_element_type=jnp.float32)
        * scaling
    ).astype(jnp.bfloat16)
    grad_keys = (
        jnp.einsum("hqk,qhd->khd", grad_scores, queries, preferred_element_type=jnp.float32)
        * scaling
    ).astype(jnp.bfloat16)
    return jnp.stack([grad_queries, grad_keys, grad_values], axis=1)


def per_device(
    hidden_in,
    out_grad,
    ln1_gain,
    ln1_bias,
    w_query,
    w_key,
    w_value,
    w_out,
    ln2_gain,
    ln2_bias,
    w_up,
    b_up,
    w_down,
    b_down,
    rand_blocks,
):
    local_heads = rand_blocks.shape[0]
    head_width = local_heads * HD
    local_rows = hidden_in.shape[0]
    seq_count = local_rows * lax.axis_size("mp") // SEQ
    scaling = HD ** (-0.5)
    allowed = block_mask(rand_blocks)
    inputs = hidden_in.astype(jnp.float32)
    w_joined = jnp.concatenate([w_query, w_key, w_value], axis=1)
    normed_one = layer_norm(inputs, ln1_gain, ln1_bias).astype(jnp.bfloat16)
    rows_one = lax.all_gather(normed_one, "mp", axis=0, tiled=True)
    joined = jnp.dot(rows_one, w_joined, preferred_element_type=jnp.float32).astype(jnp.bfloat16)
    joined_seq = joined.reshape(seq_count, SEQ, 3, local_heads, HD)
    context, row_lse = lax.map(
        lambda seq_block: attend_forward(seq_block, allowed, scaling), joined_seq
    )
    context_rows = context.reshape(seq_count * SEQ, head_width)
    middle = inputs + lax.psum_scatter(
        jnp.dot(context_rows, w_out, preferred_element_type=jnp.float32).astype(jnp.bfloat16),
        "mp",
        scatter_dimension=0,
        tiled=True,
    ).astype(jnp.float32)
    normed_two = layer_norm(middle, ln2_gain, ln2_bias).astype(jnp.bfloat16)
    rows_two = lax.all_gather(normed_two, "mp", axis=0, tiled=True)
    up_pre = jnp.dot(rows_two, w_up, preferred_element_type=jnp.float32) + b_up
    hidden = jax.nn.gelu(up_pre, approximate=True).astype(jnp.bfloat16)
    output = (
        middle
        + (
            lax.psum_scatter(
                jnp.dot(hidden, w_down, preferred_element_type=jnp.float32).astype(jnp.bfloat16),
                "mp",
                scatter_dimension=0,
                tiled=True,
            ).astype(jnp.float32)
            + b_down
        )
    ).astype(jnp.bfloat16)
    grad_out = out_grad.astype(jnp.float32)
    bias_down = jnp.sum(grad_out, axis=0)
    rows_ffn = lax.all_gather(out_grad, "mp", axis=0, tiled=True)
    grad_hidden = jnp.einsum("nd,fd->nf", rows_ffn, w_down, preferred_element_type=jnp.float32)
    grad_down = jnp.einsum("nf,nd->fd", hidden, rows_ffn, preferred_element_type=jnp.float32)
    gelu_value, gelu_pull = jax.vjp(lambda pre_act: jax.nn.gelu(pre_act, approximate=True), up_pre)
    grad_up = gelu_pull(grad_hidden)[0].astype(jnp.bfloat16)
    bias_up = jnp.sum(grad_up, axis=0, dtype=jnp.float32)
    grad_up_weight = jnp.einsum("nd,nf->df", rows_two, grad_up, preferred_element_type=jnp.float32)
    grad_normed_two = lax.psum_scatter(
        jnp.einsum("nf,df->nd", grad_up, w_up, preferred_element_type=jnp.float32).astype(
            jnp.bfloat16
        ),
        "mp",
        scatter_dimension=0,
        tiled=True,
    ).astype(jnp.float32)
    norm_value_two, norm_pull_two = jax.vjp(layer_norm, middle, ln2_gain, ln2_bias)
    grad_mid_norm, gain_two, bias_two = norm_pull_two(grad_normed_two)
    grad_middle = grad_out + grad_mid_norm
    grad_attn = grad_middle.astype(jnp.bfloat16)
    rows_attn = lax.all_gather(grad_attn, "mp", axis=0, tiled=True)
    grad_context = jnp.einsum(
        "nd,ed->ne", rows_attn, w_out, preferred_element_type=jnp.float32
    ).astype(jnp.bfloat16)
    grad_out_weight = jnp.einsum(
        "ne,nd->ed", context_rows, rows_attn, preferred_element_type=jnp.float32
    )
    grad_joined = lax.map(
        lambda seq_items: attend_backward(seq_items, allowed, scaling),
        (joined_seq, grad_context.reshape(seq_count, SEQ, local_heads, HD), row_lse),
    )
    grad_joined = grad_joined.reshape(seq_count * SEQ, 3 * head_width)
    grad_joined_weight = jnp.einsum(
        "nd,ne->de", rows_one, grad_joined, preferred_element_type=jnp.float32
    )
    grad_normed_one = lax.psum_scatter(
        jnp.einsum("ne,de->nd", grad_joined, w_joined, preferred_element_type=jnp.float32).astype(
            jnp.bfloat16
        ),
        "mp",
        scatter_dimension=0,
        tiled=True,
    ).astype(jnp.float32)
    norm_value_one, norm_pull_one = jax.vjp(layer_norm, inputs, ln1_gain, ln1_bias)
    grad_in_norm, gain_one, bias_one = norm_pull_one(grad_normed_one)
    input_grad = grad_middle + grad_in_norm
    grad_joined_weight, grad_out_weight, grad_up_weight, bias_up, grad_down = (
        lax.psum(grad_joined_weight.astype(jnp.bfloat16), "dp").astype(jnp.float32),
        lax.psum(grad_out_weight.astype(jnp.bfloat16), "dp").astype(jnp.float32),
        lax.psum(grad_up_weight.astype(jnp.bfloat16), "dp").astype(jnp.float32),
        lax.psum(bias_up.astype(jnp.bfloat16), "dp").astype(jnp.float32),
        lax.psum(grad_down.astype(jnp.bfloat16), "dp").astype(jnp.float32),
    )
    gain_one, bias_one, gain_two, bias_two, bias_down = lax.psum(
        (gain_one, bias_one, gain_two, bias_two, bias_down), ("dp", "mp")
    )
    grad_query = grad_joined_weight[:, :head_width]
    grad_key = grad_joined_weight[:, head_width : 2 * head_width]
    grad_value = grad_joined_weight[:, 2 * head_width :]
    return (
        output,
        input_grad,
        gain_one,
        bias_one,
        grad_query,
        grad_key,
        grad_value,
        grad_out_weight,
        gain_two,
        bias_two,
        grad_up_weight,
        bias_up,
        grad_down,
        bias_down,
    )


def solution(mesh):
    in_specs = (
        P(("dp", "mp"), None),
        P(("dp", "mp"), None),
        P(),
        P(),
        P(None, "mp"),
        P(None, "mp"),
        P(None, "mp"),
        P("mp", None),
        P(),
        P(),
        P(None, "mp"),
        P("mp"),
        P("mp", None),
        P(),
        P("mp", None, None),
    )
    out_specs = (
        P(("dp", "mp"), None),
        P(("dp", "mp"), None),
        P(),
        P(),
        P(None, "mp"),
        P(None, "mp"),
        P(None, "mp"),
        P("mp", None),
        P(),
        P(),
        P(None, "mp"),
        P("mp"),
        P("mp", None),
        P(),
    )
    return jax.shard_map(
        per_device, mesh=mesh, in_specs=in_specs, out_specs=out_specs, check_vma=False
    )
```

profile of v0, /device:TPU:0, one launch (start us, length us, event | category | flops | bytes accessed | tf_op | source)
XLA Modules:
  0.0 1241.2 jit_solution(840713669255894146)
XLA Ops:
  22.0 52.6 %all-gather.5.cloned.1.call-done = bf16[2048,1024]{1,0:T(8,128)(2,1)} async-done(((bf16[1024,1024]{1,0:T(8,128)(2,1)}), bf16[2048,1024]{1,0:T(8,128)(2,1)}) %all-gather.5.cloned.1.call-update) | async-done | bytes 4194320 | tf_op jit(solution)/shard_map/all_gather | solution.py:107
  74.7 11.4 convolution_convert_fusion.2
  86.1 16.3 %reshape.244 = bf16[2,1024,3,8,64]{4,3,2,1,0:T(8,128)(2,1)} reshape(bf16[2048,1536]{1,0:T(8,128)(2,1)} %convolution_convert_fusion.2) | data formatting | bytes 12582912 | tf_op jit(solution)/shard_map/reshape | solution.py:109
  102.3 14.0 %copy.56 = bf16[2,1024,3,8,64]{1,4,3,2,0:T(8,128)(2,1)} copy(bf16[2,1024,3,8,64]{4,3,2,1,0:T(8,128)(2,1)} %reshape.244) | data formatting | bytes 12582912
  116.4 113.5 %while.24 = (s32[]{:T(128)}, bf16[2,1024,8,64]{1,3,2,0:T(8,128)(2,1)}, f32[2,8,1024]{2,1,0:T(8,128)S(1)}, bf16[2,1024,3,8,64]{1,4,3,2,0:T(8,128)(2,1)}, pred[8,1024,16]{1,2,0:T(8,128)(4,1)S(1)}, /*index=5*/s32[]{:T(128)}) while((s32[]{:T(128)}, bf16[2,1024,8,64]{1,3,2,0:T(8,128)(2,1)}, f32[2,8,1024]{2,1,0:T(8,128)S(1)}, ...), condition=%wide.region_6.7_spmd.clone, body=%wide.region_3.6_spmd.clone.sunk | while | flops 2248663040 | bytes 279576704 | solution.py:110
  118.7 13.2 %fusion.101 = (f32[8,1024]{1,0:T(8,128)S(1)}, f32[8,1024,1024]{1,2,0:T(8,128)}) fusion(pred[8,1024,16]{1,2,0:T(8,128)(4,1)S(1)} %get-tuple-element.292, bf16[1024,3,8,64]{0,3,2,1:T(8,128)(2,1)S(1)} %dynamic-slice_bitcast_fusion.6), kind=kOutput, calls=%fused_computation.5.clone.1 | convolution fusion | flops 1098899456 | bytes 35815424 | tf_op jit(solution)/shard_map/while/body/eval_jaxpr/qhd,khd->hqk/dot_general | solution.py:38
  131.9 14.7 %fusion.102 = f32[8,1024]{1,0:T(8,128)S(1)} fusion(f32[8,1024,1024]{1,2,0:T(8,128)} %get-tuple-element.264, f32[8,1024]{1,0:T(8,128)S(1)} %get-tuple-element.265, pred[8,1024,16]{1,2,0:T(8,128)(4,1)S(1)} %get-tuple-element.292), kind=kLoop, calls=%fused_computation.6.clone.1 | loop fusion | flops 33546240 | bytes 33751040 | tf_op jit(solution)/shard_map/while/body/eval_jaxpr/reduce_sum | solution.py:43
  152.2 10.9 divide_convert_fusion.2
  163.1 9.8 fusion.103
  175.3 13.2 %fusion.101 = (f32[8,1024]{1,0:T(8,128)S(1)}, f32[8,1024,1024]{1,2,0:T(8,128)}) fusion(pred[8,1024,16]{1,2,0:T(8,128)(4,1)S(1)} %get-tuple-element.292, bf16[1024,3,8,64]{0,3,2,1:T(8,128)(2,1)S(1)} %dynamic-slice_bitcast_fusion.6), kind=kOutput, calls=%fused_computation.5.clone.1 | convolution fusion | flops 1098899456 | bytes 35815424 | tf_op jit(solution)/shard_map/while/body/eval_jaxpr/qhd,khd->hqk/dot_general | solution.py:38
  188.4 14.7 %fusion.102 = f32[8,1024]{1,0:T(8,128)S(1)} fusion(f32[8,1024,1024]{1,2,0:T(8,128)} %get-tuple-element.264, f32[8,1024]{1,0:T(8,128)S(1)} %get-tuple-element.265, pred[8,1024,16]{1,2,0:T(8,128)(4,1)S(1)} %get-tuple-element.292), kind=kLoop, calls=%fused_computation.6.clone.1 | loop fusion | flops 33546240 | bytes 33751040 | tf_op jit(solution)/shard_map/while/body/eval_jaxpr/reduce_sum | solution.py:43
  208.7 10.9 divide_convert_fusion.2
  219.6 9.8 fusion.103
  240.1 54.4 %reduce-scatter.5.cloned.1.call-done = bf16[1024,1024]{1,0:T(8,128)(2,1)} async-done(((bf16[2048,1024]{1,0:T(8,128)(2,1)}), bf16[1024,1024]{1,0:T(8,128)(2,1)}) %reduce-scatter.5.cloned.1.call-update) | async-done | bytes 2097168 | tf_op jit(solution)/shard_map/reduce_scatter | solution.py:114
  300.9 56.3 %all-gather.7.cloned.1.call-done = bf16[2048,1024]{1,0:T(8,128)(2,1)} async-done(((bf16[1024,1024]{1,0:T(8,128)(2,1)}), bf16[2048,1024]{1,0:T(8,128)(2,1)}) %all-gather.7.cloned.1.call-update) | async-done | bytes 4194320 | tf_op jit(solution)/shard_map/all_gather | solution.py:121
  357.2 20.6 %multiply_convert_fusion.3 = (bf16[2048,2048]{1,0:T(8,128)(2,1)}, f32[2048,2048]{1,0:T(8,128)}) fusion(f32[2048]{0:T(1024)S(1)} %copy-done.44, bf16[2048,1024]{1,0:T(8,128)(2,1)} %all-gather.7.cloned.1.call-done, bf16[1024,2048]{1,0:T(8,128)(2,1)} %param.29), kind=kOutput, calls=%fused_computation.50 | convolution fusion | flops 8631877632 | bytes 33562624 | tf_op jit(solution)/shard_map/dot_general | solution.py:122
  377.8 37.6 %all-gather.9.cloned.1.call-done = bf16[2048,1024]{1,0:T(8,128)(2,1)} async-done(((bf16[1024,1024]{1,0:T(8,128)(2,1)}), bf16[2048,1024]{1,0:T(8,128)(2,1)}) %all-gather.9.cloned.1.call-update) | async-done | bytes 4194320 | tf_op jit(solution)/shard_map/all_gather | solution.py:138
  415.4 28.1 %fusion.55 = (bf16[2048]{0:T(1024)(128)(2,1)}, bf16[2048,2048]{1,0:T(8,128)(2,1)}) fusion(f32[2048,2048]{1,0:T(8,128)} %get-tuple-element.193, f32[2048]{0:T(1024)S(1)} %copy-done.44, bf16[2048,1024]{1,0:T(8,128)(2,1)} %all-gather.9.cloned.1.call-done, bf16[2048,1024]{1,0:T(8,128)(2,1)} %param.31), kind=kOutput, calls=%fused_computation.120 | convolution fusion | flops 8682207232 | bytes 33566720 | tf_op jit(solution)/shard_map/nd,fd->nf/dot_general | solution.py:139
  443.5 12.9 %convolution_convert_fusion.6 = bf16[2048,1024]{1,0:T(8,128)(2,1)} fusion(bf16[2048,2048]{1,0:T(8,128)(2,1)} %get-tuple-element.177, bf16[1024,2048]{1,0:T(8,128)(2,1)S(1)} %copy-done.41), kind=kOutput, calls=%fused_computation.87 | convolution fusion | flops 8592031744 | bytes 16777216 | tf_op jit(solution)/shard_map/nf,df->nd/dot_general | solution.py:146
  456.5 13.8 %convolution_convert_fusion.7 = bf16[2048,1024]{1,0:T(8,128)(2,1)} fusion(bf16[2048,2048]{1,0:T(8,128)(2,1)} %get-tuple-element.192, bf16[2048,1024]{1,0:T(8,128)(2,1)} %param.31), kind=kOutput, calls=%fused_computation.88 | convolution fusion | flops 8592031744 | bytes 16777216 | tf_op jit(solution)/shard_map/dot_general | solution.py:128
  470.4 40.5 %reduce-scatter.9.cloned.1.call-done = bf16[1024,1024]{1,0:T(8,128)(2,1)} async-done(((bf16[2048,1024]{1,0:T(8,128)(2,1)}), bf16[1024,1024]{1,0:T(8,128)(2,1)}) %reduce-scatter.9.cloned.1.call-update) | async-done | bytes 2097168 | tf_op jit(solution)/shard_map/reduce_scatter | solution.py:145
  515.3 52.0 %reduce-scatter.7.cloned.1.call-done = bf16[1024,1024]{1,0:T(8,128)(2,1)} async-done(((bf16[2048,1024]{1,0:T(8,128)(2,1)}), bf16[1024,1024]{1,0:T(8,128)(2,1)}) %reduce-scatter.7.cloned.1.call-update) | async-done | bytes 2097168 | tf_op jit(solution)/shard_map/reduce_scatter | solution.py:127
  567.4 5.5 fusion.57
  576.9 14.7 %convolution_convert_fusion.9 = bf16[2048,1024]{1,0:T(8,128)(2,1)} fusion(bf16[2048,2048]{1,0:T(8,128)(2,1)} %get-tuple-element.192, bf16[2048,1024]{1,0:T(8,128)(2,1)} %all-gather.9.cloned.1.call-done), kind=kOutput, calls=%fused_computation.90 | convolution fusion | flops 8592031744 | bytes 16777216 | tf_op jit(solution)/shard_map/nf,nd->fd/dot_general | solution.py:140
  591.6 13.1 %convolution_convert_fusion.5 = bf16[1024,2048]{1,0:T(8,128)(2,1)} fusion(bf16[2048,1024]{1,0:T(8,128)(2,1)S(1)} %copy-done.43, bf16[2048,2048]{1,0:T(8,128)(2,1)} %get-tuple-element.177), kind=kOutput, calls=%fused_computation.86 | convolution fusion | flops 8592031744 | bytes 16777216 | tf_op jit(solution)/shard_map/nd,nf->df/dot_general | solution.py:144
  604.7 29.0 %all-gather.11.cloned.1.call-done = bf16[2048,1024]{1,0:T(8,128)(2,1)} async-done(((bf16[1024,1024]{1,0:T(8,128)(2,1)}), bf16[2048,1024]{1,0:T(8,128)(2,1)}) %all-gather.11.cloned.1.call-update) | async-done | bytes 4194320 | tf_op jit(solution)/shard_map/all_gather | solution.py:157
  647.3 213.0 %while.25 = (s32[]{:T(128)}, bf16[2,1024,3,8,64]{1,4,3,2,0:T(8,128)(2,1)}, bf16[2,1024,3,8,64]{1,4,3,2,0:T(8,128)(2,1)}, f32[2,8,1024]{2,1,0:T(8,128)S(1)}, bf16...) while((s32[]{:T(128)}, ...), condition=%wide.region_16.17_spmd.clone, body=%wide.region_14.16_spmd.clone.sunk | while | flops 5481422848 | bytes 287768704 | solution.py:164
  649.7 13.1 %fusion.108 = f32[8,1024,1024]{1,2,0:T(8,128)} fusion(bf16[1024,3,8,64]{0,3,2,1:T(8,128)(2,1)S(1)} %dynamic-slice_bitcast_fusion.7), kind=kOutput, calls=%fused_computation.35.clone.1 | convolution fusion | flops 1073741824 | bytes 35651584 | tf_op jit(solution)/shard_map/while/body/eval_jaxpr/qhd,khd->hqk/dot_general | solution.py:55
  662.9 23.8 %multiply_reduce_fusion.3 = (f32[8,1024]{1,0:T(8,128)S(1)}, f32[8,1024,1024]{1,2,0:T(8,128)}) fusion(f32[8,1024,1024]{1,2,0:T(8,128)} %fusion.108, f32[8,1024]{1,0:T(8,128)S(1)} %dynamic-slice_bitcast_fusion.8, pred[8,1024,16]{1,2,0:T(8,128)(4,1)S(1)} %get-tuple-element.313, bf16[1024,3,8,64]{0,3,2,1:T(8,128)(2,1)S(1)} %dynamic-slice_bitcast_fusion.7, ...), kind=kOutput, calls=%fused_computation.17.clone.1 | convolution fusion | flops 1115676672 | bytes 69402624 | tf_op jit(solution)/shard_map/while/body/eval_jaxpr/qhd,khd->hqk/dot_general | solution.py:65
  686.7 33.3 %multiply_convert_fusion.5 = (bf16[8,1024,1024]{1,2,0:T(8,128)(2,1)}, bf16[8,1024,1024]{1,2,0:T(8,128)(2,1)}) fusion(f32[8,1024,1024]{1,2,0:T(8,128)} %get-tuple-element.272, f32[8,1024,1024]{1,2,0:T(8,128)} %fusion.108, f32[8,1024]{1,0:T(8,128)S(1)} %get-tuple-element.273, f32[8,1024]{1,0:T(8,128)S(1)} %dynamic-slice_bitcast_fusion.8, ...), kind=kLoop, calls=%fused_computation.16.clone.1 | loop fusion | flops 58720256 | bytes 100859904 | tf_op jit(solution)/shard_map/while/body/eval_jaxpr/convert_element_type | solution.py:69
  720.0 11.3 fusion.109
  731.3 9.1 fusion.111
  740.5 11.3 fusion.110
  756.1 13.1 %fusion.108 = f32[8,1024,1024]{1,2,0:T(8,128)} fusion(bf16[1024,3,8,64]{0,3,2,1:T(8,128)(2,1)S(1)} %dynamic-slice_bitcast_fusion.7), kind=kOutput, calls=%fused_computation.35.clone.1 | convolution fusion | flops 1073741824 | bytes 35651584 | tf_op jit(solution)/shard_map/while/body/eval_jaxpr/qhd,khd->hqk/dot_general | solution.py:55
  769.2 23.8 %multiply_reduce_fusion.3 = (f32[8,1024]{1,0:T(8,128)S(1)}, f32[8,1024,1024]{1,2,0:T(8,128)}) fusion(f32[8,1024,1024]{1,2,0:T(8,128)} %fusion.108, f32[8,1024]{1,0:T(8,128)S(1)} %dynamic-slice_bitcast_fusion.8, pred[8,1024,16]{1,2,0:T(8,128)(4,1)S(1)} %get-tuple-element.313, bf16[1024,3,8,64]{0,3,2,1:T(8,128)(2,1)S(1)} %dynamic-slice_bitcast_fusion.7, ...), kind=kOutput, calls=%fused_computation.17.clone.1 | convolution fusion | flops 1115676672 | bytes 69402624 | tf_op jit(solution)/shard_map/while/body/eval_jaxpr/qhd,khd->hqk/dot_general | solution.py:65
  793.1 33.3 %multiply_convert_fusion.5 = (bf16[8,1024,1024]{1,2,0:T(8,128)(2,1)}, bf16[8,1024,1024]{1,2,0:T(8,128)(2,1)}) fusion(f32[8,1024,1024]{1,2,0:T(8,128)} %get-tuple-element.272, f32[8,1024,1024]{1,2,0:T(8,128)} %fusion.108, f32[8,1024]{1,0:T(8,128)S(1)} %get-tuple-element.273, f32[8,1024]{1,0:T(8,128)S(1)} %dynamic-slice_bitcast_fusion.8, ...), kind=kLoop, calls=%fused_computation.16.clone.1 | loop fusion | flops 58720256 | bytes 100859904 | tf_op jit(solution)/shard_map/while/body/eval_jaxpr/convert_element_type | solution.py:69
  826.4 11.3 fusion.109
  837.7 9.1 fusion.111
  846.8 11.3 fusion.110
  860.4 11.9 copy.61
  875.0 7.8 convolution_convert_fusion.11
  882.8 8.2 convolution_convert_fusion.3
  891.1 11.9 convolution_convert_fusion.4
  903.7 35.2 %psum.77 = bf16[2048]{0:T(1024)(128)(2,1)S(1)} all-reduce(bf16[2048]{0:T(1024)(128)(2,1)S(1)} %copy-done.38), channel_id=1, replica_groups=mesh['dp'=16,'mp'=2] {'dp'}, use_global_device_ids=true, to_apply=%region_32.33 | all-reduce | flops 2048 | bytes 8192 | tf_op jit(solution)/shard_map/psum | solution.py:187
  939.5 186.7 %all-reduce.4.cloned.1.call-done = (bf16[1024,1536]{1,0:T(8,128)(2,1)}, bf16[512,1024]{1,0:T(8,128)(2,1)}, bf16[1024,2048]{1,0:T(8,128)(2,1)}, bf16[2048,1024]{1,0:T(8,128)(2,1)}) async-done(((bf16[1024,1536]{1,0:T(8,128)(2,1)}, bf16[512,1024]{1,0:T(8,128)(2,1)}, bf16[1024,2048]{1,0:T(8,128)(2,1)}, bf16[2048,1024]{1,0:T(8,128)(2,1)}), (bf16[1024,1536]{1,0:T(8,128)(2,1)}, bf16[512,1024]{1,0:T(8,128)(2,1)}, ...) | async-done | bytes 12582928 | tf_op jit(solution)/shard_map/psum | solution.py:184
  1129.0 6.9 convert_element_type.139
  1143.3 40.2 %reduce-scatter.11.cloned.1.call-done = bf16[1024,1024]{1,0:T(8,128)(2,1)} async-done(((bf16[2048,1024]{1,0:T(8,128)(2,1)}), bf16[1024,1024]{1,0:T(8,128)(2,1)}) %reduce-scatter.11.cloned.1.call-update) | async-done | bytes 2097168 | tf_op jit(solution)/shard_map/reduce_scatter | solution.py:172
  1194.4 39.8 %all-reduce = (f32[1024]{0:T(1024)}, f32[1024]{0:T(1024)}, f32[1024]{0:T(1024)}, f32[1024]{0:T(1024)}, f32[1024]{0:T(1024)}) all-reduce(f32[1024]{0:T(1024)S(1)} %get-tuple-element.140, f32[1024]{0:T(1024)S(1)} %get-tuple-element.143, f32[1024]{0:T(1024)S(1)} %copy-done.34, ...), channel_id=1, replica_groups=mesh['dp'=16,'mp'=2] {'dp','mp'}, use_global_device_ids=true, to_apply=%region_21.22 | all-reduce | flops 5120 | bytes 40960 | tf_op jit(solution)/shard_map/psum | solution.py:190
  (166 shorter events, 102.7 us)
Async XLA Ops:
  7.2 228.5 %copy-start = (bf16[512,1024]{1,0:T(8,128)(2,1)S(1)}, bf16[512,1024]{1,0:T(8,128)(2,1)}, u32[]{:S(2)}) copy-start(bf16[512,1024]{1,0:T(8,128)(2,1)} %param.26) | copy-start | bytes 3145732
  7.2 5.7 copy-start.4
  7.2 5.7 copy-start.27
  7.2 5.7 copy-start.39
  7.2 67.4 %all-gather.5.cloned.1.call-start = ((), (), s32[]{:S(2)}) async-start(), calls=%async_computation.4 | async-start | bytes 6291456 | tf_op jit(solution)/shard_map/all_gather | solution.py:107
  9.4 2.9 copy-start.23
  9.4 5.7 copy-start.36
  15.0 3.5 copy-start.20
  15.1 279.5 %reduce-scatter.5.cloned.1.call-start = ((), (), s32[]{:S(2)}) async-start(), calls=%async_computation.5 | async-start | bytes 6291456 | tf_op jit(solution)/shard_map/reduce_scatter | solution.py:114
  131.9 20.3 %copy-start.2 = (f32[8,1024,1024]{1,2,0:T(8,128)S(1)}, f32[8,1024,1024]{1,2,0:T(8,128)}, u32[]{:S(2)}) copy-start(f32[8,1024,1024]{1,2,0:T(8,128)} %get-tuple-element.264) | copy-start | bytes 100663296 | tf_op jit(solution)/shard_map/while
  188.4 20.3 %copy-start.2 = (f32[8,1024,1024]{1,2,0:T(8,128)S(1)}, f32[8,1024,1024]{1,2,0:T(8,128)}, u32[]{:S(2)}) copy-start(f32[8,1024,1024]{1,2,0:T(8,128)} %get-tuple-element.264) | copy-start | bytes 100663296 | tf_op jit(solution)/shard_map/while
  229.8 4.4 copy-start.7
  229.8 4.4 copy-start.21
  240.0 54.5 %copy-start.5 = (bf16[1024,1024]{1,0:T(8,128)(2,1)S(1)}, bf16[1024,1024]{1,0:T(8,128)(2,1)}, u32[]{:S(2)}) copy-start(bf16[1024,1024]{1,0:T(8,128)(2,1)} %param.19) | copy-start | bytes 6291460
  240.1 57.8 %copy-start.33 = (f32[1024]{0:T(1024)S(1)}, f32[1024]{0:T(1024)}, u32[]{:S(2)}) copy-start(f32[1024]{0:T(1024)} %param.27) | copy-start | bytes 12292
  240.1 57.8 %copy-start.37 = (f32[1024]{0:T(1024)S(1)}, f32[1024]{0:T(1024)}, u32[]{:S(2)}) copy-start(f32[1024]{0:T(1024)} %param.28) | copy-start | bytes 12292
  240.1 117.1 %all-gather.7.cloned.1.call-start = ((), (), s32[]{:S(2)}) async-start(), calls=%async_computation.6 | async-start | bytes 6291456 | tf_op jit(solution)/shard_map/all_gather | solution.py:121
  297.8 59.3 %copy-start.44 = (f32[2048]{0:T(1024)S(1)}, f32[2048]{0:T(1024)}, u32[]{:S(2)}) copy-start(f32[2048]{0:T(1024)} %param.30) | copy-start | bytes 24580
  300.2 115.2 %all-gather.9.cloned.1.call-start = ((), (), s32[]{:S(2)}) async-start(), calls=%async_computation.8 | async-start | bytes 6291456 | tf_op jit(solution)/shard_map/all_gather | solution.py:138
  300.8 210.1 %reduce-scatter.9.cloned.1.call-start = ((), (), s32[]{:S(2)}) async-start(), calls=%async_computation.9 | async-start | bytes 6291456 | tf_op jit(solution)/shard_map/reduce_scatter | solution.py:145
  415.4 28.1 %copy-start.41 = (bf16[1024,2048]{1,0:T(8,128)(2,1)S(1)}, bf16[1024,2048]{1,0:T(8,128)(2,1)}, u32[]{:S(2)}) copy-start(bf16[1024,2048]{1,0:T(8,128)(2,1)} %param.29) | copy-start | bytes 12582916
  456.4 110.9 %reduce-scatter.7.cloned.1.call-start = ((), (), s32[]{:S(2)}) async-start(), calls=%async_computation.7 | async-start | bytes 6291456 | tf_op jit(solution)/shard_map/reduce_scatter | solution.py:127
  470.3 97.0 %copy-start.40 = (f32[1024]{0:T(1024)S(1)}, f32[1024]{0:T(1024)}, u32[]{:S(2)}) copy-start(f32[1024]{0:T(1024)} %param.32) | copy-start | bytes 12292
  470.3 163.4 %all-gather.11.cloned.1.call-start = ((), (), s32[]{:S(2)}) async-start(), calls=%async_computation.10 | async-start | bytes 6291456 | tf_op jit(solution)/shard_map/all_gather | solution.py:157
  567.4 7.5 copy-start.13
  576.8 549.4 %all-reduce.4.cloned.1.call-start = ((), (), s32[]{:S(2)}) async-start(), calls=%async_computation.12 | async-start | bytes 25165824 | tf_op jit(solution)/shard_map/psum | solution.py:184
  576.9 14.7 %copy-start.43 = (bf16[2048,1024]{1,0:T(8,128)(2,1)S(1)}, bf16[2048,1024]{1,0:T(8,128)(2,1)}, u32[]{:S(2)}) copy-start(bf16[2048,1024]{1,0:T(8,128)(2,1)} %all-gather.7.cloned.1.call-done) | copy-start | bytes 12582916
  641.9 5.5 copy-start.8
  641.9 5.5 copy-start.22
  649.7 13.1 %copy-start.3 = (bf16[1024,3,8,64]{0,3,2,1:T(8,128)(2,1)}, bf16[1024,3,8,64]{0,3,2,1:T(8,128)(2,1)S(1)}, u32[]{:S(2)}) copy-start(bf16[1024,3,8,64]{0,3,2,1:T(8,128)(2,1)S(1)} %dynamic-slice_bitcast_fusion.7) | copy-start | bytes 9437188 | tf_op jit(solution)/shard_map/while
  756.1 13.2 %copy-start.3 = (bf16[1024,3,8,64]{0,3,2,1:T(8,128)(2,1)}, bf16[1024,3,8,64]{0,3,2,1:T(8,128)(2,1)S(1)}, u32[]{:S(2)}) copy-start(bf16[1024,3,8,64]{0,3,2,1:T(8,128)(2,1)S(1)} %dynamic-slice_bitcast_fusion.7) | copy-start | bytes 9437188 | tf_op jit(solution)/shard_map/while
  875.0 7.8 copy-start.16
  875.0 7.8 copy-start.42
  891.1 292.4 %reduce-scatter.11.cloned.1.call-start = ((), (), s32[]{:S(2)}) async-start(), calls=%async_computation.11 | async-start | bytes 6291456 | tf_op jit(solution)/shard_map/reduce_scatter | solution.py:172
  1129.0 6.9 copy-start.17
  1135.9 4.4 copy-start.15
  1140.3 43.2 %copy-start.6 = (bf16[1024,1024]{1,0:T(8,128)(2,1)S(1)}, bf16[1024,1024]{1,0:T(8,128)(2,1)}, u32[]{:S(2)}) copy-start(bf16[1024,1024]{1,0:T(8,128)(2,1)} %param.19) | copy-start | bytes 6291460
  1140.3 43.2 %copy-start.24 = (f32[1024]{0:T(1024)S(1)}, f32[1024]{0:T(1024)}, u32[]{:S(2)}) copy-start(f32[1024]{0:T(1024)} %copy-done.23) | copy-start | bytes 12292
  1140.3 43.2 %copy-start.28 = (f32[1024]{0:T(1024)S(1)}, f32[1024]{0:T(1024)}, u32[]{:S(2)}) copy-start(f32[1024]{0:T(1024)} %param.21) | copy-start | bytes 12292
  1143.3 43.3 %copy-start.32 = (f32[1024]{0:T(1024)S(1)}, f32[1024]{0:T(1024)}, u32[]{:S(2)}) copy-start(f32[1024]{0:T(1024)} %copy-done.31) | copy-start | bytes 12292
  1143.3 43.4 %copy-start.26 = (f32[1024]{0:T(1024)S(1)}, f32[1024]{0:T(1024)}, u32[]{:S(2)}) copy-start(f32[1024]{0:T(1024)} %copy-done.25) | copy-start | bytes 12292
  1143.3 47.3 %copy-start.30 = (f32[1024]{0:T(1024)S(1)}, f32[1024]{0:T(1024)}, u32[]{:S(2)}) copy-start(f32[1024]{0:T(1024)} %copy-done.29) | copy-start | bytes 12292
  1183.5 7.1 copy-start.11
  1183.5 7.1 copy-start.12
  1183.5 7.1 copy-start.14
  1190.6 43.6 %copy-start.1 = (bf16[512,1024]{1,0:T(8,128)(2,1)S(1)}, bf16[512,1024]{1,0:T(8,128)(2,1)}, u32[]{:S(2)}) copy-start(bf16[512,1024]{1,0:T(8,128)(2,1)} %param.26) | copy-start | bytes 3145732
  1190.6 3.7 copy-start.34
  1190.7 3.7 copy-start.35
  (8 other events, 12.2 us)
Sparse Core Ops, SparseCore 0:
  15.2 59.4 all-gather.4
  240.2 54.3 reduce-scatter.4
  300.4 56.7 all-gather.6
  358.6 56.7 all-gather.8
  456.5 54.3 reduce-scatter.8
  513.0 54.2 reduce-scatter.6
  576.9 56.7 all-gather.10
  891.2 234.9 all-reduce.3
  1129.1 54.3 reduce-scatter.10
where the time goes:
time: 1250 us; the launch traced here: 1240 us
  waiting for transfers between devices  550 us (44%)
  matrix products  335 us (27%)
  other arithmetic  172 us (14%)
  local copies, waits for them, and re-layouts  93.5 us (7%)
  blocking collectives  75.1 us (6%)
  between operations  14.8 us (1%)
    psum x1, waiting for transfers between devices, per_device(): lax.psum(grad_joined_weight.astype(jnp.bfloat16), 'dp').astype(jnp.float32)  187 us
    convert_element_type x2, other arithmetic, attend_backward(): grad_scores = (attn_probs * (grad_probs - row_inner)).astype(jnp.bfloat16)  66.6 us
    all_gather x1, waiting for transfers between devices, per_device(): rows_two = lax.all_gather(normed_two, 'mp', axis=0, tiled=True)  56.3 us
    reduce_scatter x1, waiting for transfers between devices, per_device(): lax.psum_scatter(jnp.dot(context_rows, w_out, preferred_element_type=jnp....  54.4 us
    all_gather x1, waiting for transfers between devices, per_device(): rows_one = lax.all_gather(normed_one, 'mp', axis=0, tiled=True)  52.6 us
    reduce_scatter x1, waiting for transfers between devices, per_device(): lax.psum_scatter(jnp.dot(hidden, w_down, preferred_element_type=jnp.float...  52 us
    dot_general x2, matrix products, attend_backward(): jnp.einsum('qhd,khd->hqk', grad_context, value_rows, preferred_element_ty...  47.7 us
    reduce_scatter x1, waiting for transfers between devices, per_device(): lax.psum_scatter(jnp.einsum('nf,df->nd', grad_up, w_up, preferred_element...  40.5 us
  transfers between devices with their start and end apart: 9, of which 9 were waited for; matrix products, arithmetic and copies ran while one was open for 8% of the time, Pallas kernels for 0%

commit v1 on v0

--- a/solution.py
+++ b/solution.py
@@ -1,11 +1,18 @@
 import jax
 import jax.numpy as jnp
 from jax import lax
+from jax.experimental import pallas as pl
+from jax.experimental.pallas import tpu as pltpu
 from jax.sharding import PartitionSpec as P
 
 HD = 64
 BLOCK = 64
 SEQ = 1024
+PAIR = 2 * HD
+BF16 = jnp.bfloat16
+F32 = jnp.float32
+NT = (((1,), (1,)), ((), ()))
+TN = (((0,), (0,)), ((), ()))
 
 
 def layer_norm(values, norm_gain, norm_bias):
@@ -30,7 +37,7 @@
     return jnp.repeat(jnp.repeat(allowed, BLOCK, axis=1), BLOCK, axis=2)
 
 
-def attend_forward(joined_seq, allowed, scaling):
+def attend_forward_split(joined_seq, allowed, scaling):
     queries = joined_seq[:, 0]
     key_rows = joined_seq[:, 1]
     value_rows = joined_seq[:, 2]
@@ -46,7 +53,7 @@
     return (context.astype(jnp.bfloat16), (highest + jnp.log(row_totals))[..., 0])
 
 
-def attend_backward(seq_items, allowed, scaling):
+def attend_backward_split(seq_items, allowed, scaling):
     joined_seq, grad_context, row_lse = seq_items
     queries = joined_seq[:, 0]
     key_rows = joined_seq[:, 1]
@@ -78,7 +85,7 @@
     return jnp.stack([grad_queries, grad_keys, grad_values], axis=1)
 
 
-def per_device(
+def split_sequence(
     hidden_in,
     out_grad,
     ln1_gain,
@@ -108,7 +115,7 @@
     joined = jnp.dot(rows_one, w_joined, preferred_element_type=jnp.float32).astype(jnp.bfloat16)
     joined_seq = joined.reshape(seq_count, SEQ, 3, local_heads, HD)
     context, row_lse = lax.map(
-        lambda seq_block: attend_forward(seq_block, allowed, scaling), joined_seq
+        lambda seq_block: attend_forward_split(seq_block, allowed, scaling), joined_seq
     )
     context_rows = context.reshape(seq_count * SEQ, head_width)
     middle = inputs + lax.psum_scatter(
@@ -162,7 +169,7 @@
         "ne,nd->ed", context_rows, rows_attn, preferred_element_type=jnp.float32
     )
     grad_joined = lax.map(
-        lambda seq_items: attend_backward(seq_items, allowed, scaling),
+        lambda seq_items: attend_backward_split(seq_items, allowed, scaling),
         (joined_seq, grad_context.reshape(seq_count, SEQ, local_heads, HD), row_lse),
     )
     grad_joined = grad_joined.reshape(seq_count * SEQ, 3 * head_width)
@@ -211,6 +218,342 @@
     )
 
 
+def mm(left, right, dims=(((1,), (0,)), ((), ()))):
+    return lax.dot_general(left, right, dims, preferred_element_type=F32)
+
+
+def head_lanes(rows, head):
+    lanes = lax.broadcasted_iota(jnp.int32, rows.shape, 1)
+    return jnp.where(lanes // HD == head, rows, jnp.zeros_like(rows))
+
+
+def masked_scores(key_rows, queries, bias):
+    scores = mm(key_rows, queries, NT)
+    keys, width = scores.shape
+    blocked = scores.reshape(keys // BLOCK, BLOCK, width) + bias[:, None, :]
+    return blocked.reshape(keys, width)
+
+
+def attend_forward_kernel(tile, qkv_ref, bias_ref, context_ref, lse_ref):
+    scaling = HD ** (-0.5)
+    key_rows = qkv_ref[:, PAIR : 2 * PAIR]
+    values_t = qkv_ref[:, 2 * PAIR :].astype(F32).T.astype(BF16)
+    for start in range(0, qkv_ref.shape[0], tile):
+        rows = slice(start, start + tile)
+        queries = qkv_ref[rows, :PAIR] * jnp.asarray(scaling, BF16)
+        parts = []
+        for head in range(2):
+            scores = masked_scores(key_rows, head_lanes(queries, head), bias_ref[head, :, rows])
+            highest = jnp.max(scores, axis=0, keepdims=True)
+            shifted = jnp.exp(scores - highest)
+            totals = jnp.sum(shifted, axis=0, keepdims=True)
+            summed = mm(values_t[head * HD : (head + 1) * HD], shifted.astype(BF16))
+            parts.append(summed / totals)
+            lse_ref[0, head : head + 1, rows] = highest + jnp.log(totals)
+        context_ref[rows, :] = jnp.concatenate(parts, axis=0).T.astype(BF16)
+
+
+def attend_backward_kernel(
+    tile, qkv_ref, bias_ref, context_ref, lse_ref, grad_ref, out_ref, key_acc, value_acc
+):
+    scaling = HD ** (-0.5)
+    key_rows = qkv_ref[:, PAIR : 2 * PAIR]
+    value_rows = qkv_ref[:, 2 * PAIR :]
+    keys_t = key_rows.astype(F32).T.astype(BF16)
+    for start in range(0, qkv_ref.shape[0], tile):
+        rows = slice(start, start + tile)
+        queries = qkv_ref[rows, :PAIR] * jnp.asarray(scaling, BF16)
+        grads = grad_ref[rows, :]
+        inner_t = (grads.astype(F32) * context_ref[rows, :].astype(F32)).T
+        probs, slopes, masked_q, masked_g, parts = [], [], [], [], []
+        for head in range(2):
+            query_h, grad_h = head_lanes(queries, head), head_lanes(grads, head)
+            scores = masked_scores(key_rows, query_h, bias_ref[head, :, rows])
+            attn = jnp.exp(scores - lse_ref[0, head : head + 1, rows])
+            inner = jnp.sum(inner_t[head * HD : (head + 1) * HD], axis=0, keepdims=True)
+            slope = (attn * (mm(value_rows, grad_h, NT) - inner)).astype(BF16)
+            parts.append(mm(keys_t[head * HD : (head + 1) * HD], slope) * scaling)
+            probs.append(attn.astype(BF16))
+            slopes.append(slope)
+            masked_q.append(query_h)
+            masked_g.append(grad_h)
+        out_ref[rows, :PAIR] = jnp.concatenate(parts, axis=0).T.astype(BF16)
+        grad_k = mm(jnp.concatenate(slopes, axis=1), jnp.concatenate(masked_q, axis=0))
+        grad_v = mm(jnp.concatenate(probs, axis=1), jnp.concatenate(masked_g, axis=0))
+        if start == 0:
+            key_acc[...] = grad_k
+            value_acc[...] = grad_v
+        else:
+            key_acc[...] += grad_k
+            value_acc[...] += grad_v
+    out_ref[:, PAIR : 2 * PAIR] = key_acc[...].astype(BF16)
+    out_ref[:, 2 * PAIR :] = value_acc[...].astype(BF16)
+
+
+def attention_cost(pairs, matmuls):
+    return pl.CostEstimate(
+        flops=matmuls * 2 * pairs * 2 * SEQ * SEQ * 256,
+        bytes_accessed=pairs * SEQ * PAIR * 16,
+        transcendentals=pairs * 2 * SEQ * SEQ,
+    )
+
+
+VMEM_LIMIT = 48 << 20
+TILE = 256
+
+
+def attend_forward(qkv, bias):
+    pairs = qkv.shape[1] // (3 * PAIR)
+    blocks = SEQ // BLOCK
+    return pl.pallas_call(
+        lambda *refs: attend_forward_kernel(TILE, *refs),
+        grid=(pairs,),
+        in_specs=[
+            pl.BlockSpec((SEQ, 3 * PAIR), lambda pair: (0, pair)),
+            pl.BlockSpec((2, blocks, SEQ), lambda pair: (pair, 0, 0)),
+        ],
+        out_specs=[
+            pl.BlockSpec((SEQ, PAIR), lambda pair: (0, pair)),
+            pl.BlockSpec((1, 2, SEQ), lambda pair: (pair, 0, 0)),
+        ],
+        out_shape=[
+            jax.ShapeDtypeStruct((SEQ, pairs * PAIR), BF16),
+            jax.ShapeDtypeStruct((pairs, 2, SEQ), F32),
+        ],
+        compiler_params=pltpu.CompilerParams(vmem_limit_bytes=VMEM_LIMIT),
+        cost_estimate=attention_cost(pairs, 2),
+        name="attend_forward",
+    )(qkv, bias)
+
+
+def attend_backward(qkv, bias, context, row_lse, grad_context):
+    pairs = qkv.shape[1] // (3 * PAIR)
+    blocks = SEQ // BLOCK
+    return pl.pallas_call(
+        lambda *refs: attend_backward_kernel(TILE, *refs),
+        grid=(pairs,),
+        in_specs=[
+            pl.BlockSpec((SEQ, 3 * PAIR), lambda pair: (0, pair)),
+            pl.BlockSpec((2, blocks, SEQ), lambda pair: (pair, 0, 0)),
+            pl.BlockSpec((SEQ, PAIR), lambda pair: (0, pair)),
+            pl.BlockSpec((1, 2, SEQ), lambda pair: (pair, 0, 0)),
+            pl.BlockSpec((SEQ, PAIR), lambda pair: (0, pair)),
+        ],
+        out_specs=pl.BlockSpec((SEQ, 3 * PAIR), lambda pair: (0, pair)),
+        out_shape=jax.ShapeDtypeStruct((SEQ, pairs * 3 * PAIR), BF16),
+        scratch_shapes=[pltpu.VMEM((SEQ, PAIR), F32), pltpu.VMEM((SEQ, PAIR), F32)],
+        compiler_params=pltpu.CompilerParams(vmem_limit_bytes=VMEM_LIMIT),
+        cost_estimate=attention_cost(pairs, 5),
+        name="attend_backward",
+    )(qkv, bias, context, row_lse, grad_context)
+
+
+def block_bias(rand_blocks):
+    blocks = SEQ // BLOCK
+    row_ids = jnp.arange(blocks)[None, :]
+    col_ids = jnp.arange(blocks)[:, None]
+    window = (
+        (jnp.abs(row_ids - col_ids) <= 1)
+        | (col_ids == 0)
+        | (col_ids == blocks - 1)
+        | (row_ids == 0)
+        | (row_ids == blocks - 1)
+    )
+    picked = jnp.any(rand_blocks[:, None, :, :] == col_ids[None, :, :, None], axis=3)
+    bias = jnp.where(window[None] | picked, 0.0, -1e30).astype(F32)
+    return jnp.repeat(bias, BLOCK, axis=2)
+
+
+def swap(array, axis, bit):
+    size = lax.axis_size(axis)
+    return lax.ppermute(array, axis, [(place, place ^ bit) for place in range(size)])
+
+
+def halves_in_order(mine, other, bit, axis=0):
+    return jnp.where(
+        bit == 0,
+        jnp.concatenate([mine, other], axis=axis),
+        jnp.concatenate([other, mine], axis=axis),
+    )
+
+
+def add_up(*terms):
+    total = terms[0].astype(F32)
+    for term in terms[1:]:
+        total = total + term.astype(F32)
+    return total.astype(BF16)
+
+
+def reduce_grads(own_a, own_b, far_a, far_b):
+    place = lax.axis_index("dp")
+    far = add_up(far_a, swap(far_b, "dp", 1))
+    near = add_up(own_a, swap(own_b, "dp", 1), swap(far, "mp", 1))
+    bits = []
+    step = 2
+    while step < lax.axis_size("dp"):
+        bits.append(step)
+        step *= 2
+    for step in bits:
+        bit = (place // step) % 2
+        rows = near.shape[0] // 2
+        keep = lax.dynamic_slice_in_dim(near, bit * rows, rows, 0)
+        send = lax.dynamic_slice_in_dim(near, (1 - bit) * rows, rows, 0)
+        near = add_up(keep, swap(send, "dp", step))
+    for step in reversed(bits):
+        bit = (place // step) % 2
+        near = halves_in_order(near, swap(near, "dp", step), bit)
+    return near, swap(near, "dp", 1)
+
+
+def whole_sequence(
+    hidden_in,
+    out_grad,
+    ln1_gain,
+    ln1_bias,
+    w_query,
+    w_key,
+    w_value,
+    w_out,
+    ln2_gain,
+    ln2_bias,
+    w_up,
+    b_up,
+    w_down,
+    b_down,
+    rand_blocks,
+):
+    core = lax.axis_index("dp") % 2
+    side = lax.axis_index("mp")
+
+    def piece(array, axis, other):
+        size = array.shape[axis] // 2
+        return lax.dynamic_slice_in_dim(array, (core ^ other) * size, size, axis)
+
+    def weights_of(other):
+        columns = [piece(part, 1, other) for part in (w_query, w_key, w_value)]
+        pairs = columns[0].shape[1] // PAIR
+        joined = jnp.concatenate(
+            [
+                part[:, pair * PAIR : (pair + 1) * PAIR]
+                for pair in range(pairs)
+                for part in columns
+            ],
+            axis=1,
+        )
+        return joined, piece(w_out, 0, other), piece(w_up, 1, other), piece(w_down, 0, other)
+
+    own_a, own_b = weights_of(0), weights_of(1)
+    far_a = tuple(swap(part, "mp", 1) for part in own_a)
+    far_b = tuple(swap(part, "dp", 1) for part in far_a)
+    far_bup, far_rand = swap(b_up, "mp", 1), swap(rand_blocks, "mp", 1)
+    groups = (own_a, own_b, far_a, far_b)
+    joined_w, out_w, up_w, down_w = zip(*groups)
+    up_bias = [piece(b_up, 0, 0), piece(b_up, 0, 1), piece(far_bup, 0, 0), piece(far_bup, 0, 1)]
+    picks = [
+        piece(rand_blocks, 0, 0),
+        piece(rand_blocks, 0, 1),
+        piece(far_rand, 0, 0),
+        piece(far_rand, 0, 1),
+    ]
+    bias = [block_bias(pick) for pick in picks]
+    every = range(4)
+
+    inputs = hidden_in.astype(F32)
+    normed_one = layer_norm(inputs, ln1_gain, ln1_bias).astype(BF16)
+    qkv = [mm(normed_one, joined_w[g]).astype(BF16) for g in every]
+    context, row_lse = zip(*[attend_forward(qkv[g], bias[g]) for g in every])
+    middle = inputs
+    for g in every:
+        middle = middle + mm(context[g], out_w[g])
+    normed_two = layer_norm(middle, ln2_gain, ln2_bias).astype(BF16)
+    up_pre = [mm(normed_two, up_w[g]) + up_bias[g] for g in every]
+    hidden = [jax.nn.gelu(pre, approximate=True).astype(BF16) for pre in up_pre]
+    total = middle + b_down
+    for g in every:
+        total = total + mm(hidden[g], down_w[g])
+    output = total.astype(BF16)
+
+    grad_out = out_grad.astype(F32)
+    bias_down = jnp.sum(grad_out, axis=0)
+    grad_up = []
+    for g in every:
+        grad_hidden = mm(out_grad, down_w[g], NT)
+        pull = jax.vjp(lambda pre: jax.nn.gelu(pre, approximate=True), up_pre[g])[1]
+        grad_up.append(pull(grad_hidden)[0].astype(BF16))
+    grad_down_w = reduce_grads(*[mm(hidden[g], out_grad, TN).astype(BF16) for g in every])
+    bias_up = [jnp.sum(grad_up[g], axis=0, dtype=F32) for g in every]
+    grad_up_w = reduce_grads(*[mm(normed_two, grad_up[g], TN).astype(BF16) for g in every])
+    grad_normed_two = mm(grad_up[0], up_w[0], NT)
+    for g in (1, 2, 3):
+        grad_normed_two = grad_normed_two + mm(grad_up[g], up_w[g], NT)
+    grad_mid_norm, gain_two, bias_two = jax.vjp(layer_norm, middle, ln2_gain, ln2_bias)[1](
+        grad_normed_two
+    )
+    grad_middle = grad_out + grad_mid_norm
+    grad_attn = grad_middle.astype(BF16)
+    grad_out_w = reduce_grads(*[mm(context[g], grad_attn, TN).astype(BF16) for g in every])
+    grad_qkv = []
+    for g in every:
+        grad_context = mm(grad_attn, out_w[g], NT).astype(BF16)
+        grad_qkv.append(attend_backward(qkv[g], bias[g], context[g], row_lse[g], grad_context))
+    grad_joined_w = reduce_grads(*[mm(normed_one, grad_qkv[g], TN).astype(BF16) for g in every])
+    grad_normed_one = mm(grad_qkv[0], joined_w[0], NT)
+    for g in (1, 2, 3):
+        grad_normed_one = grad_normed_one + mm(grad_qkv[g], joined_w[g], NT)
+    grad_in_norm, gain_one, bias_one = jax.vjp(layer_norm, inputs, ln1_gain, ln1_bias)[1](
+        grad_normed_one
+    )
+    input_grad = grad_middle + grad_in_norm
+
+    own_bias = halves_in_order(bias_up[0], bias_up[1], core)
+    far_bias = halves_in_order(bias_up[2], bias_up[3], core)
+    small = lax.psum(
+        jnp.concatenate(
+            [gain_one, bias_one, gain_two, bias_two, bias_down]
+            + [halves_in_order(own_bias, far_bias, side)]
+        ),
+        ("dp", "mp"),
+    )
+    width = inputs.shape[1]
+    vectors = [small[place * width : (place + 1) * width] for place in range(5)]
+    bias_up_sum = lax.dynamic_slice_in_dim(small, 5 * width + side * b_up.shape[0], b_up.shape[0])
+
+    def in_order(pair, axis):
+        return halves_in_order(pair[0], pair[1], core, axis).astype(F32)
+
+    def third(pair, which):
+        slices = []
+        for part in pair:
+            pairs = part.shape[1] // (3 * PAIR)
+            slices.append(
+                jnp.concatenate(
+                    [
+                        part[:, (3 * place + which) * PAIR : (3 * place + which + 1) * PAIR]
+                        for place in range(pairs)
+                    ],
+                    axis=1,
+                )
+            )
+        return in_order(slices, 1)
+
+    return (
+        output,
+        input_grad,
+        vectors[0],
+        vectors[1],
+        third(grad_joined_w, 0),
+        third(grad_joined_w, 1),
+        third(grad_joined_w, 2),
+        in_order(grad_out_w, 0),
+        vectors[2],
+        vectors[3],
+        in_order(grad_up_w, 1),
+        bias_up_sum,
+        in_order(grad_down_w, 0),
+        vectors[4],
+    )
+
+
 def solution(mesh):
     in_specs = (
         P(("dp", "mp"), None),
@@ -245,6 +588,12 @@
         P("mp", None),
         P(),
     )
+    def per_device(hidden_in, *others):
+        whole = hidden_in.shape[0] == SEQ and mesh.shape["mp"] == 2
+        paired = others[-1].shape[0] % 4 == 0 and mesh.shape["dp"] in (2, 4, 8, 16, 32)
+        layer = whole_sequence if whole and paired else split_sequence
+        return layer(hidden_in, *others)
+
     return jax.shard_map(
         per_device, mesh=mesh, in_specs=in_specs, out_specs=out_specs, check_vma=False
     )

time: 1250 us -> 777 us (0.62)
  waiting for transfers between devices: 550 us -> 305 us
  matrix products: 335 us -> 181 us
  other arithmetic: 172 us -> 53.4 us
  Pallas kernels: 0 us -> 97.3 us
  local copies, waits for them, and re-layouts: 93.5 us -> 46 us
  starting transfers between devices: 0.37 us -> 44.5 us
  blocking collectives: 75.1 us -> 38.9 us
    ppermute x0 -> x50, waiting for transfers between devices: none -> 305 us  [swap(): lax.ppermute(array, axis, [(place, place ^ bit) for place in range(size)])]
    reduce_scatter x4 -> x0, waiting for transfers between devices: 187 us -> none  [the longest x1 54.4 us: per_device(): lax.psum_scatter(jnp.dot(context_rows, w_out, preferred_element_type=jnp....]
    psum x1 -> x0, waiting for transfers between devices: 187 us -> none  [per_device(): lax.psum(grad_joined_weight.astype(jnp.bfloat16), 'dp').astype(jnp.float32)]
    all_gather x4 -> x0, waiting for transfers between devices: 176 us -> none  [the longest x1 56.3 us: per_device(): rows_two = lax.all_gather(normed_two, 'mp', axis=0, tiled=True)]
    dot_general x26 -> x48, matrix products: 335 us -> 181 us  [mm(): return lax.dot_general(left, right, dims, preferred_element_type=F32)]
    pallas_call x0 -> x8, Pallas kernels: none -> 97.3 us  [the longest x4 50.8 us: attend_backward(): pl.pallas_call(lambda *refs: attend_backward_kernel(TILE, *refs), grid=(p...]
    convert_element_type x11 -> x26, other arithmetic: 110 us -> 33.7 us  [the longest x6 21.3 us: in_order(): return halves_in_order(pair[0], pair[1], core, axis).astype(F32)]
    ppermute x0 -> x50, starting transfers between devices: none -> 44.5 us  [swap(): lax.ppermute(array, axis, [(place, place ^ bit) for place in range(size)])]
  transfers between devices with their start and end apart: 9 -> 50, of which waited for: 9 -> 18; matrix products, arithmetic and copies ran while one was open for 8% -> 34% of each run, Pallas kernels for 0% -> 13%
where the time goes in v1:
time: 777 us; the launch traced here: 769 us
  waiting for transfers between devices  305 us (39%)
  matrix products  181 us (23%)
  Pallas kernels  97.3 us (13%)
  other arithmetic  53.4 us (7%)
  local copies, waits for them, and re-layouts  46 us (6%)
  starting transfers between devices  44.5 us (6%)
  blocking collectives  38.9 us (5%)
    ppermute x50, waiting for transfers between devices, swap(): lax.ppermute(array, axis, [(place, place ^ bit) for place in range(size)])  305 us
    dot_general x48, matrix products, mm(): return lax.dot_general(left, right, dims, preferred_element_type=F32)  181 us
    pallas_call x4, Pallas kernels, attend_backward(): pl.pallas_call(lambda *refs: attend_backward_kernel(TILE, *refs), grid=(p...  50.8 us
    pallas_call x4, Pallas kernels, attend_forward(): pl.pallas_call(lambda *refs: attend_forward_kernel(TILE, *refs), grid=(pa...  46.5 us
    ppermute x50, starting transfers between devices, swap(): lax.ppermute(array, axis, [(place, place ^ bit) for place in range(size)])  44.5 us
    psum x1, blocking collectives, whole_sequence(): lax.psum(jnp.concatenate([gain_one, bias_one, gain_two, bias_two, bias_do...  38.9 us
    unnamed x176, local copies, waits for them, and re-layouts  30.7 us
    convert_element_type x6, other arithmetic, in_order(): return halves_in_order(pair[0], pair[1], core, axis).astype(F32)  21.3 us
  transfers between devices with their start and end apart: 50, of which 18 were waited for; matrix products, arithmetic and copies ran while one was open for 34% of the time, Pallas kernels for 13%

profile of v1, /device:TPU:0, one launch (start us, length us, event | category | flops | bytes accessed | tf_op | source)
XLA Modules:
  0.0 768.7 jit_solution(15372951005264305588)
XLA Ops:
  25.6 5.3 convolution_convert_fusion.11.refs_0_
  38.8 48.7 %collective-permute-done.1 = s32[8,16,3]{1,0,2:T(8,128)S(1)} collective-permute-done((s32[8,16,3]{1,0,2:T(8,128)S(1)}, s32[8,16,3]{1,0,2:T(8,128)S(1)}, u32[]{:S(2)}, u32[]{:S(2)}) %collective-permute-start.1) | collective-permute-done | bytes 1568 | tf_op jit(solution)/shard_map/ppermute | solution.py:369
  92.3 11.6 %attend_forward.5 = (bf16[1024,256]{1,0:T(8,128)(2,1)S(1)}, f32[2,2,1024]{2,1,0:T(2,128)S(1)}) custom-call(bf16[1024,768]{1,0:T(8,128)(2,1)S(1)} %convolution_convert_fusion.10.refs_0_, f32[4,16,1024]{2,1,0:T(8,128)S(1)} %reshape.204.refs_1_), custom_call_target="tpu_custom_call" | custom-call | flops 4294967296 | bytes 4194304 | tf_op jit(solution)/shard_map/attend_forward/pallas_call | solution.py:308
  103.9 11.9 %attend_forward.4 = (bf16[1024,256]{1,0:T(8,128)(2,1)S(1)}, f32[2,2,1024]{2,1,0:T(2,128)S(1)}) custom-call(bf16[1024,768]{1,0:T(8,128)(2,1)S(1)} %copy-done.12, f32[4,16,1024]{2,1,0:T(8,128)S(1)} %reshape.203.refs_1_), custom_call_target="tpu_custom_call" | custom-call | flops 4294967296 | bytes 4194304 | tf_op jit(solution)/shard_map/attend_forward/pallas_call | solution.py:308
  127.9 11.4 %attend_forward.6 = (bf16[1024,256]{1,0:T(8,128)(2,1)S(1)}, f32[2,2,1024]{2,1,0:T(2,128)S(1)}) custom-call(bf16[1024,768]{1,0:T(8,128)(2,1)S(1)} %convolution_convert_fusion.9.refs_0_, f32[4,16,1024]{2,1,0:T(8,128)S(1)} %reshape.205.refs_1_), custom_call_target="tpu_custom_call" | custom-call | flops 4294967296 | bytes 4194304 | tf_op jit(solution)/shard_map/attend_forward/pallas_call | solution.py:308
  139.4 4.0 fusion.104
  147.3 11.6 %attend_forward.7 = (bf16[1024,256]{1,0:T(8,128)(2,1)S(1)}, f32[2,2,1024]{2,1,0:T(2,128)S(1)}) custom-call(bf16[1024,768]{1,0:T(8,128)(2,1)S(1)} %convolution_convert_fusion.8.refs_0_, f32[4,16,1024]{2,1,0:T(8,128)S(1)} %reshape.206.refs_1_), custom_call_target="tpu_custom_call" | custom-call | flops 4294967296 | bytes 4194304 | tf_op jit(solution)/shard_map/attend_forward/pallas_call | solution.py:308
  171.0 6.3 fusion.92
  177.3 7.1 convert_reduce_fusion.5
  184.5 4.6 fusion.58
  189.1 5.1 convert_reduce_fusion.4
  206.4 4.4 convolution_convert_fusion.1
  210.9 4.2 fusion.106
  215.2 4.4 fusion.93
  220.1 7.2 convert_reduce_fusion.3
  227.3 4.7 fusion.109
  232.0 4.4 fusion.91
  236.4 6.2 fusion.94
  242.5 4.0 fusion.107
  246.6 8.1 %convert_reduce_fusion.2 = (f32[1024]{0:T(1024)S(1)}, bf16[1024,1024]{1,0:T(8,128)(2,1)S(1)}) fusion(f32[1024,1024]{1,0:T(8,128)S(1)} %fusion.107, f32[1024]{0:T(1024)S(1)} %get-tuple-element.96, bf16[1024,1024]{1,0:T(8,128)(2,1)} %collective-permute-done.9, bf16[1024,1024]{1,0:T(8,128)(2,1)S(1)} %copy-done.41), kind=kOutput, calls=%fused_computation.85 | convolution fusion | flops 2171599872 | bytes 10493952 | tf_op jit(solution)/shard_map/dot_general | solution.py:222
  254.7 6.1 multiply_reduce_fusion
  272.3 4.4 convolution_convert_fusion
  276.8 12.8 %attend_backward.4 = bf16[1024,768]{1,0:T(8,128)(2,1)S(1)} custom-call(bf16[1024,768]{1,0:T(8,128)(2,1)S(1)} %copy-done.13, f32[4,16,1024]{2,1,0:T(8,128)S(1)} %copy-done.9, bf16[1024,256]{1,0:T(8,128)(2,1)S(1)} %copy-done.3, f32[2,2,1024]{2,1,0:T(2,128)S(1)} %get-tuple-element.26.refs_3_, bf16[1024,256]{1,0:T(8,128)(2,1)S(1)} %convolution_convert_fusion.19.refs_4_), custom_call_target="tpu_custom_call" | custom-call | flops 10737418240 | bytes 4194304 | tf_op jit(solution)/shard_map/attend_backward/pallas_call | solution.py:332
  289.6 5.3 fusion.110
  295.0 12.6 %attend_backward.5 = bf16[1024,768]{1,0:T(8,128)(2,1)S(1)} custom-call(bf16[1024,768]{1,0:T(8,128)(2,1)S(1)} %copy-done.11, f32[4,16,1024]{2,1,0:T(8,128)S(1)} %reshape.204.refs_1_, bf16[1024,256]{1,0:T(8,128)(2,1)S(1)} %copy-done.5, f32[2,2,1024]{2,1,0:T(2,128)S(1)} %get-tuple-element.27.refs_3_, bf16[1024,256]{1,0:T(8,128)(2,1)S(1)} %convolution_convert_fusion.18.refs_4_), custom_call_target="tpu_custom_call" | custom-call | flops 10737418240 | bytes 4194304 | tf_op jit(solution)/shard_map/attend_backward/pallas_call | solution.py:332
  312.8 12.6 %attend_backward.7 = bf16[1024,768]{1,0:T(8,128)(2,1)S(1)} custom-call(bf16[1024,768]{1,0:T(8,128)(2,1)S(1)} %copy-done.17, f32[4,16,1024]{2,1,0:T(8,128)S(1)} %reshape.206.refs_1_, bf16[1024,256]{1,0:T(8,128)(2,1)S(1)} %get-tuple-element.25.refs_2_, f32[2,2,1024]{2,1,0:T(2,128)S(1)} %get-tuple-element.29.refs_3_, ...), custom_call_target="tpu_custom_call" | custom-call | flops 10737418240 | bytes 4194304 | tf_op jit(solution)/shard_map/attend_backward/pallas_call | solution.py:332
  329.2 12.8 %attend_backward.6 = bf16[1024,768]{1,0:T(8,128)(2,1)S(1)} custom-call(bf16[1024,768]{1,0:T(8,128)(2,1)S(1)} %copy-done.15, f32[4,16,1024]{2,1,0:T(8,128)S(1)} %reshape.205.refs_1_, bf16[1024,256]{1,0:T(8,128)(2,1)S(1)} %copy-done.7, f32[2,2,1024]{2,1,0:T(2,128)S(1)} %get-tuple-element.28.refs_3_, bf16[1024,256]{1,0:T(8,128)(2,1)S(1)} %convolution_convert_fusion.17.refs_4_), custom_call_target="tpu_custom_call" | custom-call | flops 10737418240 | bytes 4194304 | tf_op jit(solution)/shard_map/attend_backward/pallas_call | solution.py:332
  346.6 4.2 fusion.95
  354.7 11.0 %add_convert_fusion.4 = bf16[1024,1024]{0,1:T(8,128)(2,1)} fusion(f32[1024,1024]{0,1:T(8,128)} %fusion.94, f32[1024,1024]{0,1:T(8,128)} %fusion.58, f32[1024,1024]{0,1:T(8,128)} %fusion.92, f32[1024,1024]{0,1:T(8,128)S(1)} %copy-done.19, f32[1024]{0:T(1024)S(1)} %copy-done.75, bf16[1024,1024]{1,0:T(8,128)(2,1)} %collective-permute-done.9, ...), kind=kOutput, calls=%fused_computation.94 | convolution fusion | flops 2164260864 | bytes 25174016 | tf_op jit(solution)/shard_map/dot_general | solution.py:222
  365.7 6.2 convert_reduce_fusion.1
  398.7 29.9 %collective-permute-done.12 = bf16[1024,768]{1,0:T(8,128)(2,1)S(1)} collective-permute-done((bf16[1024,768]{1,0:T(8,128)(2,1)S(1)}, bf16[1024,768]{1,0:T(8,128)(2,1)S(1)}, u32[]{:S(2)}, u32[]{:S(2)}) %collective-permute-start.12) | collective-permute-done | bytes 1572896 | tf_op jit(solution)/shard_map/ppermute | solution.py:369
  431.4 42.1 %collective-permute-done.32 = bf16[1024,1024]{1,0:T(8,128)(2,1)S(1)} collective-permute-done((bf16[1024,1024]{1,0:T(8,128)(2,1)S(1)}, bf16[1024,1024]{1,0:T(8,128)(2,1)S(1)}, u32[]{:S(2)}, u32[]{:S(2)}) %collective-permute-start.32) | collective-permute-done | bytes 2097184 | tf_op jit(solution)/shard_map/ppermute | solution.py:369
  478.5 39.6 %collective-permute-done.42 = bf16[1024,1024]{1,0:T(8,128)(2,1)S(1)} collective-permute-done((bf16[1024,1024]{1,0:T(8,128)(2,1)S(1)}, bf16[1024,1024]{1,0:T(8,128)(2,1)S(1)}, u32[]{:S(2)}, u32[]{:S(2)}) %collective-permute-start.42) | collective-permute-done | bytes 2097184 | tf_op jit(solution)/shard_map/ppermute | solution.py:369
  525.9 18.7 %collective-permute-done.43 = bf16[512,1024]{1,0:T(8,128)(2,1)S(1)} collective-permute-done((bf16[512,1024]{1,0:T(8,128)(2,1)S(1)}, bf16[512,1024]{1,0:T(8,128)(2,1)S(1)}, u32[]{:S(2)}, u32[]{:S(2)}) %collective-permute-start.43) | collective-permute-done | bytes 1048608 | tf_op jit(solution)/shard_map/ppermute | solution.py:369
  550.2 17.5 %collective-permute-done.44 = bf16[256,1024]{1,0:T(8,128)(2,1)S(1)} collective-permute-done((bf16[256,1024]{1,0:T(8,128)(2,1)S(1)}, bf16[256,1024]{1,0:T(8,128)(2,1)S(1)}, u32[]{:S(2)}, u32[]{:S(2)}) %collective-permute-start.44) | collective-permute-done | bytes 524320 | tf_op jit(solution)/shard_map/ppermute | solution.py:369
  573.0 19.3 %collective-permute-done.45 = bf16[128,1024]{1,0:T(8,128)(2,1)S(1)} collective-permute-done((bf16[128,1024]{1,0:T(8,128)(2,1)S(1)}, bf16[128,1024]{1,0:T(8,128)(2,1)S(1)}, u32[]{:S(2)}, u32[]{:S(2)}) %collective-permute-start.45) | collective-permute-done | bytes 262176 | tf_op jit(solution)/shard_map/ppermute | solution.py:369
  592.5 9.7 %collective-permute-done.16 = bf16[128,768]{1,0:T(8,128)(2,1)S(1)} collective-permute-done((bf16[128,768]{1,0:T(8,128)(2,1)S(1)}, bf16[128,768]{1,0:T(8,128)(2,1)S(1)}, u32[]{:S(2)}, u32[]{:S(2)}) %collective-permute-start.16) | collective-permute-done | bytes 196640 | tf_op jit(solution)/shard_map/ppermute | solution.py:369
  602.4 5.5 collective-permute-done.36
  612.3 8.1 %collective-permute-done.17 = bf16[256,768]{1,0:T(8,128)(2,1)S(1)} collective-permute-done((bf16[256,768]{1,0:T(8,128)(2,1)S(1)}, bf16[256,768]{1,0:T(8,128)(2,1)S(1)}, u32[]{:S(2)}, u32[]{:S(2)}) %collective-permute-start.17) | collective-permute-done | bytes 393248 | tf_op jit(solution)/shard_map/ppermute | solution.py:369
  622.3 9.3 %collective-permute-done.37 = bf16[256,1024]{1,0:T(8,128)(2,1)S(1)} collective-permute-done((bf16[256,1024]{1,0:T(8,128)(2,1)S(1)}, bf16[256,1024]{1,0:T(8,128)(2,1)S(1)}, u32[]{:S(2)}, u32[]{:S(2)}) %collective-permute-start.37) | collective-permute-done | bytes 524320 | tf_op jit(solution)/shard_map/ppermute | solution.py:369
  634.8 9.4 %collective-permute-done.47 = bf16[256,1024]{1,0:T(8,128)(2,1)S(1)} collective-permute-done((bf16[256,1024]{1,0:T(8,128)(2,1)S(1)}, bf16[256,1024]{1,0:T(8,128)(2,1)S(1)}, u32[]{:S(2)}, u32[]{:S(2)}) %collective-permute-start.47) | collective-permute-done | bytes 524320 | tf_op jit(solution)/shard_map/ppermute | solution.py:369
  647.4 5.0 collective-permute-done.26
  658.1 5.6 collective-permute-done.38
  664.8 25.9 %collective-permute-done.28 = bf16[128,1024]{1,0:T(8,128)(2,1)S(1)} collective-permute-done((bf16[128,1024]{1,0:T(8,128)(2,1)S(1)}, bf16[128,1024]{1,0:T(8,128)(2,1)S(1)}, u32[]{:S(2)}, u32[]{:S(2)}) %collective-permute-start.28) | collective-permute-done | bytes 262176 | tf_op jit(solution)/shard_map/ppermute | solution.py:369
  698.5 5.3 copy.68
  703.8 38.9 %psum.7 = f32[9216]{0:T(1024)S(1)} all-reduce(f32[9216]{0:T(1024)S(1)} %fusion.78), channel_id=1, replica_groups=mesh['dp'=16,'mp'=2] {'dp','mp'}, use_global_device_ids=true, to_apply=%region_21.22 | all-reduce | flops 9216 | bytes 73728 | tf_op jit(solution)/shard_map/psum | solution.py:510
  755.6 6.3 fusion.42
  761.9 6.3 fusion.43
  (382 shorter events, 199.8 us)
Async XLA Ops:
  3.9 139.5 %collective-permute-start.7 = (bf16[1024,1024]{1,0:T(8,128)(2,1)}, bf16[1024,1024]{1,0:T(8,128)(2,1)}, u32[]{:S(2)}, u32[]{:S(2)}) collective-permute-start(bf16[1024,1024]{1,0:T(8,128)(2,1)} %constant_dynamic-slice_fusion.12), channel_id=1, source_target_pairs={{0,1},{1,0},{2,3},{3,2},{4,5},{5,4},{6,7},{7,6},{8,9},{9,8},{10,11... | collective-permute-start | bytes 6291464 | tf_op jit(solution)/shard_map/ppermute | solution.py:369
  15.3 104.5 %collective-permute-start = (bf16[1024,768]{1,0:T(8,128)(2,1)}, bf16[1024,768]{1,0:T(8,128)(2,1)}, u32[]{:S(2)}, u32[]{:S(2)}) collective-permute-start(bf16[1024,768]{1,0:T(8,128)(2,1)} %dynamic-slice_dynamic-update-slice_fusion.6), channel_id=1, source_target_pairs={{0,1},{1,0},{2,3},{3,2},{4,5},{5,4},{6,7},{7,6},{8,9},{9,8},{10,11... | collective-permute-start | bytes 4718600 | tf_op jit(solution)/shard_map/ppermute | solution.py:369
  15.3 72.2 %collective-permute-start.1 = (s32[8,16,3]{1,0,2:T(8,128)S(1)}, s32[8,16,3]{1,0,2:T(8,128)S(1)}, u32[]{:S(2)}, u32[]{:S(2)}) collective-permute-start(s32[8,16,3]{1,0,2:T(8,128)S(1)} %copy-done.68), channel_id=1, source_target_pairs={{0,1},{1,0},{2,3},{3,2},{4,5},{5,4},{6,7},{7,6},{8,9},{9,8},{10,11... | collective-permute-start | bytes 4616 | tf_op jit(solution)/shard_map/ppermute | solution.py:369
  18.2 105.3 %collective-permute-start.2 = (bf16[256,1024]{1,0:T(8,128)(2,1)}, bf16[256,1024]{1,0:T(8,128)(2,1)}, u32[]{:S(2)}, u32[]{:S(2)}) collective-permute-start(bf16[256,1024]{1,0:T(8,128)(2,1)} %constant_dynamic-slice_fusion.17), channel_id=1, source_target_pairs={{0,1},{1,0},{2,3},{3,2},{4,5},{5,4},{6,7},{7,6},{8,9},{9,8},{10,11... | collective-permute-start | bytes 1572872 | tf_op jit(solution)/shard_map/ppermute | solution.py:369
  18.2 105.2 %collective-permute-start.6 = (f32[2048]{0:T(1024)S(1)}, f32[2048]{0:T(1024)S(1)}, u32[]{:S(2)}, u32[]{:S(2)}) collective-permute-start(f32[2048]{0:T(1024)S(1)} %copy-done.69), channel_id=1, source_target_pairs={{0,1},{1,0},{2,3},{3,2},{4,5},{5,4},{6,7},{7,6},{8,9},{9,8},{10,11... | collective-permute-start | bytes 24584 | tf_op jit(solution)/shard_map/ppermute | solution.py:369
  87.5 55.9 %collective-permute-start.5 = (bf16[1024,1024]{1,0:T(8,128)(2,1)}, bf16[1024,1024]{1,0:T(8,128)(2,1)}, u32[]{:S(2)}, u32[]{:S(2)}) collective-permute-start(bf16[1024,1024]{1,0:T(8,128)(2,1)} %constant_dynamic-slice_fusion.13), channel_id=1, source_target_pairs={{0,1},{1,0},{2,3},{3,2},{4,5},{5,4},{6,7},{7,6},{8,9},{9,8},{10,11... | collective-permute-start | bytes 6291464 | tf_op jit(solution)/shard_map/ppermute | solution.py:369
  119.9 24.1 %collective-permute-start.3 = (bf16[1024,768]{1,0:T(8,128)(2,1)}, bf16[1024,768]{1,0:T(8,128)(2,1)}, u32[]{:S(2)}, u32[]{:S(2)}) collective-permute-start(bf16[1024,768]{1,0:T(8,128)(2,1)} %collective-permute-done), channel_id=1, source_target_pairs={{0,2},{2,0},{4,6},{6,4},{8,10},{10,8},{12,14},{14,12},{16,18},{18,... | collective-permute-start | bytes 4718600 | tf_op jit(solution)/shard_map/ppermute | solution.py:369
  123.4 35.4 %collective-permute-start.4 = (bf16[256,1024]{1,0:T(8,128)(2,1)}, bf16[256,1024]{1,0:T(8,128)(2,1)S(1)}, u32[]{:S(2)}, u32[]{:S(2)}) collective-permute-start(bf16[256,1024]{1,0:T(8,128)(2,1)} %collective-permute-done.2), channel_id=1, source_target_pairs={{0,2},{2,0},{4,6},{6,4},{8,10},{10,8},{12,14},{14,12},{16,18},{18,... | collective-permute-start | bytes 1572872 | tf_op jit(solution)/shard_map/ppermute | solution.py:369
  143.4 103.2 %collective-permute-start.9 = (bf16[1024,1024]{1,0:T(8,128)(2,1)}, bf16[1024,1024]{1,0:T(8,128)(2,1)}, u32[]{:S(2)}, u32[]{:S(2)}) collective-permute-start(bf16[1024,1024]{1,0:T(8,128)(2,1)} %collective-permute-done.7), channel_id=1, source_target_pairs={{0,2},{2,0},{4,6},{6,4},{8,10},{10,8},{12,14},{14,12},{16,18},{18,... | collective-permute-start | bytes 6291464 | tf_op jit(solution)/shard_map/ppermute | solution.py:369
  143.5 99.1 %collective-permute-start.8 = (bf16[1024,1024]{1,0:T(8,128)(2,1)}, bf16[1024,1024]{1,0:T(8,128)(2,1)}, u32[]{:S(2)}, u32[]{:S(2)}) collective-permute-start(bf16[1024,1024]{1,0:T(8,128)(2,1)} %collective-permute-done.5), channel_id=1, source_target_pairs={{0,2},{2,0},{4,6},{6,4},{8,10},{10,8},{12,14},{14,12},{16,18},{18,... | collective-permute-start | bytes 6291464 | tf_op jit(solution)/shard_map/ppermute | solution.py:369
  210.9 220.0 %collective-permute-start.30 = (bf16[1024,1024]{1,0:T(8,128)(2,1)}, bf16[1024,1024]{1,0:T(8,128)(2,1)}, u32[]{:S(2)}, u32[]{:S(2)}) collective-permute-start(bf16[1024,1024]{1,0:T(8,128)(2,1)} %convolution_convert_fusion.3), channel_id=1, source_target_pairs={{0,2},{2,0},{4,6},{6,4},{8,10},{10,8},{12,14},{14,12},{16,18},{18,... | collective-permute-start | bytes 6291464 | tf_op jit(solution)/shard_map/ppermute | solution.py:369
  353.1 23.5 %collective-permute-start.11 = (bf16[1024,768]{1,0:T(8,128)(2,1)S(1)}, bf16[1024,768]{1,0:T(8,128)(2,1)}, u32[]{:S(2)}, u32[]{:S(2)}) collective-permute-start(bf16[1024,768]{1,0:T(8,128)(2,1)S(1)} %convolution_convert_fusion.4), channel_id=1, source_target_pairs={{0,2},{2,0},{4,6},{6,4},{8,10},{10,8},{12,14},{14,12},{16,18},{18,... | collective-permute-start | bytes 4718600 | tf_op jit(solution)/shard_map/ppermute | solution.py:369
  353.6 21.7 %collective-permute-start.21 = (bf16[256,1024]{1,0:T(8,128)(2,1)S(1)}, bf16[256,1024]{1,0:T(8,128)(2,1)S(1)}, u32[]{:S(2)}, u32[]{:S(2)}) collective-permute-start(bf16[256,1024]{1,0:T(8,128)(2,1)S(1)} %copy-done.74), channel_id=1, source_target_pairs={{0,2},{2,0},{4,6},{6,4},{8,10},{10,8},{12,14},{14,12},{16,18},{18,... | collective-permute-start | bytes 1572872 | tf_op jit(solution)/shard_map/ppermute | solution.py:369
  353.7 26.4 %collective-permute-start.31 = (bf16[1024,1024]{1,0:T(8,128)(2,1)}, bf16[1024,1024]{1,0:T(8,128)(2,1)}, u32[]{:S(2)}, u32[]{:S(2)}) collective-permute-start(bf16[1024,1024]{1,0:T(8,128)(2,1)} %convolution_convert_fusion.2), channel_id=1, source_target_pairs={{0,2},{2,0},{4,6},{6,4},{8,10},{10,8},{12,14},{14,12},{16,18},{18,... | collective-permute-start | bytes 6291464 | tf_op jit(solution)/shard_map/ppermute | solution.py:369
  354.2 32.1 %collective-permute-start.41 = (bf16[1024,1024]{1,0:T(8,128)(2,1)}, bf16[1024,1024]{1,0:T(8,128)(2,1)}, u32[]{:S(2)}, u32[]{:S(2)}) collective-permute-start(bf16[1024,1024]{1,0:T(8,128)(2,1)} %convolution_convert_fusion), channel_id=1, source_target_pairs={{0,2},{2,0},{4,6},{6,4},{8,10},{10,8},{12,14},{14,12},{16,18},{18,... | collective-permute-start | bytes 6291464 | tf_op jit(solution)/shard_map/ppermute | solution.py:369
  375.3 19.6 %collective-permute-start.10 = (bf16[1024,768]{1,0:T(8,128)(2,1)S(1)}, bf16[1024,768]{1,0:T(8,128)(2,1)S(1)}, u32[]{:S(2)}, u32[]{:S(2)}) collective-permute-start(bf16[1024,768]{1,0:T(8,128)(2,1)S(1)} %convolution_convert_fusion.6), channel_id=1, source_target_pairs={{0,2},{2,0},{4,6},{6,4},{8,10},{10,8},{12,14},{14,12},{16,18},{18,... | collective-permute-start | bytes 4718600 | tf_op jit(solution)/shard_map/ppermute | solution.py:369
  376.6 9.0 %collective-permute-start.20 = (bf16[256,1024]{1,0:T(8,128)(2,1)S(1)}, bf16[256,1024]{1,0:T(8,128)(2,1)S(1)}, u32[]{:S(2)}, u32[]{:S(2)}) collective-permute-start(bf16[256,1024]{1,0:T(8,128)(2,1)S(1)} %convolution_convert_fusion.14), channel_id=1, source_target_pairs={{0,2},{2,0},{4,6},{6,4},{8,10},{10,8},{12,14},{14,12},{16,18},{18,... | collective-permute-start | bytes 1572872 | tf_op jit(solution)/shard_map/ppermute | solution.py:369
  380.1 14.8 %collective-permute-start.22 = (bf16[256,1024]{1,0:T(8,128)(2,1)S(1)}, bf16[256,1024]{1,0:T(8,128)(2,1)S(1)}, u32[]{:S(2)}, u32[]{:S(2)}) collective-permute-start(bf16[256,1024]{1,0:T(8,128)(2,1)S(1)} %add_convert_fusion.14), channel_id=1, source_target_pairs={{0,1},{1,0},{2,3},{3,2},{4,5},{5,4},{6,7},{7,6},{8,9},{9,8},{10,11... | collective-permute-start | bytes 1572872 | tf_op jit(solution)/shard_map/ppermute | solution.py:369
  385.7 42.9 %collective-permute-start.12 = (bf16[1024,768]{1,0:T(8,128)(2,1)S(1)}, bf16[1024,768]{1,0:T(8,128)(2,1)S(1)}, u32[]{:S(2)}, u32[]{:S(2)}) collective-permute-start(bf16[1024,768]{1,0:T(8,128)(2,1)S(1)} %add_convert_fusion.7), channel_id=1, source_target_pairs={{0,1},{1,0},{2,3},{3,2},{4,5},{5,4},{6,7},{7,6},{8,9},{9,8},{10,11... | collective-permute-start | bytes 4718600 | tf_op jit(solution)/shard_map/ppermute | solution.py:369
  386.3 87.3 %collective-permute-start.32 = (bf16[1024,1024]{1,0:T(8,128)(2,1)S(1)}, bf16[1024,1024]{1,0:T(8,128)(2,1)S(1)}, u32[]{:S(2)}, u32[]{:S(2)}) collective-permute-start(bf16[1024,1024]{1,0:T(8,128)(2,1)S(1)} %add_convert_fusion.3), channel_id=1, source_target_pairs={{0,1},{1,0},{2,3},{3,2},{4,5},{5,4},{6,7},{7,6},{8,9},{9,8},{10,11... | collective-permute-start | bytes 6291464 | tf_op jit(solution)/shard_map/ppermute | solution.py:369
  394.9 83.6 %collective-permute-start.40 = (bf16[1024,1024]{1,0:T(8,128)(2,1)S(1)}, bf16[1024,1024]{1,0:T(8,128)(2,1)S(1)}, u32[]{:S(2)}, u32[]{:S(2)}) collective-permute-start(bf16[1024,1024]{1,0:T(8,128)(2,1)S(1)} %copy-done.73), channel_id=1, source_target_pairs={{0,2},{2,0},{4,6},{6,4},{8,10},{10,8},{12,14},{14,12},{16,18},{18,... | collective-permute-start | bytes 6291464 | tf_op jit(solution)/shard_map/ppermute | solution.py:369
  394.9 123.2 %collective-permute-start.42 = (bf16[1024,1024]{1,0:T(8,128)(2,1)S(1)}, bf16[1024,1024]{1,0:T(8,128)(2,1)S(1)}, u32[]{:S(2)}, u32[]{:S(2)}) collective-permute-start(bf16[1024,1024]{1,0:T(8,128)(2,1)S(1)} %add_convert_fusion.1), channel_id=1, source_target_pairs={{0,1},{1,0},{2,3},{3,2},{4,5},{5,4},{6,7},{7,6},{8,9},{9,8},{10,11... | collective-permute-start | bytes 6291464 | tf_op jit(solution)/shard_map/ppermute | solution.py:369
  428.6 92.7 %collective-permute-start.23 = (bf16[128,1024]{1,0:T(8,128)(2,1)S(1)}, bf16[128,1024]{1,0:T(8,128)(2,1)S(1)}, u32[]{:S(2)}, u32[]{:S(2)}) collective-permute-start(bf16[128,1024]{1,0:T(8,128)(2,1)S(1)} %constant_dynamic-slice_fusion.8), channel_id=1, source_target_pairs={{0,4},{2,6},{4,0},{6,2},{8,12},{10,14},{12,8},{14,10},{16,20},{18,... | collective-permute-start | bytes 786440 | tf_op jit(solution)/shard_map/ppermute | solution.py:369
  430.8 92.2 %collective-permute-start.13 = (bf16[512,768]{1,0:T(8,128)(2,1)S(1)}, bf16[512,768]{1,0:T(8,128)(2,1)S(1)}, u32[]{:S(2)}, u32[]{:S(2)}) collective-permute-start(bf16[512,768]{1,0:T(8,128)(2,1)S(1)} %constant_dynamic-slice_fusion.11), channel_id=1, source_target_pairs={{0,4},{2,6},{4,0},{6,2},{8,12},{10,14},{12,8},{14,10},{16,20},{18,... | collective-permute-start | bytes 2359304 | tf_op jit(solution)/shard_map/ppermute | solution.py:369
  476.9 46.9 %collective-permute-start.33 = (bf16[512,1024]{1,0:T(8,128)(2,1)S(1)}, bf16[512,1024]{1,0:T(8,128)(2,1)S(1)}, u32[]{:S(2)}, u32[]{:S(2)}) collective-permute-start(bf16[512,1024]{1,0:T(8,128)(2,1)S(1)} %constant_dynamic-slice_fusion.5), channel_id=1, source_target_pairs={{0,4},{2,6},{4,0},{6,2},{8,12},{10,14},{12,8},{14,10},{16,20},{18,... | collective-permute-start | bytes 3145736 | tf_op jit(solution)/shard_map/ppermute | solution.py:369
  519.7 24.9 %collective-permute-start.43 = (bf16[512,1024]{1,0:T(8,128)(2,1)S(1)}, bf16[512,1024]{1,0:T(8,128)(2,1)S(1)}, u32[]{:S(2)}, u32[]{:S(2)}) collective-permute-start(bf16[512,1024]{1,0:T(8,128)(2,1)S(1)} %constant_dynamic-slice_fusion.2), channel_id=1, source_target_pairs={{0,4},{2,6},{4,0},{6,2},{8,12},{10,14},{12,8},{14,10},{16,20},{18,... | collective-permute-start | bytes 3145736 | tf_op jit(solution)/shard_map/ppermute | solution.py:369
  521.4 90.9 %collective-permute-start.24 = (bf16[64,1024]{1,0:T(8,128)(2,1)S(1)}, bf16[64,1024]{1,0:T(8,128)(2,1)S(1)}, u32[]{:S(2)}, u32[]{:S(2)}) collective-permute-start(bf16[64,1024]{1,0:T(8,128)(2,1)S(1)} %constant_dynamic-slice_fusion.7), channel_id=1, source_target_pairs={{0,8},{2,10},{4,12},{6,14},{8,0},{10,2},{12,4},{14,6},{16,24},{18,... | collective-permute-start | bytes 393224 | tf_op jit(solution)/shard_map/ppermute | solution.py:369
  523.3 23.4 %collective-permute-start.14 = (bf16[256,768]{1,0:T(8,128)(2,1)S(1)}, bf16[256,768]{1,0:T(8,128)(2,1)S(1)}, u32[]{:S(2)}, u32[]{:S(2)}) collective-permute-start(bf16[256,768]{1,0:T(8,128)(2,1)S(1)} %constant_dynamic-slice_fusion.10), channel_id=1, source_target_pairs={{0,8},{2,10},{4,12},{6,14},{8,0},{10,2},{12,4},{14,6},{16,24},{18,... | collective-permute-start | bytes 1179656 | tf_op jit(solution)/shard_map/ppermute | solution.py:369
  524.3 25.2 %collective-permute-start.34 = (bf16[256,1024]{1,0:T(8,128)(2,1)S(1)}, bf16[256,1024]{1,0:T(8,128)(2,1)S(1)}, u32[]{:S(2)}, u32[]{:S(2)}) collective-permute-start(bf16[256,1024]{1,0:T(8,128)(2,1)S(1)} %constant_dynamic-slice_fusion.4), channel_id=1, source_target_pairs={{0,8},{2,10},{4,12},{6,14},{8,0},{10,2},{12,4},{14,6},{16,24},{18,... | collective-permute-start | bytes 1572872 | tf_op jit(solution)/shard_map/ppermute | solution.py:369
  545.1 22.6 %collective-permute-start.44 = (bf16[256,1024]{1,0:T(8,128)(2,1)S(1)}, bf16[256,1024]{1,0:T(8,128)(2,1)S(1)}, u32[]{:S(2)}, u32[]{:S(2)}) collective-permute-start(bf16[256,1024]{1,0:T(8,128)(2,1)S(1)} %constant_dynamic-slice_fusion.1), channel_id=1, source_target_pairs={{0,8},{2,10},{4,12},{6,14},{8,0},{10,2},{12,4},{14,6},{16,24},{18,... | collective-permute-start | bytes 1572872 | tf_op jit(solution)/shard_map/ppermute | solution.py:369
  546.9 22.9 %collective-permute-start.15 = (bf16[128,768]{1,0:T(8,128)(2,1)S(1)}, bf16[128,768]{1,0:T(8,128)(2,1)S(1)}, u32[]{:S(2)}, u32[]{:S(2)}) collective-permute-start(bf16[128,768]{1,0:T(8,128)(2,1)S(1)} %constant_dynamic-slice_fusion.9), channel_id=1, source_target_pairs={{0,16},{2,18},{4,20},{6,22},{8,24},{10,26},{12,28},{14,30},{16,0},... | collective-permute-start | bytes 589832 | tf_op jit(solution)/shard_map/ppermute | solution.py:369
  549.8 21.3 %collective-permute-start.35 = (bf16[128,1024]{1,0:T(8,128)(2,1)S(1)}, bf16[128,1024]{1,0:T(8,128)(2,1)S(1)}, u32[]{:S(2)}, u32[]{:S(2)}) collective-permute-start(bf16[128,1024]{1,0:T(8,128)(2,1)S(1)} %constant_dynamic-slice_fusion.3), channel_id=1, source_target_pairs={{0,16},{2,18},{4,20},{6,22},{8,24},{10,26},{12,28},{14,30},{16,0},... | collective-permute-start | bytes 786440 | tf_op jit(solution)/shard_map/ppermute | solution.py:369
  568.0 24.4 %collective-permute-start.45 = (bf16[128,1024]{1,0:T(8,128)(2,1)S(1)}, bf16[128,1024]{1,0:T(8,128)(2,1)S(1)}, u32[]{:S(2)}, u32[]{:S(2)}) collective-permute-start(bf16[128,1024]{1,0:T(8,128)(2,1)S(1)} %constant_dynamic-slice_fusion), channel_id=1, source_target_pairs={{0,16},{2,18},{4,20},{6,22},{8,24},{10,26},{12,28},{14,30},{16,0},... | collective-permute-start | bytes 786440 | tf_op jit(solution)/shard_map/ppermute | solution.py:369
  569.9 32.3 %collective-permute-start.16 = (bf16[128,768]{1,0:T(8,128)(2,1)S(1)}, bf16[128,768]{1,0:T(8,128)(2,1)S(1)}, u32[]{:S(2)}, u32[]{:S(2)}) collective-permute-start(bf16[128,768]{1,0:T(8,128)(2,1)S(1)} %add_convert_fusion.19), channel_id=1, source_target_pairs={{0,16},{2,18},{4,20},{6,22},{8,24},{10,26},{12,28},{14,30},{16,0},... | collective-permute-start | bytes 589832 | tf_op jit(solution)/shard_map/ppermute | solution.py:369
  571.2 36.7 %collective-permute-start.36 = (bf16[128,1024]{1,0:T(8,128)(2,1)S(1)}, bf16[128,1024]{1,0:T(8,128)(2,1)S(1)}, u32[]{:S(2)}, u32[]{:S(2)}) collective-permute-start(bf16[128,1024]{1,0:T(8,128)(2,1)S(1)} %add_convert_fusion.17), channel_id=1, source_target_pairs={{0,16},{2,18},{4,20},{6,22},{8,24},{10,26},{12,28},{14,30},{16,0},... | collective-permute-start | bytes 786440 | tf_op jit(solution)/shard_map/ppermute | solution.py:369
  592.4 19.6 %collective-permute-start.46 = (bf16[128,1024]{1,0:T(8,128)(2,1)S(1)}, bf16[128,1024]{1,0:T(8,128)(2,1)S(1)}, u32[]{:S(2)}, u32[]{:S(2)}) collective-permute-start(bf16[128,1024]{1,0:T(8,128)(2,1)S(1)} %add_convert_fusion.16), channel_id=1, source_target_pairs={{0,16},{2,18},{4,20},{6,22},{8,24},{10,26},{12,28},{14,30},{16,0},... | collective-permute-start | bytes 786440 | tf_op jit(solution)/shard_map/ppermute | solution.py:369
  602.3 18.1 %collective-permute-start.17 = (bf16[256,768]{1,0:T(8,128)(2,1)S(1)}, bf16[256,768]{1,0:T(8,128)(2,1)S(1)}, u32[]{:S(2)}, u32[]{:S(2)}) collective-permute-start(bf16[256,768]{1,0:T(8,128)(2,1)S(1)} %maximum_select_fusion.15), channel_id=1, source_target_pairs={{0,8},{2,10},{4,12},{6,14},{8,0},{10,2},{12,4},{14,6},{16,24},{18,... | collective-permute-start | bytes 1179656 | tf_op jit(solution)/shard_map/ppermute | solution.py:369
  608.0 23.6 %collective-permute-start.37 = (bf16[256,1024]{1,0:T(8,128)(2,1)S(1)}, bf16[256,1024]{1,0:T(8,128)(2,1)S(1)}, u32[]{:S(2)}, u32[]{:S(2)}) collective-permute-start(bf16[256,1024]{1,0:T(8,128)(2,1)S(1)} %maximum_select_fusion.13), channel_id=1, source_target_pairs={{0,8},{2,10},{4,12},{6,14},{8,0},{10,2},{12,4},{14,6},{16,24},{18,... | collective-permute-start | bytes 1572872 | tf_op jit(solution)/shard_map/ppermute | solution.py:369
  612.1 32.1 %collective-permute-start.47 = (bf16[256,1024]{1,0:T(8,128)(2,1)S(1)}, bf16[256,1024]{1,0:T(8,128)(2,1)S(1)}, u32[]{:S(2)}, u32[]{:S(2)}) collective-permute-start(bf16[256,1024]{1,0:T(8,128)(2,1)S(1)} %maximum_select_fusion.14), channel_id=1, source_target_pairs={{0,8},{2,10},{4,12},{6,14},{8,0},{10,2},{12,4},{14,6},{16,24},{18,... | collective-permute-start | bytes 1572872 | tf_op jit(solution)/shard_map/ppermute | solution.py:369
  620.7 31.8 %collective-permute-start.18 = (bf16[512,768]{1,0:T(8,128)(2,1)S(1)}, bf16[512,768]{1,0:T(8,128)(2,1)S(1)}, u32[]{:S(2)}, u32[]{:S(2)}) collective-permute-start(bf16[512,768]{1,0:T(8,128)(2,1)S(1)} %maximum_select_fusion.11), channel_id=1, source_target_pairs={{0,4},{2,6},{4,0},{6,2},{8,12},{10,14},{12,8},{14,10},{16,20},{18,... | collective-permute-start | bytes 2359304 | tf_op jit(solution)/shard_map/ppermute | solution.py:369
  632.1 31.6 %collective-permute-start.38 = (bf16[512,1024]{1,0:T(8,128)(2,1)S(1)}, bf16[512,1024]{1,0:T(8,128)(2,1)S(1)}, u32[]{:S(2)}, u32[]{:S(2)}) collective-permute-start(bf16[512,1024]{1,0:T(8,128)(2,1)S(1)} %maximum_select_fusion.9), channel_id=1, source_target_pairs={{0,4},{2,6},{4,0},{6,2},{8,12},{10,14},{12,8},{14,10},{16,20},{18,... | collective-permute-start | bytes 3145736 | tf_op jit(solution)/shard_map/ppermute | solution.py:369
  633.7 12.5 %collective-permute-start.25 = (bf16[32,1024]{1,0:T(8,128)(2,1)S(1)}, bf16[32,1024]{1,0:T(8,128)(2,1)S(1)}, u32[]{:S(2)}, u32[]{:S(2)}) collective-permute-start(bf16[32,1024]{1,0:T(8,128)(2,1)S(1)} %constant_dynamic-slice_fusion.6), channel_id=1, source_target_pairs={{0,16},{2,18},{4,20},{6,22},{8,24},{10,26},{12,28},{14,30},{16,0},... | collective-permute-start | bytes 196616 | tf_op jit(solution)/shard_map/ppermute | solution.py:369
  644.7 47.0 %collective-permute-start.48 = (bf16[512,1024]{1,0:T(8,128)(2,1)S(1)}, bf16[512,1024]{1,0:T(8,128)(2,1)S(1)}, u32[]{:S(2)}, u32[]{:S(2)}) collective-permute-start(bf16[512,1024]{1,0:T(8,128)(2,1)S(1)} %maximum_select_fusion.10), channel_id=1, source_target_pairs={{0,4},{2,6},{4,0},{6,2},{8,12},{10,14},{12,8},{14,10},{16,20},{18,... | collective-permute-start | bytes 3145736 | tf_op jit(solution)/shard_map/ppermute | solution.py:369
  654.3 94.4 %collective-permute-start.19 = (bf16[1024,768]{1,0:T(8,128)(2,1)}, bf16[1024,768]{1,0:T(8,128)(2,1)}, u32[]{:S(2)}, u32[]{:S(2)}) collective-permute-start(bf16[1024,768]{1,0:T(8,128)(2,1)} %maximum_select_fusion.4), channel_id=1, source_target_pairs={{0,2},{2,0},{4,6},{6,4},{8,10},{10,8},{12,14},{14,12},{16,18},{18,... | collective-permute-start | bytes 4718600 | tf_op jit(solution)/shard_map/ppermute | solution.py:369
  657.5 33.2 %collective-permute-start.28 = (bf16[128,1024]{1,0:T(8,128)(2,1)S(1)}, bf16[128,1024]{1,0:T(8,128)(2,1)S(1)}, u32[]{:S(2)}, u32[]{:S(2)}) collective-permute-start(bf16[128,1024]{1,0:T(8,128)(2,1)S(1)} %maximum_select_fusion.16), channel_id=1, source_target_pairs={{0,4},{2,6},{4,0},{6,2},{8,12},{10,14},{12,8},{14,10},{16,20},{18,... | collective-permute-start | bytes 786440 | tf_op jit(solution)/shard_map/ppermute | solution.py:369
  664.7 91.0 %collective-permute-start.39 = (bf16[1024,1024]{1,0:T(8,128)(2,1)S(1)}, bf16[1024,1024]{1,0:T(8,128)(2,1)}, u32[]{:S(2)}, u32[]{:S(2)}) collective-permute-start(bf16[1024,1024]{1,0:T(8,128)(2,1)S(1)} %maximum_select_fusion.2), channel_id=1, source_target_pairs={{0,2},{2,0},{4,6},{6,4},{8,10},{10,8},{12,14},{14,12},{16,18},{18,... | collective-permute-start | bytes 6291464 | tf_op jit(solution)/shard_map/ppermute | solution.py:369
  691.7 52.3 %collective-permute-start.29 = (bf16[256,1024]{1,0:T(8,128)(2,1)}, bf16[256,1024]{1,0:T(8,128)(2,1)}, u32[]{:S(2)}, u32[]{:S(2)}) collective-permute-start(bf16[256,1024]{1,0:T(8,128)(2,1)} %maximum_select_fusion.12), channel_id=1, source_target_pairs={{0,2},{2,0},{4,6},{6,4},{8,10},{10,8},{12,14},{14,12},{16,18},{18,... | collective-permute-start | bytes 1572872 | tf_op jit(solution)/shard_map/ppermute | solution.py:369
  694.0 67.9 %collective-permute-start.49 = (bf16[1024,1024]{1,0:T(8,128)(2,1)}, bf16[1024,1024]{1,0:T(8,128)(2,1)}, u32[]{:S(2)}, u32[]{:S(2)}) collective-permute-start(bf16[1024,1024]{1,0:T(8,128)(2,1)} %maximum_select_fusion.3), channel_id=1, source_target_pairs={{0,2},{2,0},{4,6},{6,4},{8,10},{10,8},{12,14},{14,12},{16,18},{18,... | collective-permute-start | bytes 6291464 | tf_op jit(solution)/shard_map/ppermute | solution.py:369
  (82 other events, 832.6 us)

commit v2 on v0

--- a/solution.py
+++ b/solution.py
@@ -1,11 +1,18 @@
 import jax
 import jax.numpy as jnp
 from jax import lax
+from jax.experimental import pallas as pl
+from jax.experimental.pallas import tpu as pltpu
 from jax.sharding import PartitionSpec as P
 
 HD = 64
 BLOCK = 64
 SEQ = 1024
+PAIR = 2 * HD
+BF16 = jnp.bfloat16
+F32 = jnp.float32
+NT = (((1,), (1,)), ((), ()))
+TN = (((0,), (0,)), ((), ()))
 
 
 def layer_norm(values, norm_gain, norm_bias):
@@ -30,7 +37,7 @@
     return jnp.repeat(jnp.repeat(allowed, BLOCK, axis=1), BLOCK, axis=2)
 
 
-def attend_forward(joined_seq, allowed, scaling):
+def attend_forward_split(joined_seq, allowed, scaling):
     queries = joined_seq[:, 0]
     key_rows = joined_seq[:, 1]
     value_rows = joined_seq[:, 2]
@@ -46,7 +53,7 @@
     return (context.astype(jnp.bfloat16), (highest + jnp.log(row_totals))[..., 0])
 
 
-def attend_backward(seq_items, allowed, scaling):
+def attend_backward_split(seq_items, allowed, scaling):
     joined_seq, grad_context, row_lse = seq_items
     queries = joined_seq[:, 0]
     key_rows = joined_seq[:, 1]
@@ -78,7 +85,7 @@
     return jnp.stack([grad_queries, grad_keys, grad_values], axis=1)
 
 
-def per_device(
+def split_sequence(
     hidden_in,
     out_grad,
     ln1_gain,
@@ -108,7 +115,7 @@
     joined = jnp.dot(rows_one, w_joined, preferred_element_type=jnp.float32).astype(jnp.bfloat16)
     joined_seq = joined.reshape(seq_count, SEQ, 3, local_heads, HD)
     context, row_lse = lax.map(
-        lambda seq_block: attend_forward(seq_block, allowed, scaling), joined_seq
+        lambda seq_block: attend_forward_split(seq_block, allowed, scaling), joined_seq
     )
     context_rows = context.reshape(seq_count * SEQ, head_width)
     middle = inputs + lax.psum_scatter(
@@ -162,7 +169,7 @@
         "ne,nd->ed", context_rows, rows_attn, preferred_element_type=jnp.float32
     )
     grad_joined = lax.map(
-        lambda seq_items: attend_backward(seq_items, allowed, scaling),
+        lambda seq_items: attend_backward_split(seq_items, allowed, scaling),
         (joined_seq, grad_context.reshape(seq_count, SEQ, local_heads, HD), row_lse),
     )
     grad_joined = grad_joined.reshape(seq_count * SEQ, 3 * head_width)
@@ -211,6 +218,768 @@
     )
 
 
+VMEM_LIMIT = 56 << 20
+TILE = 256
+PACE = 0.02
+
+
+def mm(left, right, dims=(((1,), (0,)), ((), ()))):
+    return lax.dot_general(left, right, dims, preferred_element_type=F32)
+
+
+def call(body, *, grid, in_specs, out_specs, out_shape, micros, name, scratch=(), scalars=1):
+    return pl.pallas_call(
+        body,
+        grid_spec=pltpu.PrefetchScalarGridSpec(
+            num_scalar_prefetch=scalars,
+            grid=grid,
+            in_specs=in_specs,
+            out_specs=out_specs,
+            scratch_shapes=list(scratch),
+        ),
+        out_shape=out_shape,
+        compiler_params=pltpu.CompilerParams(vmem_limit_bytes=VMEM_LIMIT),
+        cost_estimate=pl.CostEstimate(
+            flops=int(micros * PACE * 1e9), bytes_accessed=0, transcendentals=0
+        ),
+        name=name,
+    )
+
+
+def shape(rows, columns, dtype=BF16):
+    return jax.ShapeDtypeStruct((rows, columns), dtype)
+
+
+def row_tile(width, dtype=None):
+    return pl.BlockSpec((TILE, width), lambda i, s: (i, 0))
+
+
+def column_tile(height):
+    return pl.BlockSpec((height, TILE), lambda i, s: (0, i))
+
+
+def resident(rows, columns):
+    return pl.BlockSpec((rows, columns), lambda i, s: (0, 0))
+
+
+def norm_parts(values):
+    center = values - jnp.mean(values, axis=-1, keepdims=True)
+    spread = jnp.mean(center * center, axis=-1, keepdims=True)
+    return center, lax.rsqrt(spread + 1e-05)
+
+
+def norm_backward(values, gain, grads):
+    center, scale = norm_parts(values)
+    unit = center * scale
+    scaled = grads * gain
+    mean_g = jnp.mean(scaled, axis=-1, keepdims=True)
+    mean_gu = jnp.mean(scaled * unit, axis=-1, keepdims=True)
+    grad_in = scale * (scaled - mean_g - unit * mean_gu)
+    return (
+        grad_in,
+        jnp.sum(grads * unit, axis=0, keepdims=True),
+        jnp.sum(grads, axis=0, keepdims=True),
+    )
+
+
+def flipped(rows):
+    return rows.astype(F32).T.astype(BF16)
+
+
+def accumulate(ref, value):
+    @pl.when(pl.program_id(0) == 0)
+    def _():
+        ref[...] = value
+
+    @pl.when(pl.program_id(0) > 0)
+    def _():
+        ref[...] += value
+
+
+def norm_in_kernel(s, x_ref, g_ref, gain_ref, bias_ref, n_ref, nt_ref, gt_ref, sum_ref):
+    center, scale = norm_parts(x_ref[...].astype(F32))
+    normed = center * scale * gain_ref[...] + bias_ref[...]
+    n_ref[...] = normed.astype(BF16)
+    nt_ref[...] = flipped(n_ref[...])
+    grads = g_ref[...]
+    gt_ref[...] = flipped(grads)
+    accumulate(sum_ref, jnp.sum(grads.astype(F32), axis=0, keepdims=True))
+
+
+def norm_in(place, hidden_in, out_grad, gain, bias):
+    rows, width = hidden_in.shape
+    return call(
+        norm_in_kernel,
+        grid=(rows // TILE,),
+        in_specs=[row_tile(width), row_tile(width), resident(1, width), resident(1, width)],
+        out_specs=[row_tile(width), column_tile(width), column_tile(width), resident(1, width)],
+        out_shape=[shape(rows, width), shape(width, rows), shape(width, rows), shape(1, width, F32)],
+        micros=5,
+        name="norm_in",
+    )(place, hidden_in, out_grad, gain, bias)
+
+
+def head_lanes(rows, head):
+    lanes = lax.broadcasted_iota(jnp.int32, rows.shape, 1)
+    return jnp.where(lanes // HD == head, rows, jnp.zeros_like(rows))
+
+
+def masked_scores(key_rows, queries, bias):
+    scores = mm(key_rows, queries, NT)
+    keys, width = scores.shape
+    blocked = scores.reshape(keys // BLOCK, BLOCK, width) + bias[:, None, :]
+    return blocked.reshape(keys, width)
+
+
+def attend_forward_kernel(s, q_ref, k_ref, v_ref, bias_ref, context_ref, lse_ref):
+    scaling = HD ** (-0.5)
+    key_rows = k_ref[...]
+    values_t = flipped(v_ref[...])
+    for start in range(0, q_ref.shape[0], TILE):
+        rows = slice(start, start + TILE)
+        queries = q_ref[rows, :] * jnp.asarray(scaling, BF16)
+        parts = []
+        for head in range(2):
+            scores = masked_scores(key_rows, head_lanes(queries, head), bias_ref[head, :, rows])
+            highest = jnp.max(scores, axis=0, keepdims=True)
+            shifted = jnp.exp(scores - highest)
+            totals = jnp.sum(shifted, axis=0, keepdims=True)
+            summed = mm(values_t[head * HD : (head + 1) * HD], shifted.astype(BF16))
+            parts.append(summed / totals)
+            lse_ref[0, head : head + 1, rows] = highest + jnp.log(totals)
+        context_ref[rows, :] = jnp.concatenate(parts, axis=0).T.astype(BF16)
+
+
+def thin_block(column):
+    return pl.BlockSpec((SEQ, PAIR), lambda p, s: (0, column(p)))
+
+
+def attend_forward(place, which, qkv, bias):
+    pairs = 2
+    blocks = SEQ // BLOCK
+    return call(
+        attend_forward_kernel,
+        grid=(pairs,),
+        in_specs=[
+            thin_block(lambda p: p),
+            thin_block(lambda p: pairs + p),
+            thin_block(lambda p: 2 * pairs + p),
+            pl.BlockSpec((2, blocks, SEQ), lambda p, s: (s[which % 2] * pairs + p, 0, 0)),
+        ],
+        out_specs=[thin_block(lambda p: p), pl.BlockSpec((1, 2, SEQ), lambda p, s: (p, 0, 0))],
+        out_shape=[shape(SEQ, pairs * PAIR), jax.ShapeDtypeStruct((pairs, 2, SEQ), F32)],
+        micros=12,
+        name="attend_forward",
+    )(place, qkv, qkv, qkv, bias)
+
+
+def attend_backward_kernel(
+    s, q_ref, k_ref, v_ref, grad_ref, context_ref, lse_ref, bias_ref, out_ref, key_acc, value_acc
+):
+    scaling = HD ** (-0.5)
+    key_rows = k_ref[...]
+    value_rows = v_ref[...]
+    keys_t = flipped(key_rows)
+    for start in range(0, q_ref.shape[0], TILE):
+        rows = slice(start, start + TILE)
+        queries = q_ref[rows, :] * jnp.asarray(scaling, BF16)
+        grads = grad_ref[rows, :]
+        inner_t = (grads.astype(F32) * context_ref[rows, :].astype(F32)).T
+        probs, slopes, masked_q, masked_g, parts = [], [], [], [], []
+        for head in range(2):
+            query_h, grad_h = head_lanes(queries, head), head_lanes(grads, head)
+            scores = masked_scores(key_rows, query_h, bias_ref[head, :, rows])
+            attn = jnp.exp(scores - lse_ref[0, head : head + 1, rows])
+            inner = jnp.sum(inner_t[head * HD : (head + 1) * HD], axis=0, keepdims=True)
+            slope = (attn * (mm(value_rows, grad_h, NT) - inner)).astype(BF16)
+            parts.append(mm(keys_t[head * HD : (head + 1) * HD], slope) * scaling)
+            probs.append(attn.astype(BF16))
+            slopes.append(slope)
+            masked_q.append(query_h)
+            masked_g.append(grad_h)
+        out_ref[rows, :PAIR] = jnp.concatenate(parts, axis=0).T.astype(BF16)
+        grad_k = mm(jnp.concatenate(slopes, axis=1), jnp.concatenate(masked_q, axis=0))
+        grad_v = mm(jnp.concatenate(probs, axis=1), jnp.concatenate(masked_g, axis=0))
+        if start == 0:
+            key_acc[...] = grad_k
+            value_acc[...] = grad_v
+        else:
+            key_acc[...] += grad_k
+            value_acc[...] += grad_v
+    out_ref[:, PAIR : 2 * PAIR] = key_acc[...].astype(BF16)
+    out_ref[:, 2 * PAIR :] = value_acc[...].astype(BF16)
+
+
+def attend_backward(place, which, pair, qkv, grad_context, context, row_lse, bias):
+    pairs = 2
+    blocks = SEQ // BLOCK
+    return call(
+        attend_backward_kernel,
+        grid=(1,),
+        in_specs=[
+            thin_block(lambda p: pair),
+            thin_block(lambda p: pairs + pair),
+            thin_block(lambda p: 2 * pairs + pair),
+            thin_block(lambda p: pair),
+            thin_block(lambda p: pair),
+            pl.BlockSpec((1, 2, SEQ), lambda p, s: (pair, 0, 0)),
+            pl.BlockSpec((2, blocks, SEQ), lambda p, s: (s[which % 2] * pairs + pair, 0, 0)),
+        ],
+        out_specs=pl.BlockSpec((SEQ, 3 * PAIR), lambda p, s: (0, 0)),
+        out_shape=shape(SEQ, 3 * PAIR),
+        scratch=[pltpu.VMEM((SEQ, PAIR), F32), pltpu.VMEM((SEQ, PAIR), F32)],
+        micros=8,
+        name="attend_backward",
+    )(place, qkv, qkv, qkv, grad_context, context, row_lse, bias)
+
+
+def project_out_kernel(s, x_ref, *refs):
+    contexts, weights = refs[:4], refs[4:8]
+    gain_ref, bias_ref, middle_ref, n_ref, nt_ref = refs[8:]
+    middle = x_ref[...].astype(F32)
+    for context_ref, w_ref in zip(contexts, weights):
+        middle = middle + mm(context_ref[...], w_ref[...])
+    middle_ref[...] = middle
+    center, scale = norm_parts(middle)
+    normed = (center * scale * gain_ref[...] + bias_ref[...]).astype(BF16)
+    n_ref[...] = normed
+    nt_ref[...] = flipped(normed)
+
+
+def own_then_far(block, along):
+    specs = []
+    for which in range(4):
+        if along == 0:
+            specs.append(pl.BlockSpec(block, lambda i, s, which=which: (s[which], 0)))
+        else:
+            specs.append(pl.BlockSpec(block, lambda i, s, which=which: (0, s[which])))
+    return specs
+
+
+def project_out(place, hidden_in, contexts, weights, gain, bias):
+    rows, width = hidden_in.shape
+    return call(
+        project_out_kernel,
+        grid=(rows // TILE,),
+        in_specs=[row_tile(width)]
+        + [row_tile(2 * PAIR)] * 4
+        + own_then_far((2 * PAIR, width), 0)
+        + [resident(1, width)] * 2,
+        out_specs=[row_tile(width), row_tile(width), column_tile(width)],
+        out_shape=[shape(rows, width, F32), shape(rows, width), shape(width, rows)],
+        micros=7,
+        name="project_out",
+    )(place, hidden_in, *contexts, *weights, gain, bias)
+
+
+def gelu_and_slope(pre):
+    root, cubic = 0.7978845608028654, 0.044715
+    square = pre * pre
+    bent = jnp.tanh(root * (pre + cubic * pre * square))
+    half = 0.5 * pre
+    slope = 0.5 * (1.0 + bent) + half * (1.0 - bent * bent) * (root * (1.0 + 3.0 * cubic * square))
+    return half + half * bent, slope
+
+
+def feed_forward_kernel(tiles, s, n_ref, g_ref, bias_ref, *refs):
+    ups, downs = refs[: len(refs) // 2 - 1], refs[len(refs) // 2 - 1 : -3]
+    h_ref, gu_ref, sum_ref = refs[-3:]
+
+    def run(up_ref, down_ref):
+        pre = mm(n_ref[...], up_ref[...]) + bias_ref[...]
+        grad_hidden = mm(g_ref[...], down_ref[...], NT)
+        value, slope = gelu_and_slope(pre)
+        h_ref[...] = value.astype(BF16)
+        grad_up = (grad_hidden * slope).astype(BF16)
+        gu_ref[...] = grad_up
+        sum_ref[...] = jnp.sum(grad_up.astype(F32), axis=0, keepdims=True)
+
+    if len(ups) == 1:
+        run(ups[0], downs[0])
+    else:
+        mine = pl.program_id(0) // (tiles // 2) == s[4]
+
+        @pl.when(mine)
+        def _():
+            run(ups[0], downs[0])
+
+        @pl.when(jnp.logical_not(mine))
+        def _():
+            run(ups[1], downs[1])
+
+
+def feed_forward(place, which, normed, out_grad, w_up, b_up, w_down):
+    rows, width = normed.shape
+    units = b_up.shape[1] // 2
+    tiles = units // TILE
+    if which < 2:
+        columns = [lambda i, s: (0, s[which] * tiles + i)]
+        lines = [lambda i, s: (s[which] * tiles + i, 0)]
+    else:
+        columns = [lambda i, s: (0, i % (tiles // 2))] * 2
+        lines = [lambda i, s: (i % (tiles // 2), 0)] * 2
+    return call(
+        lambda *refs: feed_forward_kernel(tiles, *refs),
+        grid=(tiles,),
+        in_specs=[
+            resident(rows, width),
+            resident(rows, width),
+            pl.BlockSpec((1, TILE), lambda i, s: (0, s[which % 2] * tiles + i)),
+        ]
+        + [pl.BlockSpec((width, TILE), column) for column in columns]
+        + [pl.BlockSpec((TILE, width), line) for line in lines],
+        out_specs=[column_tile(rows), column_tile(rows), column_tile(1)],
+        out_shape=[shape(rows, units), shape(rows, units), shape(1, units, F32)],
+        micros=12,
+        name="feed_forward",
+    )(place, normed, out_grad, b_up, *w_up, *w_down)
+
+
+def unit_blocks(units, width, along):
+    half = units // 2
+    rows = [pl.BlockSpec((TILE, units), lambda i, s: (i, 0))] * 2
+    rows += [
+        pl.BlockSpec((TILE, half), lambda i, s: (i, s[4])),
+        pl.BlockSpec((TILE, half), lambda i, s: (i, 1 - s[4])),
+    ] * 2
+    if along == 0:
+        own = [
+            pl.BlockSpec((units, width), lambda i, s, which=which: (s[which], 0)) for which in (0, 1)
+        ]
+        return rows + own + [resident(half, width)] * 4
+    own = [pl.BlockSpec((width, units), lambda i, s, which=which: (0, s[which])) for which in (0, 1)]
+    return rows + own + [resident(width, half)] * 4
+
+
+def unit_arrays(slices, weights):
+    own_a, own_b, far_a, far_b = slices
+    return [own_a, own_b, far_a, far_a, far_b, far_b] + [part for group in weights for part in group]
+
+
+def middle_back_kernel(s, g_ref, middle_ref, gain_ref, *refs):
+    grads, weights = refs[:6], refs[6:12]
+    gm_ref, ga_ref, gat_ref, gain_sum, bias_sum = refs[12:]
+    total = mm(grads[0][...], weights[0][...], NT)
+    for grad_ref, w_ref in zip(grads[1:], weights[1:]):
+        total = total + mm(grad_ref[...], w_ref[...], NT)
+    grad_in, gain, bias = norm_backward(middle_ref[...], gain_ref[...], total)
+    grad_middle = g_ref[...].astype(F32) + grad_in
+    gm_ref[...] = grad_middle
+    ga_ref[...] = grad_middle.astype(BF16)
+    gat_ref[...] = flipped(ga_ref[...])
+    accumulate(gain_sum, gain)
+    accumulate(bias_sum, bias)
+
+
+def middle_back(place, out_grad, middle, gain, grad_up, weights):
+    rows, width = middle.shape
+    units = grad_up[0].shape[1]
+    return call(
+        middle_back_kernel,
+        grid=(rows // TILE,),
+        in_specs=[row_tile(width), row_tile(width), resident(1, width)]
+        + unit_blocks(units, width, 1),
+        out_specs=[row_tile(width), row_tile(width), column_tile(width)] + [resident(1, width)] * 2,
+        out_shape=[shape(rows, width, F32), shape(rows, width), shape(width, rows)]
+        + [shape(1, width, F32)] * 2,
+        micros=18,
+        name="middle_back",
+    )(place, out_grad, middle, gain, *unit_arrays(grad_up, weights))
+
+
+def input_back_kernel(s, x_ref, gm_ref, gain_ref, *refs):
+    grads, weights = refs[:8], refs[8:12]
+    out_ref, gain_sum, bias_sum = refs[12:]
+    total = None
+    for group in range(4):
+        pair_0, pair_1 = grads[2 * group][...], grads[2 * group + 1][...]
+        joined = jnp.concatenate(
+            [
+                pair[:, part * PAIR : (part + 1) * PAIR]
+                for part in range(3)
+                for pair in (pair_0, pair_1)
+            ],
+            axis=1,
+        )
+        product = mm(joined, weights[group][...], NT)
+        total = product if total is None else total + product
+    grad_in, gain, bias = norm_backward(x_ref[...].astype(F32), gain_ref[...], total)
+    out_ref[...] = gm_ref[...] + grad_in
+    accumulate(gain_sum, gain)
+    accumulate(bias_sum, bias)
+
+
+def input_back(place, hidden_in, grad_middle, gain, grads, weights):
+    rows, width = hidden_in.shape
+    return call(
+        input_back_kernel,
+        grid=(rows // TILE,),
+        in_specs=[row_tile(width), row_tile(width), resident(1, width)]
+        + [row_tile(3 * PAIR)] * 8
+        + [resident(width, 6 * PAIR)] * 4,
+        out_specs=[row_tile(width)] + [resident(1, width)] * 2,
+        out_shape=[shape(rows, width, F32)] + [shape(1, width, F32)] * 2,
+        micros=15,
+        name="input_back",
+    )(place, hidden_in, grad_middle, gain, *grads, *weights)
+
+
+def project_down_kernel(s, middle_ref, bias_ref, *refs):
+    hidden, weights, out_ref = refs[:6], refs[6:12], refs[12]
+    total = middle_ref[...] + bias_ref[...]
+    for h_ref, w_ref in zip(hidden, weights):
+        total = total + mm(h_ref[...], w_ref[...])
+    out_ref[...] = total.astype(BF16)
+
+
+def project_down(place, middle, bias, hidden, weights):
+    rows, width = middle.shape
+    units = hidden[0].shape[1]
+    return call(
+        project_down_kernel,
+        grid=(rows // TILE,),
+        in_specs=[row_tile(width), resident(1, width)] + unit_blocks(units, width, 0),
+        out_specs=row_tile(width),
+        out_shape=shape(rows, width),
+        micros=15,
+        name="project_down",
+    )(place, middle, bias, *unit_arrays(hidden, weights))
+
+
+def block_bias(rand_blocks):
+    blocks = SEQ // BLOCK
+    row_ids = jnp.arange(blocks)[None, :]
+    col_ids = jnp.arange(blocks)[:, None]
+    window = (
+        (jnp.abs(row_ids - col_ids) <= 1)
+        | (col_ids == 0)
+        | (col_ids == blocks - 1)
+        | (row_ids == 0)
+        | (row_ids == blocks - 1)
+    )
+    picked = jnp.any(rand_blocks[:, None, :, :] == col_ids[None, :, :, None], axis=3)
+    bias = jnp.where(window[None] | picked, 0.0, -1e30).astype(F32)
+    return jnp.repeat(bias, BLOCK, axis=2)
+
+
+def swap(array, axis, bit):
+    size = lax.axis_size(axis)
+    return lax.ppermute(array, axis, [(place, place ^ bit) for place in range(size)])
+
+
+def halves_in_order(mine, other, bit, axis=0):
+    return jnp.where(
+        bit == 0,
+        jnp.concatenate([mine, other], axis=axis),
+        jnp.concatenate([other, mine], axis=axis),
+    )
+
+
+def add_up(*terms):
+    total = terms[0].astype(F32)
+    for term in terms[1:]:
+        total = total + term.astype(F32)
+    return total.astype(terms[0].dtype)
+
+
+def half_of(array, bit):
+    rows = array.shape[-2] // 2
+    return lax.dynamic_slice_in_dim(array, bit * rows, rows, array.ndim - 2)
+
+
+class Sum:
+    def __init__(self, order):
+        self.plan = ["cores"]
+        self.plan += [step if step == "mp" else ("halve", step) for step in order]
+        self.plan += [("join", step) for step in reversed(order) if step != "mp"]
+        self.plan += ["finish"]
+        self.moving = None
+
+    def feed(self, own_a, own_b, far_a, far_b):
+        self.parts = own_a, own_b, far_a, far_b
+
+    def issue(self):
+        step = self.plan[0]
+        if step == "cores":
+            self.moving = swap(self.parts[1], "dp", 1), swap(self.parts[3], "dp", 1)
+        elif step == "mp":
+            self.moving = swap(self.state[1], "mp", 1)
+        elif step == "finish":
+            self.moving = swap(self.state, "dp", 1)
+        elif step[0] == "halve":
+            bit = (lax.axis_index("dp") // step[1]) % 2
+            self.moving = swap(half_of(self.state, 1 - bit), "dp", step[1])
+        else:
+            self.moving = swap(self.state, "dp", step[1])
+
+    def collect(self):
+        step = self.plan.pop(0)
+        if step == "cores":
+            own_a, own_b, far_a, far_b = self.parts
+            self.state = jnp.stack([add_up(own_a, self.moving[0]), add_up(far_a, self.moving[1])])
+        elif step == "mp":
+            self.state = add_up(self.state[0], self.moving)
+        elif step == "finish":
+            self.other = self.moving
+        elif step[0] == "halve":
+            bit = (lax.axis_index("dp") // step[1]) % 2
+            self.state = add_up(half_of(self.state, bit), self.moving)
+        else:
+            bit = (lax.axis_index("dp") // step[1]) % 2
+            self.state = halves_in_order(self.state, self.moving, bit)
+
+
+def tied(*values):
+    return lax.optimization_barrier(values)
+
+
+def turn(value, *sums):
+    for each in sums:
+        each.collect()
+    kept = tied(value, *[each.state for each in sums])
+    for each, state in zip(sums, kept[1:]):
+        each.state = state
+        if each.plan:
+            each.issue()
+    return kept[0]
+
+
+class Small(Sum):
+    def __init__(self, state, plan):
+        self.state, self.plan = state, list(plan)
+
+    def issue(self):
+        self.moving = swap(self.state, *self.plan[0])
+
+    def collect(self):
+        self.plan.pop(0)
+        self.state = self.state + self.moving
+
+
+def whole_sequence(
+    hidden_in,
+    out_grad,
+    ln1_gain,
+    ln1_bias,
+    w_query,
+    w_key,
+    w_value,
+    w_out,
+    ln2_gain,
+    ln2_bias,
+    w_up,
+    b_up,
+    w_down,
+    b_down,
+    rand_blocks,
+):
+    device = lax.axis_index("dp")
+    core, over_y, side = device % 2, (device // 2) % 2, lax.axis_index("mp")
+    zero = 0 * core
+    place = jnp.stack([core, 1 - core, zero, zero, over_y]).astype(jnp.int32)
+
+    def part(array, axis, index, count):
+        size = array.shape[axis] // count
+        return lax.dynamic_slice_in_dim(array, index * size, size, axis)
+
+    def joined(other):
+        return jnp.concatenate(
+            [part(each, 1, core ^ other, 2) for each in (w_query, w_key, w_value)], axis=1
+        )
+
+    def row(vector):
+        return vector.reshape(1, -1)
+
+    own_ja, own_jb = joined(0), joined(1)
+    quarter = 2 * core + over_y
+    out_piece, up_piece = part(w_out, 0, core, 2), part(w_up, 1, quarter, 4)
+    down_piece = part(w_down, 0, quarter, 4)
+    far_ja = swap(own_ja, "mp", 1)
+    far_rand, far_bup = swap(rand_blocks, "mp", 1), swap(b_up, "mp", 1)
+    own_bias, far_bias = block_bias(rand_blocks), block_bias(far_rand)
+    bias = [own_bias, own_bias, far_bias, far_bias]
+    normed_one, normed_one_t, out_grad_t, bias_down = norm_in(
+        place, hidden_in, out_grad, row(ln1_gain), row(ln1_bias)
+    )
+    qkv, context, row_lse = [None] * 4, [None] * 4, [None] * 4
+
+    def attend(g, normed, weights):
+        qkv[g] = mm(normed, weights).astype(BF16)
+        context[g], row_lse[g] = attend_forward(place, g, qkv[g], bias[g])
+
+    attend(0, normed_one, own_ja)
+    attend(1, tied(normed_one, context[0])[0], own_jb)
+    normed, far_ja, out_piece, _ = tied(normed_one, far_ja, out_piece, context[1])
+    far_jb, far_out_a = swap(far_ja, "dp", 1), swap(out_piece, "mp", 1)
+    attend(2, normed, far_ja)
+    normed, far_jb, far_out_a, up_piece, _ = tied(
+        normed_one, far_jb, far_out_a, up_piece, context[2]
+    )
+    far_out_b, up_mine = swap(far_out_a, "dp", 1), swap(up_piece, "mp", 1)
+    attend(3, normed, far_jb)
+    context[3], far_out_b = tied(context[3], far_out_b)
+    joined_w = [own_ja, own_jb, far_ja, far_jb]
+    out_w = [w_out, w_out, far_out_a, far_out_b]
+    middle, normed_two, normed_two_t = project_out(
+        place, hidden_in, context, out_w, row(ln2_gain), row(ln2_bias)
+    )
+
+    hidden, grad_up, bias_up, down_g, up_g = ([None] * 4 for _ in range(5))
+    up_bias = [row(b_up), row(b_up), row(far_bup), row(far_bup)]
+
+    def feed(g, normed, up, down):
+        hidden[g], grad_up[g], bias_up[g] = feed_forward(
+            place, g, normed, out_grad, up, up_bias[g], down
+        )
+
+    def down_grad(g, left):
+        down_g[g] = mm(left, hidden[g]).astype(BF16)
+
+    def up_grad(g, left):
+        up_g[g] = mm(left, grad_up[g]).astype(BF16)
+
+    normed, up_mine, down_piece = tied(normed_two, up_mine, down_piece)
+    up_other, down_mine = swap(up_mine, "dp", 2), swap(down_piece, "mp", 1)
+    feed(0, normed, (w_up,), (w_down,))
+    feed(1, tied(normed, grad_up[0])[0], (w_up,), (w_down,))
+    left_down, left_up, up_mine, up_other, down_mine, _ = tied(
+        out_grad_t, normed_two_t, up_mine, up_other, down_mine, grad_up[1]
+    )
+    up_far = [swap(up_mine, "dp", 1), swap(up_other, "dp", 1)]
+    down_other = swap(down_mine, "dp", 2)
+    for g in (1, 0):
+        down_grad(g, left_down)
+        up_grad(g, left_up)
+    normed, down_mine, down_other, *_ = tied(
+        normed_two, down_mine, down_other, *up_far, *down_g[:2], *up_g[:2]
+    )
+    down_far = [swap(down_mine, "dp", 1), swap(down_other, "dp", 1)]
+    up_w = [(w_up,), (w_up,), (up_mine, up_other), tuple(up_far)]
+    down_w = [(w_down,), (w_down,), (down_mine, down_other), tuple(down_far)]
+    feed(2, normed, up_w[2], down_w[2])
+    normed, down_fa, down_fb, _ = tied(normed_two, *down_far, grad_up[2])
+    down_w[3] = (down_fa, down_fb)
+    feed(3, normed, up_w[3], down_w[3])
+    left_down, _ = tied(out_grad_t, grad_up[3])
+    down_grad(3, left_down)
+    down_grad(2, left_down)
+    down_sum = Sum(["mp", 2, 4, 8])
+    up_sum = Sum([4, "mp", 2, 8])
+    first_sum = Sum(["mp", 2, 4, 8])
+    second_sum = Sum(["mp", 4, 2, 8])
+    *down_g, left_up = tied(*down_g, normed_two_t)
+    down_sum.feed(*down_g)
+    down_sum.issue()
+    up_grad(3, left_up)
+    up_grad(2, left_up)
+    *up_g, grads_in = tied(*up_g, out_grad)
+    up_sum.feed(*up_g)
+    up_sum.issue()
+
+    grads_in = turn(grads_in, down_sum)
+    grad_middle, grad_attn, grad_attn_t, gain_two, bias_two = middle_back(
+        place, grads_in, middle, row(ln2_gain), grad_up, up_w
+    )
+    grad_attn = turn(grad_attn, up_sum)
+    out_g = [mm(grad_attn_t, context[g]).astype(BF16) for g in range(4)]
+    out_w[0], out_w[1] = out_piece, part(w_out, 0, 1 - core, 2)
+    grad_context = [mm(grad_attn, out_w[g], NT).astype(BF16) for g in range(4)]
+    grads, joined_g = [None] * 8, [None] * 8
+
+    def attend_back(g, pair, grad_in):
+        grads[2 * g + pair] = attend_backward(
+            place, g, pair, qkv[g], grad_in, context[g], row_lse[g], bias[g]
+        )
+
+    def joined_grads(pair, groups, left):
+        for g in groups:
+            joined_g[2 * g + pair] = mm(left, grads[2 * g + pair]).astype(BF16)
+
+    grad_in, *_ = tied(grad_context[3], *grad_context[:3], *out_g)
+    attend_back(3, 0, grad_in)
+    attend_back(2, 0, tied(grad_context[2], grads[6])[0])
+    grad_in = turn(tied(grad_context[1], grads[4])[0], down_sum)
+    attend_back(1, 0, grad_in)
+    attend_back(0, 0, tied(grad_context[0], grads[2])[0])
+    joined_grads(0, (3, 2, 1, 0), tied(normed_one_t, grads[0])[0])
+    first_sum.feed(
+        *[jnp.concatenate([joined_g[2 * g], out_g[g]], axis=1) for g in range(4)]
+    )
+    first_sum.parts = tied(*first_sum.parts)
+    first_sum.issue()
+    grad_in = turn(tied(grad_context[3], *first_sum.parts)[0], up_sum, down_sum)
+    attend_back(3, 1, grad_in)
+    attend_back(2, 1, tied(grad_context[2], grads[7])[0])
+    grad_in = turn(tied(grad_context[1], grads[5])[0], down_sum, first_sum)
+    attend_back(1, 1, grad_in)
+    grad_in = turn(tied(grad_context[0], grads[3])[0], up_sum, down_sum)
+    attend_back(0, 1, grad_in)
+    joined_grads(1, (3, 2, 1, 0), tied(normed_one_t, grads[1])[0])
+    *parts, grad_in = tied(*joined_g[1::2], grad_middle)
+    second_sum.feed(*parts)
+    second_sum.issue()
+    grad_in = turn(grad_in, up_sum, down_sum)
+    input_grad, gain_one, bias_one = input_back(
+        place, hidden_in, grad_in, row(ln1_gain), grads, joined_w
+    )
+    own_up = halves_in_order(bias_up[0], bias_up[1], core, 1)
+    far_up = halves_in_order(bias_up[2], bias_up[3], core, 1)
+    width = hidden_in.shape[1]
+    small = Small(
+        jnp.concatenate(
+            [gain_one, bias_one, gain_two, bias_two, bias_down]
+            + [halves_in_order(own_up, far_up, side, 1).reshape(-1, width)]
+        ),
+        [("dp", 1), ("mp", 1), ("dp", 2), ("dp", 4), ("dp", 8)],
+    )
+    total, small.state, _ = tied(middle, small.state, input_grad)
+    small.issue()
+    total = turn(total, first_sum, second_sum, up_sum, down_sum)
+    output = project_down(place, total, row(b_down), hidden, down_w)
+    output = turn(output, small, second_sum, first_sum, up_sum, down_sum)
+    while second_sum.plan:
+        for each in (second_sum, small, first_sum, up_sum, down_sum):
+            if each.plan:
+                each.collect()
+                if each.plan:
+                    each.issue()
+
+    def in_order(total, first, last):
+        return halves_in_order(
+            total.state[:, first:last], total.other[:, first:last], core, 1
+        ).astype(F32)
+
+    def both_pairs(part_index):
+        columns = slice(part_index * PAIR, (part_index + 1) * PAIR)
+        mine = [each.state[:, columns] for each in (first_sum, second_sum)]
+        other = [each.other[:, columns] for each in (first_sum, second_sum)]
+        ordered = halves_in_order(
+            jnp.concatenate(mine, axis=1), jnp.concatenate(other, axis=1), core, 1
+        )
+        return ordered.astype(F32)
+
+    units = down_g[0].shape[1]
+    sums = small.state
+    up_rows = b_up.shape[0] // width
+    bias_up_sum = lax.dynamic_slice_in_dim(sums, 5 + side * up_rows, up_rows).reshape(-1)
+    return (
+        output,
+        input_grad,
+        sums[0],
+        sums[1],
+        both_pairs(0),
+        both_pairs(1),
+        both_pairs(2),
+        in_order(first_sum, 3 * PAIR, 5 * PAIR).T,
+        sums[2],
+        sums[3],
+        in_order(up_sum, 0, units),
+        bias_up_sum,
+        in_order(down_sum, 0, units).T,
+        sums[4],
+    )
+
+
 def solution(mesh):
     in_specs = (
         P(("dp", "mp"), None),
@@ -245,6 +1014,14 @@
         P("mp", None),
         P(),
     )
+    def per_device(hidden_in, *others):
+        w_query, w_up, rand_blocks = others[3], others[9], others[13]
+        whole = hidden_in.shape[0] == SEQ and mesh.shape["mp"] == 2
+        halved = mesh.shape["dp"] == 16 and rand_blocks.shape[0] == 8
+        sized = w_query.shape == (1024, 512) and w_up.shape == (1024, 2048)
+        layer = whole_sequence if whole and halved and sized else split_sequence
+        return layer(hidden_in, *others)
+
     return jax.shard_map(
         per_device, mesh=mesh, in_specs=in_specs, out_specs=out_specs, check_vma=False
     )

time: 1250 us -> 630 us (0.50)
  waiting for transfers between devices: 550 us -> 116 us
  matrix products: 335 us -> 76.3 us
  Pallas kernels: 0 us -> 246 us
  other arithmetic: 172 us -> 76.2 us
  blocking collectives: 75.1 us -> 0 us
  starting transfers between devices: 0.37 us -> 49 us
  local copies, waits for them, and re-layouts: 93.5 us -> 54.2 us
    dot_general x26 -> x28, matrix products: 335 us -> 76.3 us  [mm(): return lax.dot_general(left, right, dims, preferred_element_type=F32)]
    pallas_call x0 -> x21, Pallas kernels: none -> 246 us  [the longest x8 71.7 us: attend_backward(): call(attend_backward_kernel, grid=(1,), in_specs=[thin_block(lambda p: pa...]
    reduce_scatter x4 -> x0, waiting for transfers between devices: 187 us -> none  [the longest x1 54.4 us: per_device(): lax.psum_scatter(jnp.dot(context_rows, w_out, preferred_element_type=jnp....]
    psum x1 -> x0, waiting for transfers between devices: 187 us -> none  [per_device(): lax.psum(grad_joined_weight.astype(jnp.bfloat16), 'dp').astype(jnp.float32)]
    all_gather x4 -> x0, waiting for transfers between devices: 176 us -> none  [the longest x1 56.3 us: per_device(): rows_two = lax.all_gather(normed_two, 'mp', axis=0, tiled=True)]
    ppermute x0 -> x59, waiting for transfers between devices: none -> 116 us  [swap(): lax.ppermute(array, axis, [(place, place ^ bit) for place in range(size)])]
    convert_element_type x11 -> x20, other arithmetic: 110 us -> 26.3 us  [the longest x16 17.2 us: add_up(): return total.astype(terms[0].dtype)]
    psum x2 -> x0, blocking collectives: 75.1 us -> none  [the longest x1 39.8 us: per_device(): lax.psum((gain_one, bias_one, gain_two, bias_two, bias_down), ('dp', 'mp'))]
  transfers between devices with their start and end apart: 9 -> 59, of which waited for: 9 -> 18; matrix products, arithmetic and copies ran while one was open for 8% -> 24% of each run, Pallas kernels for 0% -> 36%
where the time goes in v2:
time: 630 us; the launch traced here: 620 us
  Pallas kernels  246 us (39%)
  waiting for transfers between devices  116 us (18%)
  matrix products  76.3 us (12%)
  other arithmetic  76.2 us (12%)
  local copies, waits for them, and re-layouts  54.2 us (9%)
  starting transfers between devices  49 us (8%)
    ppermute x59, waiting for transfers between devices, swap(): lax.ppermute(array, axis, [(place, place ^ bit) for place in range(size)])  116 us
    dot_general x28, matrix products, mm(): return lax.dot_general(left, right, dims, preferred_element_type=F32)  76.3 us
    pallas_call x8, Pallas kernels, attend_backward(): call(attend_backward_kernel, grid=(1,), in_specs=[thin_block(lambda p: pa...  71.7 us
    pallas_call x4, Pallas kernels, attend_forward(): call(attend_forward_kernel, grid=(pairs,), in_specs=[thin_block(lambda p:...  56.2 us
    pallas_call x4, Pallas kernels, feed_forward(): call(lambda *refs: feed_forward_kernel(tiles, *refs), grid=(tiles,), in_s...  52 us
    ppermute x59, starting transfers between devices, swap(): lax.ppermute(array, axis, [(place, place ^ bit) for place in range(size)])  49 us
    unnamed x201, local copies, waits for them, and re-layouts  27.1 us
    pallas_call x1, Pallas kernels, middle_back(): call(middle_back_kernel, grid=(rows // TILE,), in_specs=[row_tile(width),...  19.4 us
  transfers between devices with their start and end apart: 59, of which 18 were waited for; matrix products, arithmetic and copies ran while one was open for 24% of the time, Pallas kernels for 36%

profile of v2, /device:TPU:0, one launch (start us, length us, event | category | flops | bytes accessed | tf_op | source)
XLA Modules:
  0.0 620.2 jit_solution(1608364143099842241)
XLA Ops:
  10.0 7.2 %norm_in.1 = (bf16[1024,1024]{1,0:T(8,128)(2,1)}, bf16[1024,1024]{1,0:T(8,128)(2,1)}, bf16[1024,1024]{1,0:T(8,128)(2,1)}, f32[1,1024]{1,0:T(1,128)}) custom-call(s32[5]{0:T(128)} %pad_add_fusion.s.refs_0_, bf16[1024,1024]{1,0:T(8,128)(2,1)} %x_ref.5, bf16[1024,1024]{1,0:T(8,128)(2,1)} %g_ref.2, f32[1,1024]{1,0:T(1,128)} %bitcast.123, f32[1,1024]{1,0:T(1,128)} %bitcast.133), custom_call_target="tpu_custom_call" | custom-call | flops 100000000 | tf_op jit(solution)/shard_map/norm_in/pallas_call | solution.py:311
  17.3 4.6 convolution_convert_fusion.11.q_ref.k_ref.v_ref
  23.4 14.0 %attend_forward.4 = (bf16[1024,256]{1,0:T(8,128)(2,1)}, f32[2,2,1024]{2,1,0:T(2,128)}) custom-call(s32[5]{0:T(128)} %pad_add_fusion.s.refs_0_, bf16[1024,768]{1,0:T(8,128)(2,1)} %convolution_convert_fusion.11.q_ref.k_ref.v_ref, bf16[1024,768]{1,0:T(8,128)(2,1)} %convolution_convert_fusion.11.q_ref.k_ref.v_ref, ...), custom_call_target="tpu_custom_call" | custom-call | flops 240000000 | tf_op jit(solution)/shard_map/attend_forward/pallas_call | solution.py:360
  40.4 14.0 %attend_forward.5 = (bf16[1024,256]{1,0:T(8,128)(2,1)}, f32[2,2,1024]{2,1,0:T(2,128)}) custom-call(s32[5]{0:T(128)} %pad_add_fusion.s.refs_0_, bf16[1024,768]{1,0:T(8,128)(2,1)} %convolution_convert_fusion.10.q_ref.k_ref.v_ref, bf16[1024,768]{1,0:T(8,128)(2,1)} %convolution_convert_fusion.10.q_ref.k_ref.v_ref, ...), custom_call_target="tpu_custom_call" | custom-call | flops 240000000 | tf_op jit(solution)/shard_map/attend_forward/pallas_call | solution.py:360
  59.6 5.0 convolution_convert_fusion.9.q_ref.k_ref.v_ref
  64.5 14.4 %attend_forward.6 = (bf16[1024,256]{1,0:T(8,128)(2,1)}, f32[2,2,1024]{2,1,0:T(2,128)}) custom-call(s32[5]{0:T(128)} %pad_add_fusion.s.refs_0_, bf16[1024,768]{1,0:T(8,128)(2,1)} %convolution_convert_fusion.9.q_ref.k_ref.v_ref, bf16[1024,768]{1,0:T(8,128)(2,1)} %convolution_convert_fusion.9.q_ref.k_ref.v_ref, ...), custom_call_target="tpu_custom_call" | custom-call | flops 240000000 | tf_op jit(solution)/shard_map/attend_forward/pallas_call | solution.py:360
  84.6 13.8 %attend_forward.7 = (bf16[1024,256]{1,0:T(8,128)(2,1)}, f32[2,2,1024]{2,1,0:T(2,128)}) custom-call(s32[5]{0:T(128)} %pad_add_fusion.s.refs_0_, bf16[1024,768]{1,0:T(8,128)(2,1)} %convolution_convert_fusion.8.q_ref.k_ref.v_ref, bf16[1024,768]{1,0:T(8,128)(2,1)} %convolution_convert_fusion.8.q_ref.k_ref.v_ref, ...), custom_call_target="tpu_custom_call" | custom-call | flops 240000000 | tf_op jit(solution)/shard_map/attend_forward/pallas_call | solution.py:360
  99.1 8.6 %project_out.1 = (f32[1024,1024]{1,0:T(8,128)}, bf16[1024,1024]{1,0:T(8,128)(2,1)}, bf16[1024,1024]{1,0:T(8,128)(2,1)}) custom-call(s32[5]{0:T(128)} %pad_add_fusion.s.refs_0_, bf16[1024,1024]{1,0:T(8,128)(2,1)} %x_ref.5, bf16[1024,256]{1,0:T(8,128)(2,1)} %get-tuple-element.136.refs_0_.context_ref, bf16[1024,256]{1,0:T(8,128)(2,1)} %get-tuple-element.138.refs_1_.context_ref, ...), custom_call_target="tpu_custom_call" | custom-call | flops 140000000 | tf_op jit(solution)/shard_map/project_out/pallas_call | solution.py:461
  110.1 12.5 %feed_forward.4 = (bf16[1024,1024]{1,0:T(8,128)(2,1)}, bf16[1024,1024]{1,0:T(8,128)(2,1)}, f32[1,1024]{1,0:T(1,128)}) custom-call(s32[5]{0:T(128)} %pad_add_fusion.s.refs_0_, bf16[1024,1024]{1,0:T(8,128)(2,1)} %get-tuple-element.172.refs_1_, bf16[1024,1024]{1,0:T(8,128)(2,1)} %g_ref.2, f32[1,2048]{1,0:T(1,128)} %bitcast.119, bf16[1024,2048]{1,0:T(8,128)(2,1)} %refs_7_.2, ...), custom_call_target="tpu_custom_call" | custom-call | flops 240000000 | tf_op jit(solution)/shard_map/feed_forward/pallas_call | solution.py:521
  122.6 12.7 %feed_forward.5 = (bf16[1024,1024]{1,0:T(8,128)(2,1)}, bf16[1024,1024]{1,0:T(8,128)(2,1)}, f32[1,1024]{1,0:T(1,128)}) custom-call(s32[5]{0:T(128)} %pad_add_fusion.s.refs_0_, bf16[1024,1024]{1,0:T(8,128)(2,1)} %get-tuple-element.172.refs_1_, bf16[1024,1024]{1,0:T(8,128)(2,1)} %g_ref.2, f32[1,2048]{1,0:T(1,128)} %bitcast.120, bf16[1024,2048]{1,0:T(8,128)(2,1)} %refs_7_.2, ...), custom_call_target="tpu_custom_call" | custom-call | flops 240000000 | tf_op jit(solution)/shard_map/feed_forward/pallas_call | solution.py:521
  135.4 6.6 %convolution_convert_fusion.6 = bf16[1024,1024]{1,0:T(8,128)(2,1)} fusion(bf16[1024,1024]{1,0:T(8,128)(2,1)} %get-tuple-element.179, bf16[1024,1024]{1,0:T(8,128)(2,1)} %get-tuple-element.160.refs_1_), kind=kOutput, calls=%fused_computation.35 | convolution fusion | flops 2148532224 | bytes 6291456 | tf_op jit(solution)/shard_map/dot_general | solution.py:227
  142.0 3.7 convolution_convert_fusion.7
  146.5 3.7 convolution_convert_fusion.4
  152.5 18.8 %collective-permute-done.8.refs_7_.refs_9_ = bf16[512,1024]{1,0:T(8,128)(2,1)S(1)} collective-permute-done((bf16[512,1024]{1,0:T(8,128)(2,1)S(1)}, bf16[512,1024]{1,0:T(8,128)(2,1)S(1)}, u32[]{:S(2)}, u32[]{:S(2)}) %collective-permute-start.8) | collective-permute-done | bytes 1048608 | tf_op jit(solution)/shard_map/ppermute | solution.py:667
  176.2 13.2 %feed_forward.6 = (bf16[1024,1024]{1,0:T(8,128)(2,1)}, bf16[1024,1024]{1,0:T(8,128)(2,1)}, f32[1,1024]{1,0:T(1,128)}) custom-call(s32[5]{0:T(128)} %pad_add_fusion.s.refs_0_, bf16[1024,1024]{1,0:T(8,128)(2,1)} %get-tuple-element.172.refs_1_, bf16[1024,1024]{1,0:T(8,128)(2,1)} %g_ref.2, f32[1,2048]{1,0:T(1,128)} %bitcast.117, bf16[1024,512]{1,0:T(8,128)(2,1)} %copy-done.24, ...), custom_call_target="tpu_custom_call" | custom-call | flops 240000000 | tf_op jit(solution)/shard_map/feed_forward/pallas_call | solution.py:521
  190.7 13.6 %feed_forward.7 = (bf16[1024,1024]{1,0:T(8,128)(2,1)}, bf16[1024,1024]{1,0:T(8,128)(2,1)}, f32[1,1024]{1,0:T(1,128)}) custom-call(s32[5]{0:T(128)} %pad_add_fusion.s.refs_0_, bf16[1024,1024]{1,0:T(8,128)(2,1)} %get-tuple-element.172.refs_1_, bf16[1024,1024]{1,0:T(8,128)(2,1)} %g_ref.2, f32[1,2048]{1,0:T(1,128)} %bitcast.118, ...), custom_call_target="tpu_custom_call" | custom-call | flops 240000000 | tf_op jit(solution)/shard_map/feed_forward/pallas_call | solution.py:521
  204.4 6.0 convolution_convert_fusion.2
  210.4 3.7 convolution_convert_fusion.3
  214.6 3.7 convolution_convert_fusion
  218.3 3.7 convolution_convert_fusion.1
  231.4 19.4 %middle_back.1 = (f32[1024,1024]{1,0:T(8,128)}, bf16[1024,1024]{1,0:T(8,128)(2,1)}, bf16[1024,1024]{1,0:T(8,128)(2,1)}, f32[1,1024]{1,0:T(1,128)}, f32[1,1024]{1,0:T(1,128)}) custom-call(s32[5]{0:T(128)} %pad_add_fusion.s.refs_0_, bf16[1024,1024]{1,0:T(8,128)(2,1)} %g_ref.2, f32[1024,1024]{1,0:T(8,128)} %get-tuple-element.244.middle_ref, ...), custom_call_target="tpu_custom_call" | custom-call | flops 360000000 | tf_op jit(solution)/shard_map/middle_back/pallas_call | solution.py:577
  273.0 9.1 %attend_backward.8.refs_6_ = bf16[1024,384]{1,0:T(8,128)(2,1)} custom-call(s32[5]{0:T(128)} %pad_add_fusion.s.refs_0_, bf16[1024,768]{1,0:T(8,128)(2,1)} %convolution_convert_fusion.8.q_ref.k_ref.v_ref, bf16[1024,768]{1,0:T(8,128)(2,1)} %convolution_convert_fusion.8.q_ref.k_ref.v_ref, bf16[1024,768]{1,0:T(8,128)(2,1)} %convolution_convert_fusion.8.q_ref.k_ref.v_ref, ...), custom_call_target="tpu_custom_call" | custom-call | flops 160000000 | tf_op jit(solution)/shard_map/attend_backward/pallas_call | solution.py:416
  282.1 8.9 %attend_backward.9.refs_4_ = bf16[1024,384]{1,0:T(8,128)(2,1)} custom-call(s32[5]{0:T(128)} %pad_add_fusion.s.refs_0_, bf16[1024,768]{1,0:T(8,128)(2,1)} %convolution_convert_fusion.9.q_ref.k_ref.v_ref, bf16[1024,768]{1,0:T(8,128)(2,1)} %convolution_convert_fusion.9.q_ref.k_ref.v_ref, bf16[1024,768]{1,0:T(8,128)(2,1)} %convolution_convert_fusion.9.q_ref.k_ref.v_ref, ...), custom_call_target="tpu_custom_call" | custom-call | flops 160000000 | tf_op jit(solution)/shard_map/attend_backward/pallas_call | solution.py:416
  296.6 9.2 %attend_backward.10.refs_2_ = bf16[1024,384]{1,0:T(8,128)(2,1)} custom-call(s32[5]{0:T(128)} %pad_add_fusion.s.refs_0_, bf16[1024,768]{1,0:T(8,128)(2,1)} %convolution_convert_fusion.10.q_ref.k_ref.v_ref, bf16[1024,768]{1,0:T(8,128)(2,1)} %convolution_convert_fusion.10.q_ref.k_ref.v_ref, bf16[1024,768]{1,0:T(8,128)(2,1)} %convolution_convert_fusion.10.q_ref.k_ref.v_ref, ...), custom_call_target="tpu_custom_call" | custom-call | flops 160000000 | tf_op jit(solution)/shard_map/attend_backward/pallas_call | solution.py:416
  305.8 9.0 %attend_backward.11.refs_0_ = bf16[1024,384]{1,0:T(8,128)(2,1)} custom-call(s32[5]{0:T(128)} %pad_add_fusion.s.refs_0_, bf16[1024,768]{1,0:T(8,128)(2,1)} %convolution_convert_fusion.11.q_ref.k_ref.v_ref, bf16[1024,768]{1,0:T(8,128)(2,1)} %convolution_convert_fusion.11.q_ref.k_ref.v_ref, bf16[1024,768]{1,0:T(8,128)(2,1)} %convolution_convert_fusion.11.q_ref.k_ref.v_ref, ...), custom_call_target="tpu_custom_call" | custom-call | flops 160000000 | tf_op jit(solution)/shard_map/attend_backward/pallas_call | solution.py:416
  328.8 11.3 %collective-permute-done.19 = bf16[2,512,1024]{2,1,0:T(8,128)(2,1)} collective-permute-done((bf16[2,512,1024]{2,1,0:T(8,128)(2,1)}, bf16[2,512,1024]{2,1,0:T(8,128)(2,1)}, u32[]{:S(2)}, u32[]{:S(2)}) %collective-permute-start.19) | collective-permute-done | bytes 2097184 | tf_op jit(solution)/shard_map/ppermute | solution.py:667
  348.3 8.8 %attend_backward.12.refs_7_ = bf16[1024,384]{1,0:T(8,128)(2,1)} custom-call(s32[5]{0:T(128)} %pad_add_fusion.s.refs_0_, bf16[1024,768]{1,0:T(8,128)(2,1)} %convolution_convert_fusion.8.q_ref.k_ref.v_ref, bf16[1024,768]{1,0:T(8,128)(2,1)} %convolution_convert_fusion.8.q_ref.k_ref.v_ref, bf16[1024,768]{1,0:T(8,128)(2,1)} %convolution_convert_fusion.8.q_ref.k_ref.v_ref, ...), custom_call_target="tpu_custom_call" | custom-call | flops 160000000 | tf_op jit(solution)/shard_map/attend_backward/pallas_call | solution.py:416
  357.1 8.9 %attend_backward.13.refs_5_ = bf16[1024,384]{1,0:T(8,128)(2,1)} custom-call(s32[5]{0:T(128)} %pad_add_fusion.s.refs_0_, bf16[1024,768]{1,0:T(8,128)(2,1)} %convolution_convert_fusion.9.q_ref.k_ref.v_ref, bf16[1024,768]{1,0:T(8,128)(2,1)} %convolution_convert_fusion.9.q_ref.k_ref.v_ref, bf16[1024,768]{1,0:T(8,128)(2,1)} %convolution_convert_fusion.9.q_ref.k_ref.v_ref, ...), custom_call_target="tpu_custom_call" | custom-call | flops 160000000 | tf_op jit(solution)/shard_map/attend_backward/pallas_call | solution.py:416
  375.9 8.9 %attend_backward.14.refs_3_ = bf16[1024,384]{1,0:T(8,128)(2,1)} custom-call(s32[5]{0:T(128)} %pad_add_fusion.s.refs_0_, bf16[1024,768]{1,0:T(8,128)(2,1)} %convolution_convert_fusion.10.q_ref.k_ref.v_ref, bf16[1024,768]{1,0:T(8,128)(2,1)} %convolution_convert_fusion.10.q_ref.k_ref.v_ref, bf16[1024,768]{1,0:T(8,128)(2,1)} %convolution_convert_fusion.10.q_ref.k_ref.v_ref, ...), custom_call_target="tpu_custom_call" | custom-call | flops 160000000 | tf_op jit(solution)/shard_map/attend_backward/pallas_call | solution.py:416
  387.4 3.6 collective-permute-done.24
  392.6 8.9 %attend_backward.15.refs_1_ = bf16[1024,384]{1,0:T(8,128)(2,1)} custom-call(s32[5]{0:T(128)} %pad_add_fusion.s.refs_0_, bf16[1024,768]{1,0:T(8,128)(2,1)} %convolution_convert_fusion.11.q_ref.k_ref.v_ref, bf16[1024,768]{1,0:T(8,128)(2,1)} %convolution_convert_fusion.11.q_ref.k_ref.v_ref, bf16[1024,768]{1,0:T(8,128)(2,1)} %convolution_convert_fusion.11.q_ref.k_ref.v_ref, ...), custom_call_target="tpu_custom_call" | custom-call | flops 160000000 | tf_op jit(solution)/shard_map/attend_backward/pallas_call | solution.py:416
  401.6 4.1 convolution_convert_fusion.12
  416.9 7.2 %collective-permute-done.27 = bf16[128,1024]{1,0:T(8,128)(2,1)S(1)} collective-permute-done((bf16[128,1024]{1,0:T(8,128)(2,1)S(1)}, bf16[128,1024]{1,0:T(8,128)(2,1)S(1)}, u32[]{:S(2)}, u32[]{:S(2)}) %collective-permute-start.27) | collective-permute-done | bytes 262176 | tf_op jit(solution)/shard_map/ppermute | solution.py:667
  427.8 14.9 %input_back.1 = (f32[1024,1024]{1,0:T(8,128)}, f32[1,1024]{1,0:T(1,128)}, f32[1,1024]{1,0:T(1,128)}) custom-call(s32[5]{0:T(128)} %pad_add_fusion.s.refs_0_, bf16[1024,1024]{1,0:T(8,128)(2,1)} %x_ref.5, f32[1024,1024]{1,0:T(8,128)} %get-tuple-element.225.gm_ref, f32[1,1024]{1,0:T(1,128)} %bitcast.124, bf16[1024,384]{1,0:T(8,128)(2,1)} %attend_backward.11.refs_0_, ...), custom_call_target="tpu_custom_call" | custom-call | flops 300000000 | tf_op jit(solution)/shard_map/input_back/pallas_call | solution.py:614
  458.1 16.1 %project_down.1 = bf16[1024,1024]{1,0:T(8,128)(2,1)} custom-call(s32[5]{0:T(128)} %pad_add_fusion.s.refs_0_, f32[1024,1024]{1,0:T(8,128)} %get-tuple-element.244.middle_ref, f32[1,1024]{1,0:T(1,128)} %bitcast.127, bf16[1024,1024]{1,0:T(8,128)(2,1)} %get-tuple-element.163.refs_0_, bf16[1024,1024]{1,0:T(8,128)(2,1)} %get-tuple-element.164.refs_1_, ...), custom_call_target="tpu_custom_call" | custom-call | flops 300000000 | tf_op jit(solution)/shard_map/project_down/pallas_call | solution.py:638
  476.1 15.6 %collective-permute-done.37 = bf16[512,1024]{1,0:T(8,128)(2,1)} collective-permute-done((bf16[512,1024]{1,0:T(8,128)(2,1)S(1)}, bf16[512,1024]{1,0:T(8,128)(2,1)}, u32[]{:S(2)}, u32[]{:S(2)}) %collective-permute-start.37) | collective-permute-done | bytes 1048608 | tf_op jit(solution)/shard_map/ppermute | solution.py:667
  498.0 8.7 %collective-permute-done.42 = bf16[256,640]{0,1:T(8,128)(2,1)S(1)} collective-permute-done((bf16[256,640]{0,1:T(8,128)(2,1)S(1)}, bf16[256,640]{0,1:T(8,128)(2,1)S(1)}, u32[]{:S(2)}, u32[]{:S(2)}) %collective-permute-start.42) | collective-permute-done | bytes 327712 | tf_op jit(solution)/shard_map/ppermute | solution.py:667
  506.9 5.0 collective-permute-done.47
  513.7 5.4 collective-permute-done.43
  522.3 6.8 %collective-permute-done.44 = bf16[128,640]{0,1:T(8,128)(2,1)S(1)} collective-permute-done((bf16[128,640]{0,1:T(8,128)(2,1)S(1)}, bf16[128,640]{0,1:T(8,128)(2,1)S(1)}, u32[]{:S(2)}, u32[]{:S(2)}) %collective-permute-start.44) | collective-permute-done | bytes 163872 | tf_op jit(solution)/shard_map/ppermute | solution.py:667
  534.2 5.4 collective-permute-done.50
  542.1 3.5 collective-permute-done.38
  552.2 10.5 %collective-permute-done.40 = f32[9,1024]{1,0:T(8,128)S(1)} collective-permute-done((f32[9,1024]{1,0:T(8,128)S(1)}, f32[9,1024]{1,0:T(8,128)S(1)}, u32[]{:S(2)}, u32[]{:S(2)}) %collective-permute-start.40) | collective-permute-done | bytes 36896 | tf_op jit(solution)/shard_map/ppermute | solution.py:667
  563.4 5.9 collective-permute-done.41
  575.3 4.6 maximum_select_fusion.3
  583.7 6.3 %convert_bitcast_fusion = f32[2048,1024]{0,1:T(8,128)} fusion(bf16[1024,1024]{1,0:T(8,128)(2,1)} %collective-permute-done.58, bf16[1024,1024]{1,0:T(8,128)(2,1)S(1)} %maximum_select_fusion.2, pred[]{:T(512)S(6)} %eq.142), kind=kLoop, calls=%fused_computation | loop fusion | flops 20971520 | bytes 12582913 | tf_op jit(solution)/shard_map/transpose | solution.py:978
  590.1 9.2 %copy.48 = f32[2048,1024]{1,0:T(8,128)} copy(f32[2048,1024]{0,1:T(8,128)} %convert_bitcast_fusion) | data formatting | bytes 16777216
  612.2 7.8 %fusion = f32[1024,2048]{1,0:T(8,128)} fusion(bf16[1024,1024]{1,0:T(8,128)(2,1)} %collective-permute-done.57, bf16[1024,1024]{1,0:T(8,128)(2,1)} %maximum_select_fusion.3, pred[]{:T(512)S(6)} %eq.142), kind=kLoop, calls=%fused_computation.4 | loop fusion | flops 20971520 | bytes 12582913 | tf_op jit(solution)/shard_map/convert_element_type | solution.py:950
  (422 shorter events, 191.2 us)
Async XLA Ops:
  0.7 21.2 %collective-permute-start.1 = (s32[8,16,3]{1,0,2:T(8,128)}, s32[8,16,3]{1,0,2:T(8,128)S(1)}, u32[]{:S(2)}, u32[]{:S(2)}) collective-permute-start(s32[8,16,3]{1,0,2:T(8,128)} %param.29), channel_id=1, source_target_pairs={{0,1},{1,0},{2,3},{3,2},{4,5},{5,4},{6,7},{7,6},{8,9},{9,8},{10,11... | collective-permute-start | bytes 4616 | tf_op jit(solution)/shard_map/ppermute | solution.py:667
  7.6 46.8 %collective-permute-start = (bf16[1024,768]{1,0:T(8,128)(2,1)S(1)}, bf16[1024,768]{1,0:T(8,128)(2,1)}, u32[]{:S(2)}, u32[]{:S(2)}) collective-permute-start(bf16[1024,768]{1,0:T(8,128)(2,1)S(1)} %pad_maximum_fusion.3.refs_8_), channel_id=1, source_target_pairs={{0,1},{1,0},{2,3},{3,2},{4,5},{5,4},{6,7},{7,6},{8,9},{9,8},{10,11... | collective-permute-start | bytes 4718600 | tf_op jit(solution)/shard_map/ppermute | solution.py:667
  54.4 24.5 %collective-permute-start.2 = (bf16[1024,768]{1,0:T(8,128)(2,1)}, bf16[1024,768]{1,0:T(8,128)(2,1)S(1)}, u32[]{:S(2)}, u32[]{:S(2)}) collective-permute-start(bf16[1024,768]{1,0:T(8,128)(2,1)} %collective-permute-done.refs_10_), channel_id=1, source_target_pairs={{0,2},{2,0},{4,6},{6,4},{8,10},{10,8},{12,14},{14,12},{16,18},{18,... | collective-permute-start | bytes 4718600 | tf_op jit(solution)/shard_map/ppermute | solution.py:667
  54.5 24.4 %collective-permute-start.3 = (bf16[256,1024]{1,0:T(8,128)(2,1)}, bf16[256,1024]{1,0:T(8,128)(2,1)S(1)}, u32[]{:S(2)}, u32[]{:S(2)}) collective-permute-start(bf16[256,1024]{1,0:T(8,128)(2,1)} %constant_dynamic-slice_fusion.15), channel_id=1, source_target_pairs={{0,1},{1,0},{2,3},{3,2},{4,5},{5,4},{6,7},{7,6},{8,9},{9,8},{10,11... | collective-permute-start | bytes 1572872 | tf_op jit(solution)/shard_map/ppermute | solution.py:667
  79.0 28.7 %collective-permute-start.5 = (bf16[1024,512]{1,0:T(8,128)(2,1)S(1)}, bf16[1024,512]{1,0:T(8,128)(2,1)S(1)}, u32[]{:S(2)}, u32[]{:S(2)}) collective-permute-start(bf16[1024,512]{1,0:T(8,128)(2,1)S(1)} %copy-done.59), channel_id=1, source_target_pairs={{0,1},{1,0},{2,3},{3,2},{4,5},{5,4},{6,7},{7,6},{8,9},{9,8},{10,11... | collective-permute-start | bytes 3145736 | tf_op jit(solution)/shard_map/ppermute | solution.py:667
  79.8 18.5 %collective-permute-start.4 = (bf16[256,1024]{1,0:T(8,128)(2,1)S(1)}, bf16[256,1024]{1,0:T(8,128)(2,1)S(1)}, u32[]{:S(2)}, u32[]{:S(2)}) collective-permute-start(bf16[256,1024]{1,0:T(8,128)(2,1)S(1)} %collective-permute-done.3.refs_6_), channel_id=1, source_target_pairs={{0,2},{2,0},{4,6},{6,4},{8,10},{10,8},{12,14},{14,12},{16,18},{18,... | collective-permute-start | bytes 1572872 | tf_op jit(solution)/shard_map/ppermute | solution.py:667
  107.7 27.6 %collective-permute-start.6 = (bf16[1024,512]{1,0:T(8,128)(2,1)S(1)}, bf16[1024,512]{1,0:T(8,128)(2,1)S(1)}, u32[]{:S(2)}, u32[]{:S(2)}) collective-permute-start(bf16[1024,512]{1,0:T(8,128)(2,1)S(1)} %collective-permute-done.5.refs_4_.refs_8_), channel_id=1, source_target_pairs={{0,4},{2,6},{4,0},{6,2},{8,12},{10,14},{12,8},{14,10},{16,20},{18,... | collective-permute-start | bytes 3145736 | tf_op jit(solution)/shard_map/ppermute | solution.py:667
  109.3 26.0 %collective-permute-start.7 = (bf16[512,1024]{1,0:T(8,128)(2,1)S(1)}, bf16[512,1024]{1,0:T(8,128)(2,1)S(1)}, u32[]{:S(2)}, u32[]{:S(2)}) collective-permute-start(bf16[512,1024]{1,0:T(8,128)(2,1)S(1)} %constant_dynamic-slice_fusion.13), channel_id=1, source_target_pairs={{0,1},{1,0},{2,3},{3,2},{4,5},{5,4},{6,7},{7,6},{8,9},{9,8},{10,11... | collective-permute-start | bytes 3145736 | tf_op jit(solution)/shard_map/ppermute | solution.py:667
  145.7 25.6 %collective-permute-start.8 = (bf16[512,1024]{1,0:T(8,128)(2,1)S(1)}, bf16[512,1024]{1,0:T(8,128)(2,1)S(1)}, u32[]{:S(2)}, u32[]{:S(2)}) collective-permute-start(bf16[512,1024]{1,0:T(8,128)(2,1)S(1)} %collective-permute-done.7.refs_6_.refs_8_), channel_id=1, source_target_pairs={{0,4},{2,6},{4,0},{6,2},{8,12},{10,14},{12,8},{14,10},{16,20},{18,... | collective-permute-start | bytes 3145736 | tf_op jit(solution)/shard_map/ppermute | solution.py:667
  146.3 25.1 %collective-permute-start.9 = (bf16[1024,512]{1,0:T(8,128)(2,1)S(1)}, bf16[1024,512]{1,0:T(8,128)(2,1)}, u32[]{:S(2)}, u32[]{:S(2)}) collective-permute-start(bf16[1024,512]{1,0:T(8,128)(2,1)S(1)} %collective-permute-done.5.refs_4_.refs_8_), channel_id=1, source_target_pairs={{0,2},{2,0},{4,6},{6,4},{8,10},{10,8},{12,14},{14,12},{16,18},{18,... | collective-permute-start | bytes 3145736 | tf_op jit(solution)/shard_map/ppermute | solution.py:667
  171.3 18.1 %collective-permute-start.11 = (bf16[512,1024]{1,0:T(8,128)(2,1)S(1)}, bf16[512,1024]{1,0:T(8,128)(2,1)S(1)}, u32[]{:S(2)}, u32[]{:S(2)}) collective-permute-start(bf16[512,1024]{1,0:T(8,128)(2,1)S(1)} %collective-permute-done.7.refs_6_.refs_8_), channel_id=1, source_target_pairs={{0,2},{2,0},{4,6},{6,4},{8,10},{10,8},{12,14},{14,12},{16,18},{18,... | collective-permute-start | bytes 3145736 | tf_op jit(solution)/shard_map/ppermute | solution.py:667
  171.4 18.0 %collective-permute-start.12 = (bf16[512,1024]{1,0:T(8,128)(2,1)S(1)}, bf16[512,1024]{1,0:T(8,128)(2,1)S(1)}, u32[]{:S(2)}, u32[]{:S(2)}) collective-permute-start(bf16[512,1024]{1,0:T(8,128)(2,1)S(1)} %collective-permute-done.8.refs_7_.refs_9_), channel_id=1, source_target_pairs={{0,2},{2,0},{4,6},{6,4},{8,10},{10,8},{12,14},{14,12},{16,18},{18,... | collective-permute-start | bytes 3145736 | tf_op jit(solution)/shard_map/ppermute | solution.py:667
  214.1 11.1 %collective-permute-start.15 = (bf16[1024,1024]{1,0:T(8,128)(2,1)}, bf16[1024,1024]{1,0:T(8,128)(2,1)}, u32[]{:S(2)}, u32[]{:S(2)}) collective-permute-start(bf16[1024,1024]{1,0:T(8,128)(2,1)} %convolution_convert_fusion.2), channel_id=1, source_target_pairs={{0,2},{2,0},{4,6},{6,4},{8,10},{10,8},{12,14},{14,12},{16,18},{18,... | collective-permute-start | bytes 6291464 | tf_op jit(solution)/shard_map/ppermute | solution.py:667
  222.0 31.4 %collective-permute-start.16 = (bf16[1024,1024]{1,0:T(8,128)(2,1)}, bf16[1024,1024]{1,0:T(8,128)(2,1)}, u32[]{:S(2)}, u32[]{:S(2)}) collective-permute-start(bf16[1024,1024]{1,0:T(8,128)(2,1)} %convolution_convert_fusion.6), channel_id=1, source_target_pairs={{0,2},{2,0},{4,6},{6,4},{8,10},{10,8},{12,14},{14,12},{16,18},{18,... | collective-permute-start | bytes 6291464 | tf_op jit(solution)/shard_map/ppermute | solution.py:667
  222.0 34.1 %collective-permute-start.17 = (bf16[1024,1024]{1,0:T(8,128)(2,1)}, bf16[1024,1024]{1,0:T(8,128)(2,1)}, u32[]{:S(2)}, u32[]{:S(2)}) collective-permute-start(bf16[1024,1024]{1,0:T(8,128)(2,1)} %convolution_convert_fusion), channel_id=1, source_target_pairs={{0,2},{2,0},{4,6},{6,4},{8,10},{10,8},{12,14},{14,12},{16,18},{18,... | collective-permute-start | bytes 6291464 | tf_op jit(solution)/shard_map/ppermute | solution.py:667
  230.2 63.9 %collective-permute-start.18 = (bf16[1024,1024]{1,0:T(8,128)(2,1)S(1)}, bf16[1024,1024]{1,0:T(8,128)(2,1)}, u32[]{:S(2)}, u32[]{:S(2)}) collective-permute-start(bf16[1024,1024]{1,0:T(8,128)(2,1)S(1)} %slice_bitcast_fusion), channel_id=1, source_target_pairs={{0,1},{1,0},{2,3},{3,2},{4,5},{5,4},{6,7},{7,6},{8,9},{9,8},{10,11... | collective-permute-start | bytes 6291464 | tf_op jit(solution)/shard_map/ppermute | solution.py:667
  292.5 47.6 %collective-permute-start.19 = (bf16[2,512,1024]{2,1,0:T(8,128)(2,1)}, bf16[2,512,1024]{2,1,0:T(8,128)(2,1)}, u32[]{:S(2)}, u32[]{:S(2)}) collective-permute-start(bf16[2,512,1024]{2,1,0:T(8,128)(2,1)} %constant_dynamic-slice_fusion.12), channel_id=1, source_target_pairs={{0,8},{2,10},{4,12},{6,14},{8,0},{10,2},{12,4},{14,6},{16,24},{18,... | collective-permute-start | bytes 6291464 | tf_op jit(solution)/shard_map/ppermute | solution.py:667
  315.9 27.4 %collective-permute-start.20 = (bf16[512,1024]{1,0:T(8,128)(2,1)}, bf16[512,1024]{1,0:T(8,128)(2,1)}, u32[]{:S(2)}, u32[]{:S(2)}) collective-permute-start(bf16[512,1024]{1,0:T(8,128)(2,1)} %constant_dynamic-slice_fusion.11), channel_id=1, source_target_pairs={{0,4},{2,6},{4,0},{6,2},{8,12},{10,14},{12,8},{14,10},{16,20},{18,... | collective-permute-start | bytes 3145736 | tf_op jit(solution)/shard_map/ppermute | solution.py:667
  325.7 42.1 %collective-permute-start.22 = (bf16[1024,640]{0,1:T(8,128)(2,1)}, bf16[1024,640]{0,1:T(8,128)(2,1)}, u32[]{:S(2)}, u32[]{:S(2)}) collective-permute-start(bf16[1024,640]{0,1:T(8,128)(2,1)} %pad_maximum_fusion.7), channel_id=1, source_target_pairs={{0,2},{2,0},{4,6},{6,4},{8,10},{10,8},{12,14},{14,12},{16,18},{18,... | collective-permute-start | bytes 3932168 | tf_op jit(solution)/shard_map/ppermute | solution.py:667
  328.3 41.4 %collective-permute-start.23 = (bf16[1024,640]{0,1:T(8,128)(2,1)}, bf16[1024,640]{0,1:T(8,128)(2,1)}, u32[]{:S(2)}, u32[]{:S(2)}) collective-permute-start(bf16[1024,640]{0,1:T(8,128)(2,1)} %pad_maximum_fusion.9), channel_id=1, source_target_pairs={{0,2},{2,0},{4,6},{6,4},{8,10},{10,8},{12,14},{14,12},{16,18},{18,... | collective-permute-start | bytes 3932168 | tf_op jit(solution)/shard_map/ppermute | solution.py:667
  346.5 25.3 %collective-permute-start.21 = (bf16[256,1024]{1,0:T(8,128)(2,1)}, bf16[256,1024]{1,0:T(8,128)(2,1)}, u32[]{:S(2)}, u32[]{:S(2)}) collective-permute-start(bf16[256,1024]{1,0:T(8,128)(2,1)} %constant_dynamic-slice_fusion.10), channel_id=1, source_target_pairs={{0,8},{2,10},{4,12},{6,14},{8,0},{10,2},{12,4},{14,6},{16,24},{18,... | collective-permute-start | bytes 1572872 | tf_op jit(solution)/shard_map/ppermute | solution.py:667
  367.0 23.9 %collective-permute-start.24 = (bf16[512,1024]{1,0:T(8,128)(2,1)}, bf16[512,1024]{1,0:T(8,128)(2,1)}, u32[]{:S(2)}, u32[]{:S(2)}) collective-permute-start(bf16[512,1024]{1,0:T(8,128)(2,1)} %slice_bitcast_fusion.2), channel_id=1, source_target_pairs={{0,1},{1,0},{2,3},{3,2},{4,5},{5,4},{6,7},{7,6},{8,9},{9,8},{10,11... | collective-permute-start | bytes 3145736 | tf_op jit(solution)/shard_map/ppermute | solution.py:667
  373.1 13.2 %collective-permute-start.25 = (bf16[128,1024]{1,0:T(8,128)(2,1)S(1)}, bf16[128,1024]{1,0:T(8,128)(2,1)}, u32[]{:S(2)}, u32[]{:S(2)}) collective-permute-start(bf16[128,1024]{1,0:T(8,128)(2,1)S(1)} %constant_dynamic-slice_fusion.9), channel_id=1, source_target_pairs={{0,16},{2,18},{4,20},{6,22},{8,24},{10,26},{12,28},{14,30},{16,0},... | collective-permute-start | bytes 786440 | tf_op jit(solution)/shard_map/ppermute | solution.py:667
  409.6 14.6 %collective-permute-start.26 = (bf16[256,1024]{1,0:T(8,128)(2,1)S(1)}, bf16[256,1024]{1,0:T(8,128)(2,1)S(1)}, u32[]{:S(2)}, u32[]{:S(2)}) collective-permute-start(bf16[256,1024]{1,0:T(8,128)(2,1)S(1)} %constant_dynamic-slice_fusion.8), channel_id=1, source_target_pairs={{0,4},{2,6},{4,0},{6,2},{8,12},{10,14},{12,8},{14,10},{16,20},{18,... | collective-permute-start | bytes 1572872 | tf_op jit(solution)/shard_map/ppermute | solution.py:667
  412.1 12.0 %collective-permute-start.27 = (bf16[128,1024]{1,0:T(8,128)(2,1)S(1)}, bf16[128,1024]{1,0:T(8,128)(2,1)S(1)}, u32[]{:S(2)}, u32[]{:S(2)}) collective-permute-start(bf16[128,1024]{1,0:T(8,128)(2,1)S(1)} %add_convert_fusion.16), channel_id=1, source_target_pairs={{0,16},{2,18},{4,20},{6,22},{8,24},{10,26},{12,28},{14,30},{16,0},... | collective-permute-start | bytes 786440 | tf_op jit(solution)/shard_map/ppermute | solution.py:667
  414.7 29.0 %collective-permute-start.29 = (bf16[1024,384]{0,1:T(8,128)(2,1)}, bf16[1024,384]{0,1:T(8,128)(2,1)}, u32[]{:S(2)}, u32[]{:S(2)}) collective-permute-start(bf16[1024,384]{0,1:T(8,128)(2,1)} %convolution_convert_fusion.14), channel_id=1, source_target_pairs={{0,2},{2,0},{4,6},{6,4},{8,10},{10,8},{12,14},{14,12},{16,18},{18,... | collective-permute-start | bytes 2359304 | tf_op jit(solution)/shard_map/ppermute | solution.py:667
  415.9 33.1 %collective-permute-start.28 = (bf16[1024,640]{0,1:T(8,128)(2,1)}, bf16[1024,640]{0,1:T(8,128)(2,1)}, u32[]{:S(2)}, u32[]{:S(2)}) collective-permute-start(bf16[1024,640]{0,1:T(8,128)(2,1)} %slice_bitcast_fusion.1), channel_id=1, source_target_pairs={{0,1},{1,0},{2,3},{3,2},{4,5},{5,4},{6,7},{7,6},{8,9},{9,8},{10,11... | collective-permute-start | bytes 3932168 | tf_op jit(solution)/shard_map/ppermute | solution.py:667
  416.6 28.8 %collective-permute-start.30 = (bf16[1024,384]{0,1:T(8,128)(2,1)}, bf16[1024,384]{0,1:T(8,128)(2,1)}, u32[]{:S(2)}, u32[]{:S(2)}) collective-permute-start(bf16[1024,384]{0,1:T(8,128)(2,1)} %convolution_convert_fusion.12), channel_id=1, source_target_pairs={{0,2},{2,0},{4,6},{6,4},{8,10},{10,8},{12,14},{14,12},{16,18},{18,... | collective-permute-start | bytes 2359304 | tf_op jit(solution)/shard_map/ppermute | solution.py:667
  424.5 26.4 %collective-permute-start.32 = (bf16[256,1024]{1,0:T(8,128)(2,1)S(1)}, bf16[256,1024]{1,0:T(8,128)(2,1)}, u32[]{:S(2)}, u32[]{:S(2)}) collective-permute-start(bf16[256,1024]{1,0:T(8,128)(2,1)S(1)} %maximum_select_fusion.13), channel_id=1, source_target_pairs={{0,8},{2,10},{4,12},{6,14},{8,0},{10,2},{12,4},{14,6},{16,24},{18,... | collective-permute-start | bytes 1572872 | tf_op jit(solution)/shard_map/ppermute | solution.py:667
  424.6 22.4 %collective-permute-start.31 = (bf16[128,1024]{1,0:T(8,128)(2,1)S(1)}, bf16[128,1024]{1,0:T(8,128)(2,1)}, u32[]{:S(2)}, u32[]{:S(2)}) collective-permute-start(bf16[128,1024]{1,0:T(8,128)(2,1)S(1)} %constant_dynamic-slice_fusion.7), channel_id=1, source_target_pairs={{0,16},{2,18},{4,20},{6,22},{8,24},{10,26},{12,28},{14,30},{16,0},... | collective-permute-start | bytes 786440 | tf_op jit(solution)/shard_map/ppermute | solution.py:667
  453.9 20.5 %collective-permute-start.35 = (bf16[512,640]{0,1:T(8,128)(2,1)}, bf16[512,640]{0,1:T(8,128)(2,1)}, u32[]{:S(2)}, u32[]{:S(2)}) collective-permute-start(bf16[512,640]{0,1:T(8,128)(2,1)} %constant_dynamic-slice_fusion.6), channel_id=1, source_target_pairs={{0,4},{2,6},{4,0},{6,2},{8,12},{10,14},{12,8},{14,10},{16,20},{18,... | collective-permute-start | bytes 1966088 | tf_op jit(solution)/shard_map/ppermute | solution.py:667
  455.5 20.3 %collective-permute-start.34 = (bf16[1024,384]{0,1:T(8,128)(2,1)S(1)}, bf16[1024,384]{0,1:T(8,128)(2,1)S(1)}, u32[]{:S(2)}, u32[]{:S(2)}) collective-permute-start(bf16[1024,384]{0,1:T(8,128)(2,1)S(1)} %slice_bitcast_fusion.3), channel_id=1, source_target_pairs={{0,1},{1,0},{2,3},{3,2},{4,5},{5,4},{6,7},{7,6},{8,9},{9,8},{10,11... | collective-permute-start | bytes 2359304 | tf_op jit(solution)/shard_map/ppermute | solution.py:667
  456.3 35.4 %collective-permute-start.37 = (bf16[512,1024]{1,0:T(8,128)(2,1)S(1)}, bf16[512,1024]{1,0:T(8,128)(2,1)}, u32[]{:S(2)}, u32[]{:S(2)}) collective-permute-start(bf16[512,1024]{1,0:T(8,128)(2,1)S(1)} %maximum_select_fusion.5), channel_id=1, source_target_pairs={{0,4},{2,6},{4,0},{6,2},{8,12},{10,14},{12,8},{14,10},{16,20},{18,... | collective-permute-start | bytes 3145736 | tf_op jit(solution)/shard_map/ppermute | solution.py:667
  456.8 17.4 %collective-permute-start.36 = (bf16[128,1024]{1,0:T(8,128)(2,1)S(1)}, bf16[128,1024]{1,0:T(8,128)(2,1)S(1)}, u32[]{:S(2)}, u32[]{:S(2)}) collective-permute-start(bf16[128,1024]{1,0:T(8,128)(2,1)S(1)} %add_convert_fusion.15), channel_id=1, source_target_pairs={{0,16},{2,18},{4,20},{6,22},{8,24},{10,26},{12,28},{14,30},{16,0},... | collective-permute-start | bytes 786440 | tf_op jit(solution)/shard_map/ppermute | solution.py:667
  494.3 12.5 %collective-permute-start.42 = (bf16[256,640]{0,1:T(8,128)(2,1)S(1)}, bf16[256,640]{0,1:T(8,128)(2,1)S(1)}, u32[]{:S(2)}, u32[]{:S(2)}) collective-permute-start(bf16[256,640]{0,1:T(8,128)(2,1)S(1)} %constant_dynamic-slice_fusion.5), channel_id=1, source_target_pairs={{0,8},{2,10},{4,12},{6,14},{8,0},{10,2},{12,4},{14,6},{16,24},{18,... | collective-permute-start | bytes 983048 | tf_op jit(solution)/shard_map/ppermute | solution.py:667
  494.7 17.2 %collective-permute-start.47 = (bf16[512,384]{0,1:T(8,128)(2,1)S(1)}, bf16[512,384]{0,1:T(8,128)(2,1)S(1)}, u32[]{:S(2)}, u32[]{:S(2)}) collective-permute-start(bf16[512,384]{0,1:T(8,128)(2,1)S(1)} %constant_dynamic-slice_fusion.3), channel_id=1, source_target_pairs={{0,8},{2,10},{4,12},{6,14},{8,0},{10,2},{12,4},{14,6},{16,24},{18,... | collective-permute-start | bytes 1179656 | tf_op jit(solution)/shard_map/ppermute | solution.py:667
  496.5 87.3 %collective-permute-start.58 = (bf16[1024,1024]{1,0:T(8,128)(2,1)S(1)}, bf16[1024,1024]{1,0:T(8,128)(2,1)}, u32[]{:S(2)}, u32[]{:S(2)}) collective-permute-start(bf16[1024,1024]{1,0:T(8,128)(2,1)S(1)} %maximum_select_fusion.2), channel_id=1, source_target_pairs={{0,2},{2,0},{4,6},{6,4},{8,10},{10,8},{12,14},{14,12},{16,18},{18,... | collective-permute-start | bytes 6291464 | tf_op jit(solution)/shard_map/ppermute | solution.py:667
  496.5 33.9 %collective-permute-start.55 = (bf16[256,1024]{1,0:T(8,128)(2,1)S(1)}, bf16[256,1024]{1,0:T(8,128)(2,1)S(1)}, u32[]{:S(2)}, u32[]{:S(2)}) collective-permute-start(bf16[256,1024]{1,0:T(8,128)(2,1)S(1)} %maximum_select_fusion.14), channel_id=1, source_target_pairs={{0,4},{2,6},{4,0},{6,2},{8,12},{10,14},{12,8},{14,10},{16,20},{18,... | collective-permute-start | bytes 1572872 | tf_op jit(solution)/shard_map/ppermute | solution.py:667
  506.9 12.3 %collective-permute-start.43 = (bf16[128,640]{0,1:T(8,128)(2,1)S(1)}, bf16[128,640]{0,1:T(8,128)(2,1)S(1)}, u32[]{:S(2)}, u32[]{:S(2)}) collective-permute-start(bf16[128,640]{0,1:T(8,128)(2,1)S(1)} %constant_dynamic-slice_fusion.4), channel_id=1, source_target_pairs={{0,16},{2,18},{4,20},{6,22},{8,24},{10,26},{12,28},{14,30},{16,0},... | collective-permute-start | bytes 491528 | tf_op jit(solution)/shard_map/ppermute | solution.py:667
  529.3 16.8 %collective-permute-start.45 = (bf16[256,640]{0,1:T(8,128)(2,1)S(1)}, bf16[256,640]{0,1:T(8,128)(2,1)S(1)}, u32[]{:S(2)}, u32[]{:S(2)}) collective-permute-start(bf16[256,640]{0,1:T(8,128)(2,1)S(1)} %maximum_select_fusion.16), channel_id=1, source_target_pairs={{0,8},{2,10},{4,12},{6,14},{8,0},{10,2},{12,4},{14,6},{16,24},{18,... | collective-permute-start | bytes 983048 | tf_op jit(solution)/shard_map/ppermute | solution.py:667
  531.8 43.5 %collective-permute-start.56 = (bf16[512,1024]{1,0:T(8,128)(2,1)}, bf16[512,1024]{1,0:T(8,128)(2,1)}, u32[]{:S(2)}, u32[]{:S(2)}) collective-permute-start(bf16[512,1024]{1,0:T(8,128)(2,1)} %maximum_select_fusion.10), channel_id=1, source_target_pairs={{0,8},{2,10},{4,12},{6,14},{8,0},{10,2},{12,4},{14,6},{16,24},{18,... | collective-permute-start | bytes 3145736 | tf_op jit(solution)/shard_map/ppermute | solution.py:667
  539.7 12.3 %collective-permute-start.51 = (bf16[256,384]{0,1:T(8,128)(2,1)S(1)}, bf16[256,384]{0,1:T(8,128)(2,1)S(1)}, u32[]{:S(2)}, u32[]{:S(2)}) collective-permute-start(bf16[256,384]{0,1:T(8,128)(2,1)S(1)} %maximum_select_fusion.17), channel_id=1, source_target_pairs={{0,4},{2,6},{4,0},{6,2},{8,12},{10,14},{12,8},{14,10},{16,20},{18,... | collective-permute-start | bytes 589832 | tf_op jit(solution)/shard_map/ppermute | solution.py:667
  546.3 26.3 %collective-permute-start.46 = (bf16[512,640]{0,1:T(8,128)(2,1)S(1)}, bf16[512,640]{0,1:T(8,128)(2,1)}, u32[]{:S(2)}, u32[]{:S(2)}) collective-permute-start(bf16[512,640]{0,1:T(8,128)(2,1)S(1)} %maximum_select_fusion.12), channel_id=1, source_target_pairs={{0,4},{2,6},{4,0},{6,2},{8,12},{10,14},{12,8},{14,10},{16,20},{18,... | collective-permute-start | bytes 1966088 | tf_op jit(solution)/shard_map/ppermute | solution.py:667
  550.0 12.8 %collective-permute-start.40 = (f32[9,1024]{1,0:T(8,128)S(1)}, f32[9,1024]{1,0:T(8,128)S(1)}, u32[]{:S(2)}, u32[]{:S(2)}) collective-permute-start(f32[9,1024]{1,0:T(8,128)S(1)} %add.247), channel_id=1, source_target_pairs={{0,8},{2,10},{4,12},{6,14},{8,0},{10,2},{12,4},{14,6},{16,24},{18,... | collective-permute-start | bytes 110600 | tf_op jit(solution)/shard_map/ppermute | solution.py:667
  552.1 19.4 %collective-permute-start.52 = (bf16[512,384]{0,1:T(8,128)(2,1)S(1)}, bf16[512,384]{0,1:T(8,128)(2,1)S(1)}, u32[]{:S(2)}, u32[]{:S(2)}) collective-permute-start(bf16[512,384]{0,1:T(8,128)(2,1)S(1)} %maximum_select_fusion.15), channel_id=1, source_target_pairs={{0,8},{2,10},{4,12},{6,14},{8,0},{10,2},{12,4},{14,6},{16,24},{18,... | collective-permute-start | bytes 1179656 | tf_op jit(solution)/shard_map/ppermute | solution.py:667
  572.5 26.8 %collective-permute-start.54 = (bf16[1024,384]{0,1:T(8,128)(2,1)}, bf16[1024,384]{0,1:T(8,128)(2,1)}, u32[]{:S(2)}, u32[]{:S(2)}) collective-permute-start(bf16[1024,384]{0,1:T(8,128)(2,1)} %maximum_select_fusion.11), channel_id=1, source_target_pairs={{0,2},{2,0},{4,6},{6,4},{8,10},{10,8},{12,14},{14,12},{16,18},{18,... | collective-permute-start | bytes 2359304 | tf_op jit(solution)/shard_map/ppermute | solution.py:667
  574.7 26.6 %collective-permute-start.53 = (bf16[1024,640]{0,1:T(8,128)(2,1)S(1)}, bf16[1024,640]{0,1:T(8,128)(2,1)}, u32[]{:S(2)}, u32[]{:S(2)}) collective-permute-start(bf16[1024,640]{0,1:T(8,128)(2,1)S(1)} %maximum_select_fusion.4), channel_id=1, source_target_pairs={{0,2},{2,0},{4,6},{6,4},{8,10},{10,8},{12,14},{14,12},{16,18},{18,... | collective-permute-start | bytes 3932168 | tf_op jit(solution)/shard_map/ppermute | solution.py:667
  579.9 32.3 %collective-permute-start.57 = (bf16[1024,1024]{1,0:T(8,128)(2,1)}, bf16[1024,1024]{1,0:T(8,128)(2,1)}, u32[]{:S(2)}, u32[]{:S(2)}) collective-permute-start(bf16[1024,1024]{1,0:T(8,128)(2,1)} %maximum_select_fusion.3), channel_id=1, source_target_pairs={{0,2},{2,0},{4,6},{6,4},{8,10},{10,8},{12,14},{14,12},{16,18},{18,... | collective-permute-start | bytes 6291464 | tf_op jit(solution)/shard_map/ppermute | solution.py:667
  (108 other events, 772.8 us)

commit v3 on v2

v3 whole, which is shorter than its diff:
```python
import jax
import jax.numpy as jnp
from jax import lax
from jax.experimental import pallas as pl
from jax.experimental.pallas import tpu as pltpu
from jax.sharding import PartitionSpec as P

HD = 64
BLOCK = 64
SEQ = 1024
PAIR = 2 * HD
BF16 = jnp.bfloat16
F32 = jnp.float32
NT = (((1,), (1,)), ((), ()))
TN = (((0,), (0,)), ((), ()))


def layer_norm(values, norm_gain, norm_bias):
    center = values - jnp.mean(values, axis=-1, keepdims=True)
    spread = jnp.mean(center * center, axis=-1, keepdims=True)
    return center * lax.rsqrt(spread + 1e-05) * norm_gain + norm_bias


def block_mask(rand_blocks):
    blocks = SEQ // BLOCK
    row_ids = jnp.arange(blocks)[:, None]
    col_ids = jnp.arange(blocks)[None, :]
    window = (
        (jnp.abs(row_ids - col_ids) <= 1)
        | (col_ids == 0)
        | (col_ids == blocks - 1)
        | (row_ids == 0)
        | (row_ids == blocks - 1)
    )
    picked = jnp.any(rand_blocks[:, :, :, None] == jnp.arange(blocks)[None, None, None, :], axis=2)
    allowed = window[None] | picked
    return jnp.repeat(jnp.repeat(allowed, BLOCK, axis=1), BLOCK, axis=2)


def attend_forward_split(joined_seq, allowed, scaling):
    queries = joined_seq[:, 0]
    key_rows = joined_seq[:, 1]
    value_rows = joined_seq[:, 2]
    scores = (
        jnp.einsum("qhd,khd->hqk", queries, key_rows, preferred_element_type=jnp.float32) * scaling
    )
    scores = jnp.where(allowed, scores, -1e30)
    highest = jnp.max(scores, axis=-1, keepdims=True)
    shifted = jnp.exp(scores - highest)
    row_totals = jnp.sum(shifted, axis=-1, keepdims=True)
    attn_probs = (shifted / row_totals).astype(jnp.bfloat16)
    context = jnp.einsum("hqk,khd->qhd", attn_probs, value_rows, preferred_element_type=jnp.float32)
    return (context.astype(jnp.bfloat16), (highest + jnp.log(row_totals))[..., 0])


def attend_backward_split(seq_items, allowed, scaling):
    joined_seq, grad_context, row_lse = seq_items
    queries = joined_seq[:, 0]
    key_rows = joined_seq[:, 1]
    value_rows = joined_seq[:, 2]
    scores = (
        jnp.einsum("qhd,khd->hqk", queries, key_rows, preferred_element_type=jnp.float32) * scaling
    )
    scores = jnp.where(allowed, scores, -1e30)
    attn_probs = jnp.exp(scores - row_lse[..., None])
    grad_values = jnp.einsum(
        "hqk,qhd->khd",
        attn_probs.astype(jnp.bfloat16),
        grad_context,
        preferred_element_type=jnp.float32,
    ).astype(jnp.bfloat16)
    grad_probs = jnp.einsum(
        "qhd,khd->hqk", grad_context, value_rows, preferred_element_type=jnp.float32
    )
    row_inner = jnp.sum(grad_probs * attn_probs, axis=-1, keepdims=True)
    grad_scores = (attn_probs * (grad_probs - row_inner)).astype(jnp.bfloat16)
    grad_queries = (
        jnp.einsum("hqk,khd->qhd", grad_scores, key_rows, preferred_element_type=jnp.float32)
        * scaling
    ).astype(jnp.bfloat16)
    grad_keys = (
        jnp.einsum("hqk,qhd->khd", grad_scores, queries, preferred_element_type=jnp.float32)
        * scaling
    ).astype(jnp.bfloat16)
    return jnp.stack([grad_queries, grad_keys, grad_values], axis=1)


def split_sequence(
    hidden_in,
    out_grad,
    ln1_gain,
    ln1_bias,
    w_query,
    w_key,
    w_value,
    w_out,
    ln2_gain,
    ln2_bias,
    w_up,
    b_up,
    w_down,
    b_down,
    rand_blocks,
):
    local_heads = rand_blocks.shape[0]
    head_width = local_heads * HD
    local_rows = hidden_in.shape[0]
    seq_count = local_rows * lax.axis_size("mp") // SEQ
    scaling = HD ** (-0.5)
    allowed = block_mask(rand_blocks)
    inputs = hidden_in.astype(jnp.float32)
    w_joined = jnp.concatenate([w_query, w_key, w_value], axis=1)
    normed_one = layer_norm(inputs, ln1_gain, ln1_bias).astype(jnp.bfloat16)
    rows_one = lax.all_gather(normed_one, "mp", axis=0, tiled=True)
    joined = jnp.dot(rows_one, w_joined, preferred_element_type=jnp.float32).astype(jnp.bfloat16)
    joined_seq = joined.reshape(seq_count, SEQ, 3, local_heads, HD)
    context, row_lse = lax.map(
        lambda seq_block: attend_forward_split(seq_block, allowed, scaling), joined_seq
    )
    context_rows = context.reshape(seq_count * SEQ, head_width)
    middle = inputs + lax.psum_scatter(
        jnp.dot(context_rows, w_out, preferred_element_type=jnp.float32).astype(jnp.bfloat16),
        "mp",
        scatter_dimension=0,
        tiled=True,
    ).astype(jnp.float32)
    normed_two = layer_norm(middle, ln2_gain, ln2_bias).astype(jnp.bfloat16)
    rows_two = lax.all_gather(normed_two, "mp", axis=0, tiled=True)
    up_pre = jnp.dot(rows_two, w_up, preferred_element_type=jnp.float32) + b_up
    hidden = jax.nn.gelu(up_pre, approximate=True).astype(jnp.bfloat16)
    output = (
        middle
        + (
            lax.psum_scatter(
                jnp.dot(hidden, w_down, preferred_element_type=jnp.float32).astype(jnp.bfloat16),
                "mp",
                scatter_dimension=0,
                tiled=True,
            ).astype(jnp.float32)
            + b_down
        )
    ).astype(jnp.bfloat16)
    grad_out = out_grad.astype(jnp.float32)
    bias_down = jnp.sum(grad_out, axis=0)
    rows_ffn = lax.all_gather(out_grad, "mp", axis=0, tiled=True)
    grad_hidden = jnp.einsum("nd,fd->nf", rows_ffn, w_down, preferred_element_type=jnp.float32)
    grad_down = jnp.einsum("nf,nd->fd", hidden, rows_ffn, preferred_element_type=jnp.float32)
    gelu_value, gelu_pull = jax.vjp(lambda pre_act: jax.nn.gelu(pre_act, approximate=True), up_pre)
    grad_up = gelu_pull(grad_hidden)[0].astype(jnp.bfloat16)
    bias_up = jnp.sum(grad_up, axis=0, dtype=jnp.float32)
    grad_up_weight = jnp.einsum("nd,nf->df", rows_two, grad_up, preferred_element_type=jnp.float32)
    grad_normed_two = lax.psum_scatter(
        jnp.einsum("nf,df->nd", grad_up, w_up, preferred_element_type=jnp.float32).astype(
            jnp.bfloat16
        ),
        "mp",
        scatter_dimension=0,
        tiled=True,
    ).astype(jnp.float32)
    norm_value_two, norm_pull_two = jax.vjp(layer_norm, middle, ln2_gain, ln2_bias)
    grad_mid_norm, gain_two, bias_two = norm_pull_two(grad_normed_two)
    grad_middle = grad_out + grad_mid_norm
    grad_attn = grad_middle.astype(jnp.bfloat16)
    rows_attn = lax.all_gather(grad_attn, "mp", axis=0, tiled=True)
    grad_context = jnp.einsum(
        "nd,ed->ne", rows_attn, w_out, preferred_element_type=jnp.float32
    ).astype(jnp.bfloat16)
    grad_out_weight = jnp.einsum(
        "ne,nd->ed", context_rows, rows_attn, preferred_element_type=jnp.float32
    )
    grad_joined = lax.map(
        lambda seq_items: attend_backward_split(seq_items, allowed, scaling),
        (joined_seq, grad_context.reshape(seq_count, SEQ, local_heads, HD), row_lse),
    )
    grad_joined = grad_joined.reshape(seq_count * SEQ, 3 * head_width)
    grad_joined_weight = jnp.einsum(
        "nd,ne->de", rows_one, grad_joined, preferred_element_type=jnp.float32
    )
    grad_normed_one = lax.psum_scatter(
        jnp.einsum("ne,de->nd", grad_joined, w_joined, preferred_element_type=jnp.float32).astype(
            jnp.bfloat16
        ),
        "mp",
        scatter_dimension=0,
        tiled=True,
    ).astype(jnp.float32)
    norm_value_one, norm_pull_one = jax.vjp(layer_norm, inputs, ln1_gain, ln1_bias)
    grad_in_norm, gain_one, bias_one = norm_pull_one(grad_normed_one)
    input_grad = grad_middle + grad_in_norm
    grad_joined_weight, grad_out_weight, grad_up_weight, bias_up, grad_down = (
        lax.psum(grad_joined_weight.astype(jnp.bfloat16), "dp").astype(jnp.float32),
        lax.psum(grad_out_weight.astype(jnp.bfloat16), "dp").astype(jnp.float32),
        lax.psum(grad_up_weight.astype(jnp.bfloat16), "dp").astype(jnp.float32),
        lax.psum(bias_up.astype(jnp.bfloat16), "dp").astype(jnp.float32),
        lax.psum(grad_down.astype(jnp.bfloat16), "dp").astype(jnp.float32),
    )
    gain_one, bias_one, gain_two, bias_two, bias_down = lax.psum(
        (gain_one, bias_one, gain_two, bias_two, bias_down), ("dp", "mp")
    )
    grad_query = grad_joined_weight[:, :head_width]
    grad_key = grad_joined_weight[:, head_width : 2 * head_width]
    grad_value = grad_joined_weight[:, 2 * head_width :]
    return (
        output,
        input_grad,
        gain_one,
        bias_one,
        grad_query,
        grad_key,
        grad_value,
        grad_out_weight,
        gain_two,
        bias_two,
        grad_up_weight,
        bias_up,
        grad_down,
        bias_down,
    )


VMEM_LIMIT = 56 << 20
TILE = 256
SPAN = 512
WIDE = 512
PACE = 0.02


def mm(left, right, dims=(((1,), (0,)), ((), ()))):
    return lax.dot_general(left, right, dims, preferred_element_type=F32)


def call(body, *, grid, in_specs, out_specs, out_shape, micros, name, scratch=(), scalars=1):
    return pl.pallas_call(
        body,
        grid_spec=pltpu.PrefetchScalarGridSpec(
            num_scalar_prefetch=scalars,
            grid=grid,
            in_specs=in_specs,
            out_specs=out_specs,
            scratch_shapes=list(scratch),
        ),
        out_shape=out_shape,
        compiler_params=pltpu.CompilerParams(vmem_limit_bytes=VMEM_LIMIT),
        cost_estimate=pl.CostEstimate(
            flops=int(micros * PACE * 1e9), bytes_accessed=0, transcendentals=0
        ),
        name=name,
    )


def shape(rows, columns, dtype=BF16):
    return jax.ShapeDtypeStruct((rows, columns), dtype)


def row_tile(width, dtype=None):
    return pl.BlockSpec((TILE, width), lambda i, s: (i, 0))


def column_tile(height):
    return pl.BlockSpec((height, TILE), lambda i, s: (0, i))


def resident(rows, columns):
    return pl.BlockSpec((rows, columns), lambda i, s: (0, 0))


def norm_parts(values):
    center = values - jnp.mean(values, axis=-1, keepdims=True)
    spread = jnp.mean(center * center, axis=-1, keepdims=True)
    return center, lax.rsqrt(spread + 1e-05)


def norm_backward(values, gain, grads):
    center, scale = norm_parts(values)
    unit = center * scale
    scaled = grads * gain
    mean_g = jnp.mean(scaled, axis=-1, keepdims=True)
    mean_gu = jnp.mean(scaled * unit, axis=-1, keepdims=True)
    grad_in = scale * (scaled - mean_g - unit * mean_gu)
    return (
        grad_in,
        jnp.sum(grads * unit, axis=0, keepdims=True),
        jnp.sum(grads, axis=0, keepdims=True),
    )


def flipped(rows):
    return rows.astype(F32).T.astype(BF16)


def accumulate(ref, value):
    @pl.when(pl.program_id(0) == 0)
    def _():
        ref[...] = value

    @pl.when(pl.program_id(0) > 0)
    def _():
        ref[...] += value


def norm_in_kernel(s, x_ref, g_ref, gain_ref, bias_ref, n_ref, sum_ref):
    center, scale = norm_parts(x_ref[...].astype(F32))
    n_ref[...] = (center * scale * gain_ref[...] + bias_ref[...]).astype(BF16)
    accumulate(sum_ref, jnp.sum(g_ref[...].astype(F32), axis=0, keepdims=True))


def norm_in(place, hidden_in, out_grad, gain, bias):
    rows, width = hidden_in.shape
    return call(
        norm_in_kernel,
        grid=(rows // TILE,),
        in_specs=[row_tile(width), row_tile(width), resident(1, width), resident(1, width)],
        out_specs=[row_tile(width), resident(1, width)],
        out_shape=[shape(rows, width), shape(1, width, F32)],
        micros=5,
        name="norm_in",
    )(place, hidden_in, out_grad, gain, bias)


def head_lanes(rows, head):
    lanes = lax.broadcasted_iota(jnp.int32, rows.shape, 1)
    return jnp.where(lanes // HD == head, rows, jnp.zeros_like(rows))


def spread_bias(bias, dims):
    blocks = bias.shape[0]
    tokens = lax.broadcasted_iota(jnp.int32, (blocks, blocks * BLOCK), 1) // BLOCK
    which = lax.broadcasted_iota(jnp.int32, tokens.shape, 0)
    return mm(bias, jnp.where(tokens == which, 1.0, 0.0).astype(BF16), dims)


def add_blocks(scores, bias):
    rows, width = scores.shape
    return (scores.reshape(rows // BLOCK, BLOCK, width) + bias[:, None, :]).reshape(rows, width)


def attend_forward_kernel(s, q_ref, k_ref, v_ref, bias_ref, context_ref, lse_ref):
    scaling = HD ** (-0.5)
    bias = [spread_bias(bias_ref[head], (((1,), (0,)), ((), ()))) for head in range(2)]
    jobs = [(start, head) for start in range(0, q_ref.shape[0], SPAN) for head in range(2)]

    def score(job):
        start, head = job
        queries = q_ref[start : start + SPAN, :] * jnp.asarray(scaling, BF16)
        return mm(head_lanes(queries, head), k_ref[...], NT)

    ahead = score(jobs[0])
    parts = []
    for index, (start, head) in enumerate(jobs):
        rows = slice(start, start + SPAN)
        scores = ahead
        if index + 1 < len(jobs):
            ahead = score(jobs[index + 1])
        scores = add_blocks(scores, bias[head][start // BLOCK : (start + SPAN) // BLOCK])
        highest = jnp.max(scores, axis=1, keepdims=True)
        shifted = jnp.exp(scores - highest)
        totals = jnp.sum(shifted, axis=1, keepdims=True)
        parts.append(mm(shifted.astype(BF16), v_ref[...]) / totals)
        lse_ref[0, head : head + 1, rows] = (highest + jnp.log(totals)).T
        if head == 1:
            lanes = lax.broadcasted_iota(jnp.int32, parts[0].shape, 1)
            context_ref[rows, :] = jnp.where(lanes < HD, parts[0], parts[1]).astype(BF16)
            parts = []


def thin_block(column):
    return pl.BlockSpec((SEQ, PAIR), lambda p, s: (0, column(p)))


def attend_forward(place, which, qkv, bias):
    pairs = 2
    blocks = SEQ // BLOCK
    return call(
        attend_forward_kernel,
        grid=(pairs,),
        in_specs=[
            thin_block(lambda p: p),
            thin_block(lambda p: pairs + p),
            thin_block(lambda p: 2 * pairs + p),
            pl.BlockSpec((2, blocks, blocks), lambda p, s: (s[which % 2] * pairs + p, 0, 0)),
        ],
        out_specs=[thin_block(lambda p: p), pl.BlockSpec((1, 2, SEQ), lambda p, s: (p, 0, 0))],
        out_shape=[shape(SEQ, pairs * PAIR), jax.ShapeDtypeStruct((pairs, 2, SEQ), F32)],
        micros=12,
        name="attend_forward",
    )(place, qkv, qkv, qkv, bias)


def attend_backward_kernel(
    outs,
    s,
    q_ref,
    k_ref,
    v_ref,
    grad_ref,
    context_ref,
    lse_ref,
    bias_ref,
    n_hbm,
    ga_hbm,
    *refs,
):
    *extras, out_ref, w_ref, key_acc, value_acc, flat_ref, n_ref, ga_ref, more_ref, sem = refs
    copies = [pltpu.make_async_copy(n_hbm, n_ref, sem.at[0])]
    if outs:
        all_contexts_ref = extras.pop(0)
        copies.append(pltpu.make_async_copy(ga_hbm, ga_ref, sem.at[1]))
    if extras:
        copies.append(pltpu.make_async_copy(extras[0], more_ref, sem.at[2]))
    for copy in copies:
        copy.start()
    scaling = HD ** (-0.5)
    key_rows = k_ref[...]
    value_rows = v_ref[...]
    keys_t = flipped(key_rows)
    bias = [spread_bias(bias_ref[head], TN) for head in range(2)]
    for start in range(0, q_ref.shape[0], SPAN):
        rows = slice(start, start + SPAN)
        queries = q_ref[rows, :] * jnp.asarray(scaling, BF16)
        grads = grad_ref[rows, :]
        inner_t = (grads.astype(F32) * context_ref[rows, :].astype(F32)).T
        probs, slopes, masked_q, masked_g, parts = [], [], [], [], []
        for head in range(2):
            query_h, grad_h = head_lanes(queries, head), head_lanes(grads, head)
            scores = add_blocks(mm(key_rows, query_h, NT), bias[head][:, rows])
            attn = jnp.exp(scores - lse_ref[0, head : head + 1, rows])
            inner = jnp.sum(inner_t[head * HD : (head + 1) * HD], axis=0, keepdims=True)
            slope = (attn * (mm(value_rows, grad_h, NT) - inner)).astype(BF16)
            parts.append(mm(keys_t[head * HD : (head + 1) * HD], slope) * scaling)
            probs.append(attn.astype(BF16))
            slopes.append(slope)
            masked_q.append(query_h)
            masked_g.append(grad_h)
        grad_q = jnp.concatenate(parts, axis=0)
        flat_ref[:PAIR, rows] = grad_q.astype(BF16)
        out_ref[rows, :PAIR] = grad_q.T.astype(BF16)
        grad_k = mm(jnp.concatenate(slopes, axis=1), jnp.concatenate(masked_q, axis=0))
        grad_v = mm(jnp.concatenate(probs, axis=1), jnp.concatenate(masked_g, axis=0))
        if start == 0:
            key_acc[...] = grad_k
            value_acc[...] = grad_v
        else:
            key_acc[...] += grad_k
            value_acc[...] += grad_v
    for part, acc in ((1, key_acc), (2, value_acc)):
        columns = slice(part * PAIR, (part + 1) * PAIR)
        total = acc[...]
        out_ref[:, columns] = total.astype(BF16)
        flat_ref[columns, :] = total.T.astype(BF16)
    for copy in copies:
        copy.wait()

    def give(lines, product):
        if extras:
            product = product + more_ref[lines, :].astype(F32)
        w_ref[lines, :] = product.astype(BF16)

    for part in range(3):
        lines = slice(part * PAIR, (part + 1) * PAIR)
        give(lines, mm(flat_ref[lines, :], n_ref[...]))
    if outs:
        give(slice(3 * PAIR, w_ref.shape[0]), mm(flipped(all_contexts_ref[...]), ga_ref[...]))


def attend_backward(
    place, which, pair, qkv, grad_context, context, row_lse, bias, normed, grad, more=None
):
    pairs = 2
    blocks = SEQ // BLOCK
    width = normed.shape[1]
    lines = 3 * PAIR + (context.shape[1] if pair == 0 else 0)
    outs = pair == 0
    return call(
        lambda *refs: attend_backward_kernel(outs, *refs),
        grid=(1,),
        in_specs=[
            thin_block(lambda p: pair),
            thin_block(lambda p: pairs + pair),
            thin_block(lambda p: 2 * pairs + pair),
            thin_block(lambda p: pair),
            thin_block(lambda p: pair),
            pl.BlockSpec((1, 2, SEQ), lambda p, s: (pair, 0, 0)),
            pl.BlockSpec((2, blocks, blocks), lambda p, s: (s[which % 2] * pairs + pair, 0, 0)),
            pl.BlockSpec(memory_space=pl.ANY),
            pl.BlockSpec(memory_space=pl.ANY),
        ]
        + [resident(*context.shape)] * outs
        + [pl.BlockSpec(memory_space=pl.ANY)] * (more is not None),
        out_specs=[resident(SEQ, 3 * PAIR), resident(lines, width)],
        out_shape=[shape(SEQ, 3 * PAIR), shape(lines, width)],
        scratch=[
            pltpu.VMEM((SEQ, PAIR), F32),
            pltpu.VMEM((SEQ, PAIR), F32),
            pltpu.VMEM((3 * PAIR, SEQ), BF16),
            pltpu.VMEM(normed.shape, BF16),
            pltpu.VMEM(grad.shape if outs else (16, PAIR), BF16),
            pltpu.VMEM((lines, width) if more is not None else (16, PAIR), BF16),
            pltpu.SemaphoreType.DMA((3,)),
        ],
        micros=10,
        name="attend_backward",
    )(
        place,
        qkv,
        qkv,
        qkv,
        grad_context,
        context,
        row_lse,
        bias,
        normed,
        grad,
        *[context] * outs,
        *[more] * (more is not None),
    )


def project_out_kernel(s, x_ref, *refs):
    contexts, weights = refs[:4], refs[4:8]
    gain_ref, bias_ref, middle_ref, n_ref = refs[8:]
    middle = x_ref[...].astype(F32)
    for context_ref, w_ref in zip(contexts, weights):
        middle = middle + mm(context_ref[...], w_ref[...])
    middle_ref[...] = middle
    center, scale = norm_parts(middle)
    n_ref[...] = (center * scale * gain_ref[...] + bias_ref[...]).astype(BF16)


def own_then_far(block, along):
    specs = []
    for which in range(4):
        if along == 0:
            specs.append(pl.BlockSpec(block, lambda i, s, which=which: (s[which], 0)))
        else:
            specs.append(pl.BlockSpec(block, lambda i, s, which=which: (0, s[which])))
    return specs


def project_out(place, hidden_in, contexts, weights, gain, bias):
    rows, width = hidden_in.shape
    return call(
        project_out_kernel,
        grid=(rows // TILE,),
        in_specs=[row_tile(width)]
        + [row_tile(2 * PAIR)] * 4
        + own_then_far((2 * PAIR, width), 0)
        + [resident(1, width)] * 2,
        out_specs=[row_tile(width), row_tile(width)],
        out_shape=[shape(rows, width, F32), shape(rows, width)],
        micros=7,
        name="project_out",
    )(place, hidden_in, *contexts, *weights, gain, bias)


def gelu_and_slope(pre):
    root, cubic = 0.7978845608028654, 0.044715
    square = pre * pre
    bent = jnp.tanh(root * (pre + cubic * pre * square))
    half = 0.5 * pre
    slope = 0.5 * (1.0 + bent) + half * (1.0 - bent * bent) * (root * (1.0 + 3.0 * cubic * square))
    return half + half * bent, slope


def feed_forward_kernel(tiles, s, n_ref, g_ref, bias_ref, *refs):
    *ups, down_ref, h_ref, gu_ref, sum_ref = refs

    def run(up_ref):
        pre = mm(n_ref[...], up_ref[...]) + bias_ref[...]
        grad_hidden = mm(g_ref[...], down_ref[...], NT)
        value, slope = gelu_and_slope(pre)
        h_ref[...] = value.astype(BF16)
        grad_up = (grad_hidden * slope).astype(BF16)
        gu_ref[...] = grad_up
        sum_ref[...] = jnp.sum(grad_up.astype(F32), axis=0, keepdims=True)

    if len(ups) == 1:
        run(ups[0])
    else:
        mine = pl.program_id(0) // (tiles // 2) == s[4]

        @pl.when(mine)
        def _():
            run(ups[0])

        @pl.when(jnp.logical_not(mine))
        def _():
            run(ups[1])


def wide_tile(height):
    return pl.BlockSpec((height, WIDE), lambda i, s: (0, i))


def feed_forward(place, which, normed, out_grad, w_up, b_up, w_down):
    rows, width = normed.shape
    units = b_up.shape[1] // 2
    tiles = units // WIDE
    if which < 2:
        columns = [lambda i, s: (0, s[which] * tiles + i)]
    else:
        columns = [lambda i, s: (0, i % (tiles // 2))] * 2
    return call(
        lambda *refs: feed_forward_kernel(tiles, *refs),
        grid=(tiles,),
        in_specs=[
            resident(rows, width),
            resident(rows, width),
            pl.BlockSpec((1, WIDE), lambda i, s: (0, s[which % 2] * tiles + i)),
        ]
        + [pl.BlockSpec((width, WIDE), column) for column in columns]
        + [pl.BlockSpec((WIDE, width), lambda i, s: (s[which] * tiles + i, 0))],
        out_specs=[wide_tile(rows), wide_tile(rows), wide_tile(1)],
        out_shape=[shape(rows, units), shape(rows, units), shape(1, units, F32)],
        micros=12,
        name="feed_forward",
    )(place, normed, out_grad, b_up, *w_up, w_down)


def unit_blocks(units, width, halved, along):
    half = units // 2
    rows = [pl.BlockSpec((TILE, units), lambda i, s: (i, 0))] * 2
    if halved:
        rows += [
            pl.BlockSpec((TILE, half), lambda i, s: (i, s[4])),
            pl.BlockSpec((TILE, half), lambda i, s: (i, 1 - s[4])),
        ] * 2
    else:
        rows += rows
    far = half if halved else units
    count = 4 if halved else 2
    if along == 0:
        own = [
            pl.BlockSpec((units, width), lambda i, s, which=which: (s[which], 0)) for which in (0, 1)
        ]
        return rows + own + [resident(far, width)] * count
    own = [pl.BlockSpec((width, units), lambda i, s, which=which: (0, s[which])) for which in (0, 1)]
    return rows + own + [resident(width, far)] * count


def unit_arrays(slices, weights):
    arrays = [each for each, group in zip(slices, weights) for _ in group]
    return arrays + [part for group in weights for part in group]


def middle_back_kernel(s, g_ref, middle_ref, gain_ref, *refs):
    grads, weights, outs = refs[:6], refs[6:12], refs[12:16]
    gm_ref, ga_ref, gain_sum, bias_sum, *context_grads = refs[16:]
    total = mm(grads[0][...], weights[0][...], NT)
    for grad_ref, w_ref in zip(grads[1:], weights[1:]):
        total = total + mm(grad_ref[...], w_ref[...], NT)
    grad_in, gain, bias = norm_backward(middle_ref[...], gain_ref[...], total)
    grad_middle = g_ref[...].astype(F32) + grad_in
    gm_ref[...] = grad_middle
    ga_ref[...] = grad_middle.astype(BF16)
    accumulate(gain_sum, gain)
    accumulate(bias_sum, bias)
    for w_ref, out_ref in zip(outs, context_grads):
        out_ref[...] = mm(ga_ref[...], w_ref[...], NT).astype(BF16)


def middle_back(place, out_grad, middle, gain, grad_up, weights, out_weights):
    rows, width = middle.shape
    units = grad_up[0].shape[1]
    return call(
        middle_back_kernel,
        grid=(rows // TILE,),
        in_specs=[row_tile(width), row_tile(width), resident(1, width)]
        + unit_blocks(units, width, True, 1)
        + own_then_far((2 * PAIR, width), 0),
        out_specs=[row_tile(width), row_tile(width)]
        + [resident(1, width)] * 2
        + [row_tile(2 * PAIR)] * 4,
        out_shape=[shape(rows, width, F32), shape(rows, width)]
        + [shape(1, width, F32)] * 2
        + [shape(rows, 2 * PAIR)] * 4,
        micros=18,
        name="middle_back",
    )(place, out_grad, middle, gain, *unit_arrays(grad_up, weights), *out_weights)


def input_back_kernel(s, x_ref, gm_ref, gain_ref, *refs):
    grads, weights = refs[:8], refs[8:12]
    out_ref, gain_sum, bias_sum = refs[12:]
    total = None
    for group in range(4):
        pair_0, pair_1 = grads[2 * group][...], grads[2 * group + 1][...]
        joined = jnp.concatenate(
            [
                pair[:, part * PAIR : (part + 1) * PAIR]
                for part in range(3)
                for pair in (pair_0, pair_1)
            ],
            axis=1,
        )
        product = mm(joined, weights[group][...], NT)
        total = product if total is None else total + product
    grad_in, gain, bias = norm_backward(x_ref[...].astype(F32), gain_ref[...], total)
    out_ref[...] = gm_ref[...] + grad_in
    accumulate(gain_sum, gain)
    accumulate(bias_sum, bias)


def input_back(place, hidden_in, grad_middle, gain, grads, weights):
    rows, width = hidden_in.shape
    return call(
        input_back_kernel,
        grid=(rows // TILE,),
        in_specs=[row_tile(width), row_tile(width), resident(1, width)]
        + [row_tile(3 * PAIR)] * 8
        + [resident(width, 6 * PAIR)] * 4,
        out_specs=[row_tile(width)] + [resident(1, width)] * 2,
        out_shape=[shape(rows, width, F32)] + [shape(1, width, F32)] * 2,
        micros=15,
        name="input_back",
    )(place, hidden_in, grad_middle, gain, *grads, *weights)


def project_down_kernel(s, middle_ref, bias_ref, *refs):
    hidden, weights, out_ref = refs[:4], refs[4:8], refs[8]
    total = middle_ref[...] + bias_ref[...]
    for h_ref, w_ref in zip(hidden, weights):
        total = total + mm(h_ref[...], w_ref[...])
    out_ref[...] = total.astype(BF16)


def project_down(place, middle, bias, hidden, weights):
    rows, width = middle.shape
    units = hidden[0].shape[1]
    return call(
        project_down_kernel,
        grid=(rows // TILE,),
        in_specs=[row_tile(width), resident(1, width)] + unit_blocks(units, width, False, 0),
        out_specs=row_tile(width),
        out_shape=shape(rows, width),
        micros=15,
        name="project_down",
    )(place, middle, bias, *unit_arrays(hidden, weights))


def block_bias(rand_blocks):
    blocks = SEQ // BLOCK
    row_ids = jnp.arange(blocks)[:, None]
    col_ids = jnp.arange(blocks)[None, :]
    window = (
        (jnp.abs(row_ids - col_ids) <= 1)
        | (col_ids == 0)
        | (col_ids == blocks - 1)
        | (row_ids == 0)
        | (row_ids == blocks - 1)
    )
    picked = jnp.any(rand_blocks[:, :, :, None] == col_ids[None, :, None, :], axis=2)
    return jnp.where(window[None] | picked, 0.0, -1e30).astype(BF16)


def swap(array, axis, bit):
    size = lax.axis_size(axis)
    return lax.ppermute(array, axis, [(place, place ^ bit) for place in range(size)])


def add_up(*terms):
    total = terms[0].astype(F32)
    for term in terms[1:]:
        total = total + term.astype(F32)
    return total.astype(terms[0].dtype)


def tied(*values):
    return lax.optimization_barrier(values)


class Sum:
    def __init__(self, steps):
        self.steps = list(steps)
        self.paired = self.steps[0] != "mp"
        self.state, self.sending, self.moving = None, [], []

    def parts_of(self, terms):
        if not self.steps:
            self.state, self.sending = add_up(*terms), []
        elif self.steps[0] == "mp":
            near, far = zip(*terms)
            self.state, self.sending = add_up(*near), [add_up(*far)]
        else:
            bits = self.steps[0]
            partners = [0]
            for bit in bits:
                partners += [bit | other for other in partners]
            self.partners = partners[1:]
            rows = terms[0][0].shape[0] if isinstance(terms[0], tuple) else terms[0].shape[0]
            rows //= len(partners)
            index = lax.axis_index("dp") // bits[0] % len(partners)

            def cut(term, other):
                start = (index ^ (other // bits[0])) * rows
                return lax.dynamic_slice_in_dim(term, start, rows, 0)

            def summed(other):
                if isinstance(terms[0], tuple):
                    return jnp.concatenate(
                        [add_up(*[cut(term, other) for term in half]) for half in zip(*terms)]
                    )
                return add_up(*[cut(term, other) for term in terms])

            self.state = summed(0)
            self.sending = [summed(other) for other in self.partners]

    def go(self):
        step = self.steps.pop(0)
        if step == "mp":
            self.moving = [swap(part, "mp", 1) for part in self.sending]
        else:
            self.moving = [swap(part, "dp", way) for part, way in zip(self.sending, self.partners)]

    def take(self):
        terms = [self.state] + self.moving
        if self.paired and self.steps[0] == "mp":
            self.paired = False
            rows = terms[0].shape[0] // 2
            terms = [(term[:rows], term[rows:]) for term in terms]
        self.parts_of(terms)


class Tied(dict):
    def tie(self, *names):
        for name, value in zip(names, tied(*[self[name] for name in names])):
            self[name] = value
        return self[names[0]]

    def turn(self, *names, sums=()):
        counts = [len(each.moving) for each in sums]
        flat = [part for each in sums for part in each.moving]
        kept = list(tied(*[self[name] for name in names], *flat))
        for name in names:
            self[name] = kept.pop(0)
        for each, count in zip(sums, counts):
            each.moving = [kept.pop(0) for _ in range(count)]
            if count:
                each.take()
        flat = [self[name] for name in names]
        for each in sums:
            flat += [each.state] + each.sending
        kept = list(tied(*flat))
        for name in names:
            self[name] = kept.pop(0)
        for each in sums:
            each.state = kept.pop(0)
            each.sending = [kept.pop(0) for _ in each.sending]
            each.moving = []
            if each.steps:
                each.go()


class Gather:
    def __init__(self, state, steps):
        self.state, self.steps, self.sending, self.moving = state, list(steps), [], []

    def go(self):
        bits = self.steps.pop(0)
        partners = [0]
        for bit in bits:
            partners += [bit | other for other in partners]
        self.moving = [swap(self.state, "dp", way) for way in partners[1:]]

    def take(self):
        self.state = jnp.concatenate([self.state] + self.moving)


class Butterfly:
    def __init__(self, state, steps):
        self.state, self.steps, self.sending, self.moving = state, list(steps), [], []

    def go(self):
        self.moving = [swap(self.state, *self.steps.pop(0))]

    def take(self):
        self.state = self.state + self.moving[0]


def spread_kernel(s, *refs):
    *parts, out_ref = refs
    height = parts[0].shape[0]
    for index, part in enumerate(parts):
        out_ref[index * height : (index + 1) * height, :] = part[...].astype(F32)


def spread(place, gathered, sources, target, rows, columns):
    width = gathered.shape[1]
    height = rows * columns // width // 4 // len(sources)
    return call(
        spread_kernel,
        grid=(2, 2),
        in_specs=[
            pl.BlockSpec((height, width), lambda c, y, s, source=source: (source(c, y), 0))
            for source in sources
        ],
        out_specs=pl.BlockSpec((height * len(sources), width), lambda c, y, s: target(c, y)),
        out_shape=shape(rows, columns, F32),
        micros=4,
        name="spread",
    )(place, *[gathered] * len(sources))


def spread_joined_kernel(s, one_a, one_b, two_a, two_b, q_ref, k_ref, v_ref, o_ref, flat):
    mine = pl.program_id(0) == s[0]
    first = 0
    for part_a, part_b in ((one_a, one_b), (two_a, two_b)):
        height = part_a.shape[0] // 8
        for y in range(2):
            for z in range(4):
                start = first + (y * 4 + z) * height
                source = ((y ^ s[4]) * 4 + (z ^ s[5])) * height
                lines = pl.ds(pl.multiple_of(source, height), height)
                flat[start : start + height, :] = jnp.where(mine, part_a[lines, :], part_b[lines, :])
        first += 8 * height
    second = one_a.shape[0]
    for part, ref in enumerate((q_ref, k_ref, v_ref)):
        for pair, first in enumerate((0, second)):
            lines = slice(first + part * PAIR, first + (part + 1) * PAIR)
            ref[:, pair * PAIR : (pair + 1) * PAIR] = flat[lines, :].astype(F32).T
    o_ref[...] = flat[3 * PAIR : second, :].astype(F32)


def spread_joined(place, one, two):
    width = one[0].shape[1]
    columns = pl.BlockSpec((width, 2 * PAIR), lambda c, s: (0, c))
    return call(
        spread_joined_kernel,
        grid=(2,),
        in_specs=[resident(*each.shape) for each in (*one, *two)],
        out_specs=[columns] * 3 + [pl.BlockSpec((2 * PAIR, width), lambda c, s: (c, 0))],
        out_shape=[shape(width, 4 * PAIR, F32)] * 3 + [shape(4 * PAIR, width, F32)],
        scratch=[pltpu.VMEM((one[0].shape[0] + two[0].shape[0], width), BF16)],
        micros=4,
        name="spread_joined",
    )(place, *one, *two)


class At:
    (
        out_piece, up_piece, down_piece, far_ja, n1, qkv, ctx, far_jb,
        far_out_a, far_out_b, up_mine, down_a, middle, n2, g, gu,
        down, up, up_other, up_b0, up_b1, down_b, near_down, near_up,
        far_down, far_up, gm, ga, gc, gj, joined, far_b,
        own_b, down_all, up_all, input_grad, output, grad_down_w, grad_up_w, first,
    ) = range(40)


def whole_sequence(
    hidden_in,
    out_grad,
    ln1_gain,
    ln1_bias,
    w_query,
    w_key,
    w_value,
    w_out,
    ln2_gain,
    ln2_bias,
    w_up,
    b_up,
    w_down,
    b_down,
    rand_blocks,
):
    device = lax.axis_index("dp")
    core, over_y, side = device % 2, (device // 2) % 2, lax.axis_index("mp")
    zero = 0 * core
    place = jnp.stack([core, 1 - core, zero, zero, over_y, device // 4]).astype(jnp.int32)

    def part(array, axis, index, count):
        size = array.shape[axis] // count
        return lax.dynamic_slice_in_dim(array, index * size, size, axis)

    def joined(other):
        return jnp.concatenate(
            [part(each, 1, core ^ other, 2) for each in (w_query, w_key, w_value)], axis=1
        )

    def halves_in_order(mine, other, bit):
        return jnp.where(
            bit == 0,
            jnp.concatenate([mine, other], axis=1),
            jnp.concatenate([other, mine], axis=1),
        )

    def row(vector):
        return vector.reshape(1, -1)

    v = Tied()
    own_ja, own_jb = joined(0), joined(1)
    quarter = 2 * core + over_y
    v[At.out_piece], v[At.up_piece] = part(w_out, 0, core, 2), part(w_up, 1, quarter, 4)
    v[At.down_piece] = part(w_down, 0, core, 2)
    v[At.far_ja] = swap(own_ja, "mp", 1)
    far_rand, far_bup = swap(rand_blocks, "mp", 1), swap(b_up, "mp", 1)
    own_bias, far_bias = block_bias(rand_blocks), block_bias(far_rand)
    bias = [own_bias, own_bias, far_bias, far_bias]
    v[At.n1], bias_down = norm_in(place, hidden_in, out_grad, row(ln1_gain), row(ln1_bias))
    row_lse = [None] * 4

    def attend(g, weights):
        v[At.qkv, g] = mm(v[At.n1], weights).astype(BF16)
        v[At.ctx, g], row_lse[g] = attend_forward(place, g, v[At.qkv, g], bias[g])

    attend(0, own_ja)
    v.tie(At.n1, (At.ctx, 0))
    attend(1, own_jb)
    v.tie(At.n1, At.far_ja, At.out_piece, (At.ctx, 1))
    v[At.far_jb], v[At.far_out_a] = swap(v[At.far_ja], "dp", 1), swap(v[At.out_piece], "mp", 1)
    attend(2, v[At.far_ja])
    v.tie(At.n1, At.far_jb, At.far_out_a, At.up_piece, (At.ctx, 2))
    v[At.far_out_b], v[At.up_mine] = swap(v[At.far_out_a], "dp", 1), swap(v[At.up_piece], "mp", 1)
    attend(3, v[At.far_jb])
    v.tie((At.ctx, 3), At.far_out_b, At.down_piece)
    v[At.down_a] = swap(v[At.down_piece], "mp", 1)
    joined_w = [own_ja, own_jb, v[At.far_ja], v[At.far_jb]]
    out_w = [w_out, w_out, v[At.far_out_a], v[At.far_out_b]]
    v[At.middle], v[At.n2] = project_out(
        place, hidden_in, [v[At.ctx, g] for g in range(4)], out_w, row(ln2_gain), row(ln2_bias)
    )

    hidden, bias_up = [None] * 4, [None] * 4
    up_bias = [row(b_up), row(b_up), row(far_bup), row(far_bup)]
    v[At.g] = out_grad

    def feed(g, up, down):
        hidden[g], v[At.gu, g], bias_up[g] = feed_forward(
            place, g, v[At.n2], v[At.g], up, up_bias[g], down
        )

    def down_grad(g):
        v[At.down, g] = mm(hidden[g], v[At.g], TN).astype(BF16)

    def up_grad(g):
        v[At.up, g] = mm(v[At.n2], v[At.gu, g], TN).astype(BF16)

    v.tie(At.n2, At.up_mine)
    v[At.up_other] = swap(v[At.up_mine], "dp", 2)
    feed(1, (w_up,), w_down)
    v.tie(At.n2, (At.gu, 1))
    feed(0, (w_up,), w_down)
    v.tie(At.g, At.n2, At.up_mine, At.up_other, (At.gu, 0))
    v[At.up_b0], v[At.up_b1] = swap(v[At.up_mine], "dp", 1), swap(v[At.up_other], "dp", 1)
    for g in (1, 0):
        down_grad(g)
        up_grad(g)
    v.tie(At.n2, At.g, At.down_a, At.up_b0, At.up_b1, *[(name, g) for name in (At.down, At.up) for g in (0, 1)])
    v[At.down_b] = swap(v[At.down_a], "dp", 1)
    v[At.near_down], v[At.near_up] = swap(v[At.down, 1], "dp", 1), swap(v[At.up, 1], "dp", 1)
    feed(2, (v[At.up_mine], v[At.up_other]), v[At.down_a])
    v.tie(At.n2, At.g, At.down_b, At.near_down, At.near_up, (At.gu, 2))
    feed(3, (v[At.up_b0], v[At.up_b1]), v[At.down_b])
    up_w = [(w_up,), (w_up,), (v[At.up_mine], v[At.up_other]), (v[At.up_b0], v[At.up_b1])]
    down_w = [(w_down,), (w_down,), (v[At.down_a],), (v[At.down_b],)]
    v.tie(At.g, At.n2, (At.gu, 3))
    down_grad(3)
    v.tie(At.g, At.n2, (At.down, 3))
    v[At.far_down] = swap(v[At.down, 3], "dp", 1)
    up_grad(3)
    v.tie(At.g, At.n2, (At.up, 3))
    v[At.far_up] = swap(v[At.up, 3], "dp", 1)
    down_grad(2)
    down_sum = Sum(["mp", (2,), (4,), (8,)])
    down_sum.parts_of([(v[At.down, 0], v[At.down, 2]), (v[At.near_down], v[At.far_down])])
    v.turn(At.g, At.n2, sums=[down_sum])
    up_grad(2)
    up_sum = Sum([(4,), "mp", (2,), (8,)])
    up_sum.parts_of([(v[At.up, 0], v[At.up, 2]), (v[At.near_up], v[At.far_up])])
    v.turn(At.g, sums=[up_sum])

    v[At.gm], v[At.ga], gain_two, bias_two, *context_grads = middle_back(
        place,
        v[At.g],
        v[At.middle],
        row(ln2_gain),
        [v[At.gu, g] for g in range(4)],
        up_w,
        [w_out, w_out, v[At.far_out_a], v[At.far_out_b]],
    )
    for g in range(4):
        v[At.gc, g] = context_grads[g]
    v.tie(At.ga, *[(At.gc, g) for g in range(4)])

    def attend_back(g, pair, more=None):
        v[At.gj, g, pair], v[At.joined, g, pair] = attend_backward(
            place,
            g,
            pair,
            v[At.qkv, g],
            v[At.gc, g],
            v[At.ctx, g],
            row_lse[g],
            bias[g],
            v[At.n1],
            v[At.ga],
            more,
        )

    first, second = Sum(["mp", (2,), (4, 8)]), Sum(["mp", (2,), (4, 8)])
    for each in (first, second):
        each.steps.pop(0)
    attend_back(3, 0)
    v.tie((At.gc, 1), (At.joined, 3, 0))
    v[At.far_b] = swap(v[At.joined, 3, 0], "dp", 1)
    attend_back(1, 0)
    v.turn((At.gc, 2), (At.joined, 1, 0), At.far_b, sums=[down_sum, up_sum])
    v[At.own_b] = swap(v[At.joined, 1, 0], "dp", 1)
    attend_back(2, 0, v[At.far_b])
    v.tie((At.gc, 0), (At.joined, 2, 0), At.own_b)
    first_mp = swap(v[At.joined, 2, 0], "mp", 1)
    attend_back(0, 0, v[At.own_b])
    v.turn((At.gc, 3), (At.joined, 0, 0), sums=[down_sum, up_sum])
    attend_back(3, 1)
    v.turn((At.gc, 1), (At.joined, 3, 1), sums=[down_sum, up_sum])
    v[At.far_b] = swap(v[At.joined, 3, 1], "dp", 1)
    attend_back(1, 1)
    v.turn((At.gc, 2), (At.joined, 1, 1), At.far_b, sums=[down_sum])
    v[At.own_b] = swap(v[At.joined, 1, 1], "dp", 1)
    v[At.down_all] = lax.all_gather(down_sum.state, "dp", tiled=True)
    attend_back(2, 1, v[At.far_b])
    first.state, first.moving = v[At.joined, 0, 0], [first_mp]
    v.turn((At.gc, 0), (At.joined, 2, 1), At.own_b, sums=[up_sum, first])
    second_mp = swap(v[At.joined, 2, 1], "mp", 1)
    v[At.up_all] = lax.all_gather(up_sum.state, "dp", tiled=True)
    attend_back(0, 1, v[At.own_b])
    second.state, second.moving = v[At.joined, 0, 1], [second_mp]
    v.turn(At.gm, (At.joined, 0, 1), sums=[second, first])
    v[At.input_grad], gain_one, bias_one = input_back(
        place,
        hidden_in,
        v[At.gm],
        row(ln1_gain),
        [v[At.gj, g, pair] for g in range(4) for pair in range(2)],
        joined_w,
    )
    own_up = halves_in_order(bias_up[0], bias_up[1], core)
    far_up = halves_in_order(bias_up[2], bias_up[3], core)
    width = hidden_in.shape[1]
    small = Butterfly(
        jnp.concatenate(
            [gain_one, bias_one, gain_two, bias_two, bias_down]
            + [halves_in_order(own_up, far_up, side).reshape(-1, width)]
        ),
        [("dp", 1), ("mp", 1), ("dp", 2), ("dp", 4), ("dp", 8)],
    )
    v.turn(At.middle, At.input_grad, sums=[second, first, small])
    first = Gather(first.state, [(4, 8), (2,), (1,)])
    v.turn(At.middle, sums=[first])
    v[At.output] = project_down(place, v[At.middle], row(b_down), hidden, down_w)
    v.turn(At.output, sums=[second, first, small])
    second = Gather(second.state, [(4, 8), (2,), (1,)])
    v.turn(At.output, sums=[second])
    v.tie(At.down_all, At.output)
    v[At.grad_down_w] = spread(
        place,
        v[At.down_all],
        [lambda c, y, z=z, x=x: (x * 2 + z) * 4 + y * 2 + c for z in range(2) for x in range(2)],
        lambda c, y: (c * 2 + y, 0),
        *w_down.shape,
    )
    v.turn(At.grad_down_w, At.up_all, sums=[second, first, small])
    v[At.grad_up_w] = spread(
        place,
        v[At.up_all],
        [lambda c, z, y=y, x=x: (x * 2 + z) * 4 + y * 2 + c for y in range(2) for x in range(2)],
        lambda c, z: (z, c),
        *w_up.shape,
    )
    v[At.first] = first.moving[0]
    v.turn(At.grad_up_w, At.first, sums=[second, small])
    grad_q, grad_k, grad_v, grad_out_w = spread_joined(
        place, (first.state, v[At.first]), (second.state, second.moving[0])
    )
    small.take()
    if small.steps:
        small.go()
        small.take()
    sums = small.state
    up_rows = b_up.shape[0] // width
    bias_up_sum = lax.dynamic_slice_in_dim(sums, 5 + side * up_rows, up_rows).reshape(-1)
    return (
        v[At.output],
        v[At.input_grad],
        sums[0],
        sums[1],
        grad_q,
        grad_k,
        grad_v,
        grad_out_w,
        sums[2],
        sums[3],
        v[At.grad_up_w],
        bias_up_sum,
        v[At.grad_down_w],
        sums[4],
    )


def solution(mesh):
    in_specs = (
        P(("dp", "mp"), None),
        P(("dp", "mp"), None),
        P(),
        P(),
        P(None, "mp"),
        P(None, "mp"),
        P(None, "mp"),
        P("mp", None),
        P(),
        P(),
        P(None, "mp"),
        P("mp"),
        P("mp", None),
        P(),
        P("mp", None, None),
    )
    out_specs = (
        P(("dp", "mp"), None),
        P(("dp", "mp"), None),
        P(),
        P(),
        P(None, "mp"),
        P(None, "mp"),
        P(None, "mp"),
        P("mp", None),
        P(),
        P(),
        P(None, "mp"),
        P("mp"),
        P("mp", None),
        P(),
    )
    def per_device(hidden_in, *others):
        w_query, w_up, rand_blocks = others[3], others[9], others[13]
        whole = hidden_in.shape[0] == SEQ and mesh.shape["mp"] == 2
        halved = mesh.shape["dp"] == 16 and rand_blocks.shape[0] == 8
        sized = w_query.shape == (1024, 512) and w_up.shape == (1024, 2048)
        layer = whole_sequence if whole and halved and sized else split_sequence
        return layer(hidden_in, *others)

    return jax.shard_map(
        per_device, mesh=mesh, in_specs=in_specs, out_specs=out_specs, check_vma=False
    )
```

time: 630 us -> 511 us (0.81)
  other arithmetic: 76.2 us -> 30.3 us
  local copies, waits for them, and re-layouts: 54.2 us -> 20.4 us
  waiting for transfers between devices: 116 us -> 83.7 us
  matrix products: 76.3 us -> 48.2 us
  between operations: 2.45 us -> 15.4 us
    ppermute x59 -> x53, waiting for transfers between devices: 116 us -> 83.7 us  [swap(): lax.ppermute(array, axis, [(place, place ^ bit) for place in range(size)])]
    pallas_call x8 -> x11, Pallas kernels: 71.7 us -> 102 us  [the longest x8 82.3 us: attend_backward(): call(lambda *refs: attend_backward_kernel(outs, *refs), grid=(1,), in_spe...]
    dot_general x28 -> x12, matrix products: 76.3 us -> 48.2 us  [mm(): return lax.dot_general(left, right, dims, preferred_element_type=F32)]
    pallas_call x4, Pallas kernels: 56.2 us -> 35.7 us  [attend_forward(): call(attend_forward_kernel, grid=(pairs,), in_specs=[thin_block(lambda p:...]
    another operation x13 -> x0, other arithmetic: 19.2 us -> none  [the longest x12 18.5 us: collect(): jnp.stack([add_up(own_a, self.moving[0]), add_up(far_a, self.moving[1])])]
    unnamed x201 -> x121, local copies, waits for them, and re-layouts: 27.1 us -> 8.7 us
    select_n x16 -> x3, other arithmetic: 14.7 us -> 0.07 us  [halves_in_order(): jnp.where(bit == 0, jnp.concatenate([mine, other], axis=1), jnp.concatena...]
    convert_element_type x4 -> x1, other arithmetic: 9.14 us -> 0.65 us  [block_bias(): return jnp.where(window[None] | picked, 0.0, -1e+30).astype(BF16)]
  transfers between devices with their start and end apart: 59 -> 55, of which waited for: 18 -> 19; matrix products, arithmetic and copies ran while one was open for 24% -> 14% of each run, Pallas kernels for 36% -> 46%
where the time goes in v3:
time: 511 us; the launch traced here: 501 us
  Pallas kernels  249 us (49%)
  waiting for transfers between devices  83.7 us (16%)
  starting transfers between devices  53.6 us (10%)
  matrix products  48.2 us (9%)
  other arithmetic  30.3 us (6%)
  local copies, waits for them, and re-layouts  20.4 us (4%)
  between operations  15.4 us (3%)
    ppermute x53, waiting for transfers between devices, swap(): lax.ppermute(array, axis, [(place, place ^ bit) for place in range(size)])  83.7 us
    pallas_call x8, Pallas kernels, attend_backward(): call(lambda *refs: attend_backward_kernel(outs, *refs), grid=(1,), in_spe...  82.3 us
    ppermute x53, starting transfers between devices, swap(): lax.ppermute(array, axis, [(place, place ^ bit) for place in range(size)])  53.5 us
    dot_general x12, matrix products, mm(): return lax.dot_general(left, right, dims, preferred_element_type=F32)  48.2 us
    pallas_call x4, Pallas kernels, feed_forward(): call(lambda *refs: feed_forward_kernel(tiles, *refs), grid=(tiles,), in_s...  44.8 us
    pallas_call x4, Pallas kernels, attend_forward(): call(attend_forward_kernel, grid=(pairs,), in_specs=[thin_block(lambda p:...  35.7 us
    convert_element_type x17, other arithmetic, add_up(): return total.astype(terms[0].dtype)  24.5 us
    pallas_call x1, Pallas kernels, middle_back(): call(middle_back_kernel, grid=(rows // TILE,), in_specs=[row_tile(width),...  21.5 us
  transfers between devices with their start and end apart: 55, of which 19 were waited for; matrix products, arithmetic and copies ran while one was open for 14% of the time, Pallas kernels for 46%

profile of v3, /device:TPU:0, one launch (start us, length us, event | category | flops | bytes accessed | tf_op | source)
XLA Modules:
  0.0 500.6 jit_solution(15904725414694178991)
XLA Ops:
  15.7 5.9 %norm_in.1 = (bf16[1024,1024]{1,0:T(8,128)(2,1)}, f32[1,1024]{1,0:T(1,128)}) custom-call(s32[6]{0:T(128)} %stack.19.s.refs_0_, bf16[1024,1024]{1,0:T(8,128)(2,1)} %x_ref.5, bf16[1024,1024]{1,0:T(8,128)(2,1)} %g_ref.2, f32[1,1024]{1,0:T(1,128)} %bitcast.49, f32[1,1024]{1,0:T(1,128)} %bitcast.59), custom_call_target="tpu_custom_call" | custom-call | flops 100000000 | tf_op jit(solution)/shard_map/norm_in/pallas_call | solution.py:309
  22.4 4.5 convolution_convert_fusion.10.q_ref.k_ref.v_ref.refs_1_.refs_2_.refs_3_
  27.9 9.1 %attend_forward.4 = (bf16[1024,256]{1,0:T(8,128)(2,1)}, f32[2,2,1024]{2,1,0:T(2,128)}) custom-call(s32[6]{0:T(128)} %stack.19.s.refs_0_, bf16[1024,768]{1,0:T(8,128)(2,1)} %convolution_convert_fusion.10.q_ref.k_ref.v_ref.refs_1_.refs_2_.refs_3_, bf16[1024,768]{1,0:T(8,128)(2,1)} %convolution_convert_fusion.10.q_ref.k_ref.v_ref.refs_1_.refs_2_.refs_3_, ...), custom_call_target="tpu_custom_call" | custom-call | flops 240000000 | tf_op jit(solution)/shard_map/attend_forward/pallas_call | solution.py:373
  40.0 8.9 %attend_forward.5 = (bf16[1024,256]{1,0:T(8,128)(2,1)}, f32[2,2,1024]{2,1,0:T(2,128)}) custom-call(s32[6]{0:T(128)} %stack.19.s.refs_0_, bf16[1024,768]{1,0:T(8,128)(2,1)} %convolution_convert_fusion.9.q_ref.k_ref.v_ref.refs_1_.refs_2_.refs_3_, bf16[1024,768]{1,0:T(8,128)(2,1)} %convolution_convert_fusion.9.q_ref.k_ref.v_ref.refs_1_.refs_2_.refs_3_, ...), custom_call_target="tpu_custom_call" | custom-call | flops 240000000 | tf_op jit(solution)/shard_map/attend_forward/pallas_call | solution.py:373
  53.6 4.4 convolution_convert_fusion.8.q_ref.k_ref.v_ref.refs_1_.refs_2_.refs_3_
  58.0 8.9 %attend_forward.6 = (bf16[1024,256]{1,0:T(8,128)(2,1)}, f32[2,2,1024]{2,1,0:T(2,128)}) custom-call(s32[6]{0:T(128)} %stack.19.s.refs_0_, bf16[1024,768]{1,0:T(8,128)(2,1)} %convolution_convert_fusion.8.q_ref.k_ref.v_ref.refs_1_.refs_2_.refs_3_, bf16[1024,768]{1,0:T(8,128)(2,1)} %convolution_convert_fusion.8.q_ref.k_ref.v_ref.refs_1_.refs_2_.refs_3_, ...), custom_call_target="tpu_custom_call" | custom-call | flops 240000000 | tf_op jit(solution)/shard_map/attend_forward/pallas_call | solution.py:373
  71.8 4.3 convolution_convert_fusion.7.q_ref.k_ref.v_ref.refs_1_.refs_2_.refs_3_
  76.1 8.8 %attend_forward.7 = (bf16[1024,256]{1,0:T(8,128)(2,1)}, f32[2,2,1024]{2,1,0:T(2,128)}) custom-call(s32[6]{0:T(128)} %stack.19.s.refs_0_, bf16[1024,768]{1,0:T(8,128)(2,1)} %convolution_convert_fusion.7.q_ref.k_ref.v_ref.refs_1_.refs_2_.refs_3_, bf16[1024,768]{1,0:T(8,128)(2,1)} %convolution_convert_fusion.7.q_ref.k_ref.v_ref.refs_1_.refs_2_.refs_3_, ...), custom_call_target="tpu_custom_call" | custom-call | flops 240000000 | tf_op jit(solution)/shard_map/attend_forward/pallas_call | solution.py:373
  85.7 8.1 %project_out.1 = (f32[1024,1024]{1,0:T(8,128)}, bf16[1024,1024]{1,0:T(8,128)(2,1)}) custom-call(s32[6]{0:T(128)} %stack.19.s.refs_0_, bf16[1024,1024]{1,0:T(8,128)(2,1)} %x_ref.5, bf16[1024,256]{1,0:T(8,128)(2,1)} %get-tuple-element.250.refs_0_.refs_5_.refs_10_, bf16[1024,256]{1,0:T(8,128)(2,1)} %get-tuple-element.253.refs_1_.refs_5_.refs_10_, ...), custom_call_target="tpu_custom_call" | custom-call | flops 140000000 | tf_op jit(solution)/shard_map/project_out/pallas_call | solution.py:541
  96.0 10.9 %feed_forward.4 = (bf16[1024,1024]{1,0:T(8,128)(2,1)}, bf16[1024,1024]{1,0:T(8,128)(2,1)}, f32[1,1024]{1,0:T(1,128)}) custom-call(s32[6]{0:T(128)} %stack.19.s.refs_0_, bf16[1024,1024]{1,0:T(8,128)(2,1)} %get-tuple-element.310.refs_1_, bf16[1024,1024]{1,0:T(8,128)(2,1)} %g_ref.2, f32[1,2048]{1,0:T(1,128)} %bitcast.45, bf16[1024,2048]{1,0:T(8,128)(2,1)} %refs_7_.1, ...), custom_call_target="tpu_custom_call" | custom-call | flops 240000000 | tf_op jit(solution)/shard_map/feed_forward/pallas_call | solution.py:602
  106.8 11.5 %feed_forward.5 = (bf16[1024,1024]{1,0:T(8,128)(2,1)}, bf16[1024,1024]{1,0:T(8,128)(2,1)}, f32[1,1024]{1,0:T(1,128)}) custom-call(s32[6]{0:T(128)} %stack.19.s.refs_0_, bf16[1024,1024]{1,0:T(8,128)(2,1)} %get-tuple-element.310.refs_1_, bf16[1024,1024]{1,0:T(8,128)(2,1)} %g_ref.2, f32[1,2048]{1,0:T(1,128)} %bitcast.46, bf16[1024,2048]{1,0:T(8,128)(2,1)} %refs_7_.1, ...), custom_call_target="tpu_custom_call" | custom-call | flops 240000000 | tf_op jit(solution)/shard_map/feed_forward/pallas_call | solution.py:602
  120.1 3.7 convolution_convert_fusion.3
  123.8 3.7 convolution_convert_fusion.4
  127.5 3.7 convolution_convert_fusion.5
  131.3 3.7 convolution_convert_fusion.6
  135.0 8.4 %collective-permute-done.7.refs_6_ = bf16[1024,1024]{1,0:T(8,128)(2,1)S(1)} collective-permute-done((bf16[1024,1024]{1,0:T(8,128)(2,1)}, bf16[1024,1024]{1,0:T(8,128)(2,1)S(1)}, u32[]{:S(2)}, u32[]{:S(2)}) %collective-permute-start.7) | collective-permute-done | bytes 2097184 | tf_op jit(solution)/shard_map/ppermute | solution.py:757
  150.2 11.0 %feed_forward.6 = (bf16[1024,1024]{1,0:T(8,128)(2,1)}, bf16[1024,1024]{1,0:T(8,128)(2,1)}, f32[1,1024]{1,0:T(1,128)}) custom-call(s32[6]{0:T(128)} %stack.19.s.refs_0_, bf16[1024,1024]{1,0:T(8,128)(2,1)} %get-tuple-element.310.refs_1_, bf16[1024,1024]{1,0:T(8,128)(2,1)} %g_ref.2, f32[1,2048]{1,0:T(1,128)} %bitcast.43, bf16[1024,512]{1,0:T(8,128)(2,1)} %copy-done.13, ...), custom_call_target="tpu_custom_call" | custom-call | flops 240000000 | tf_op jit(solution)/shard_map/feed_forward/pallas_call | solution.py:602
  163.2 11.4 %feed_forward.7 = (bf16[1024,1024]{1,0:T(8,128)(2,1)}, bf16[1024,1024]{1,0:T(8,128)(2,1)}, f32[1,1024]{1,0:T(1,128)}) custom-call(s32[6]{0:T(128)} %stack.19.s.refs_0_, bf16[1024,1024]{1,0:T(8,128)(2,1)} %get-tuple-element.310.refs_1_, bf16[1024,1024]{1,0:T(8,128)(2,1)} %g_ref.2, f32[1,2048]{1,0:T(1,128)} %bitcast.44, bf16[1024,512]{1,0:T(8,128)(2,1)} %copy-done.14, ...), custom_call_target="tpu_custom_call" | custom-call | flops 240000000 | tf_op jit(solution)/shard_map/feed_forward/pallas_call | solution.py:602
  174.6 5.4 %convolution_convert_fusion.2 = bf16[1024,1024]{1,0:T(8,128)(2,1)} fusion(bf16[1024,1024]{1,0:T(8,128)(2,1)} %get-tuple-element.295.refs_3_, bf16[1024,1024]{1,0:T(8,128)(2,1)S(1)} %copy-done.2), kind=kOutput, calls=%fused_computation.14 | convolution fusion | flops 2148532224 | bytes 6291456 | tf_op jit(solution)/shard_map/dot_general | solution.py:229
  180.0 3.8 convolution_convert_fusion.1
  184.3 3.3 add_convert_fusion.7
  190.1 5.5 %add_convert_fusion = bf16[1024,1024]{1,0:T(8,128)(2,1)} fusion(bf16[1024,1024]{1,0:T(8,128)(2,1)} %collective-permute-done.14, bf16[1024,1024]{1,0:T(8,128)(2,1)S(1)} %copy-done.20, bf16[1024,1024]{1,0:T(8,128)(2,1)S(1)} %copy-done.2), kind=kOutput, calls=%fused_computation | convolution fusion | flops 2152726528 | bytes 8388608 | tf_op jit(solution)/shard_map/dot_general | solution.py:229
  204.8 21.5 %middle_back.1 = (f32[1024,1024]{1,0:T(8,128)}, bf16[1024,1024]{1,0:T(8,128)(2,1)}, f32[1,1024]{1,0:T(1,128)}, f32[1,1024]{1,0:T(1,128)}, bf16[1024,256]{1,0:T(8...) custom-call(s32[6]{0:T(128)} %stack.19.s.refs_0_, ...), custom_call_target="tpu_custom_call" | custom-call | flops 360000000 | tf_op jit(solution)/shard_map/middle_back/pallas_call | solution.py:664
  226.3 10.6 %attend_backward.8 = (bf16[1024,384]{1,0:T(8,128)(2,1)}, bf16[640,1024]{1,0:T(8,128)(2,1)}) custom-call(s32[6]{0:T(128)} %stack.19.s.refs_0_, bf16[1024,768]{1,0:T(8,128)(2,1)} %convolution_convert_fusion.7.q_ref.k_ref.v_ref.refs_1_.refs_2_.refs_3_, bf16[1024,768]{1,0:T(8,128)(2,1)} %convolution_convert_fusion.7.q_ref.k_ref.v_ref.refs_1_.refs_2_.refs_3_, ...), custom_call_target="tpu_custom_call" | custom-call | flops 200000000 | tf_op jit(solution)/shard_map/attend_backward/pallas_call | solution.py:473
  237.0 10.9 %attend_backward.9 = (bf16[1024,384]{1,0:T(8,128)(2,1)}, bf16[640,1024]{1,0:T(8,128)(2,1)}) custom-call(s32[6]{0:T(128)} %stack.19.s.refs_0_, bf16[1024,768]{1,0:T(8,128)(2,1)} %convolution_convert_fusion.9.q_ref.k_ref.v_ref.refs_1_.refs_2_.refs_3_, bf16[1024,768]{1,0:T(8,128)(2,1)} %convolution_convert_fusion.9.q_ref.k_ref.v_ref.refs_1_.refs_2_.refs_3_, ...), custom_call_target="tpu_custom_call" | custom-call | flops 200000000 | tf_op jit(solution)/shard_map/attend_backward/pallas_call | solution.py:473
  251.8 3.6 add_convert_fusion.2
  255.5 3.5 add_convert_fusion.4
  260.0 10.6 %attend_backward.10 = (bf16[1024,384]{1,0:T(8,128)(2,1)}, bf16[640,1024]{1,0:T(8,128)(2,1)}) custom-call(s32[6]{0:T(128)} %stack.19.s.refs_0_, bf16[1024,768]{1,0:T(8,128)(2,1)} %convolution_convert_fusion.8.q_ref.k_ref.v_ref.refs_1_.refs_2_.refs_3_, bf16[1024,768]{1,0:T(8,128)(2,1)} %convolution_convert_fusion.8.q_ref.k_ref.v_ref.refs_1_.refs_2_.refs_3_, ...), custom_call_target="tpu_custom_call" | custom-call | flops 200000000 | tf_op jit(solution)/shard_map/attend_backward/pallas_call | solution.py:473
  270.6 10.7 %attend_backward.11 = (bf16[1024,384]{1,0:T(8,128)(2,1)}, bf16[640,1024]{1,0:T(8,128)(2,1)}) custom-call(s32[6]{0:T(128)} %stack.19.s.refs_0_, bf16[1024,768]{1,0:T(8,128)(2,1)} %convolution_convert_fusion.10.q_ref.k_ref.v_ref.refs_1_.refs_2_.refs_3_, bf16[1024,768]{1,0:T(8,128)(2,1)} %convolution_convert_fusion.10.q_ref.k_ref.v_ref.refs_1_.refs_2_.refs_3_, ...), custom_call_target="tpu_custom_call" | custom-call | flops 200000000 | tf_op jit(solution)/shard_map/attend_backward/pallas_call | solution.py:473
  281.3 3.4 collective-permute-done.20
  290.0 9.7 %attend_backward.12 = (bf16[1024,384]{1,0:T(8,128)(2,1)}, bf16[384,1024]{1,0:T(8,128)(2,1)}) custom-call(s32[6]{0:T(128)} %stack.19.s.refs_0_, bf16[1024,768]{1,0:T(8,128)(2,1)} %convolution_convert_fusion.7.q_ref.k_ref.v_ref.refs_1_.refs_2_.refs_3_, bf16[1024,768]{1,0:T(8,128)(2,1)} %convolution_convert_fusion.7.q_ref.k_ref.v_ref.refs_1_.refs_2_.refs_3_, ...), custom_call_target="tpu_custom_call" | custom-call | flops 200000000 | tf_op jit(solution)/shard_map/attend_backward/pallas_call | solution.py:473
  306.7 9.9 %attend_backward.13 = (bf16[1024,384]{1,0:T(8,128)(2,1)}, bf16[384,1024]{1,0:T(8,128)(2,1)}) custom-call(s32[6]{0:T(128)} %stack.19.s.refs_0_, bf16[1024,768]{1,0:T(8,128)(2,1)} %convolution_convert_fusion.9.q_ref.k_ref.v_ref.refs_1_.refs_2_.refs_3_, bf16[1024,768]{1,0:T(8,128)(2,1)} %convolution_convert_fusion.9.q_ref.k_ref.v_ref.refs_1_.refs_2_.refs_3_, ...), custom_call_target="tpu_custom_call" | custom-call | flops 200000000 | tf_op jit(solution)/shard_map/attend_backward/pallas_call | solution.py:473
  320.9 9.9 %attend_backward.14 = (bf16[1024,384]{1,0:T(8,128)(2,1)}, bf16[384,1024]{1,0:T(8,128)(2,1)}) custom-call(s32[6]{0:T(128)} %stack.19.s.refs_0_, bf16[1024,768]{1,0:T(8,128)(2,1)} %convolution_convert_fusion.8.q_ref.k_ref.v_ref.refs_1_.refs_2_.refs_3_, bf16[1024,768]{1,0:T(8,128)(2,1)} %convolution_convert_fusion.8.q_ref.k_ref.v_ref.refs_1_.refs_2_.refs_3_, ...), custom_call_target="tpu_custom_call" | custom-call | flops 200000000 | tf_op jit(solution)/shard_map/attend_backward/pallas_call | solution.py:473
  330.8 13.7 %collective-permute-done.27 = bf16[128,1024]{1,0:T(8,128)(2,1)S(1)} collective-permute-done((bf16[128,1024]{1,0:T(8,128)(2,1)S(1)}, bf16[128,1024]{1,0:T(8,128)(2,1)S(1)}, u32[]{:S(2)}, u32[]{:S(2)}) %collective-permute-start.27) | collective-permute-done | bytes 262176 | tf_op jit(solution)/shard_map/ppermute | solution.py:757
  344.5 6.3 %collective-permute-done.28 = bf16[640,1024]{1,0:T(8,128)(2,1)S(1)} collective-permute-done((bf16[640,1024]{1,0:T(8,128)(2,1)}, bf16[640,1024]{1,0:T(8,128)(2,1)S(1)}, u32[]{:S(2)}, u32[]{:S(2)}) %collective-permute-start.28) | collective-permute-done | bytes 1310752 | tf_op jit(solution)/shard_map/ppermute | solution.py:757
  356.2 10.0 %attend_backward.15 = (bf16[1024,384]{1,0:T(8,128)(2,1)}, bf16[384,1024]{1,0:T(8,128)(2,1)}) custom-call(s32[6]{0:T(128)} %stack.19.s.refs_0_, bf16[1024,768]{1,0:T(8,128)(2,1)} %convolution_convert_fusion.10.q_ref.k_ref.v_ref.refs_1_.refs_2_.refs_3_, bf16[1024,768]{1,0:T(8,128)(2,1)} %convolution_convert_fusion.10.q_ref.k_ref.v_ref.refs_1_.refs_2_.refs_3_, ...), custom_call_target="tpu_custom_call" | custom-call | flops 200000000 | tf_op jit(solution)/shard_map/attend_backward/pallas_call | solution.py:473
  366.3 9.8 %collective-permute-done.30 = bf16[320,1024]{1,0:T(8,128)(2,1)} collective-permute-done((bf16[320,1024]{1,0:T(8,128)(2,1)}, bf16[320,1024]{1,0:T(8,128)(2,1)}, u32[]{:S(2)}, u32[]{:S(2)}) %collective-permute-start.30) | collective-permute-done | bytes 655392 | tf_op jit(solution)/shard_map/ppermute | solution.py:757
  382.8 15.1 %input_back.1 = (f32[1024,1024]{1,0:T(8,128)}, f32[1,1024]{1,0:T(1,128)}, f32[1,1024]{1,0:T(1,128)}) custom-call(s32[6]{0:T(128)} %stack.19.s.refs_0_, bf16[1024,1024]{1,0:T(8,128)(2,1)} %x_ref.5, f32[1024,1024]{1,0:T(8,128)} %get-tuple-element.400.gm_ref, f32[1,1024]{1,0:T(1,128)} %bitcast.50, bf16[1024,384]{1,0:T(8,128)(2,1)} %get-tuple-element.401.refs_0_, ...), custom_call_target="tpu_custom_call" | custom-call | flops 300000000 | tf_op jit(solution)/shard_map/input_back/pallas_call | solution.py:705
  399.1 7.0 %collective-permute-start.35 = (bf16[48,1024]{1,0:T(8,128)(2,1)S(1)}, bf16[48,1024]{1,0:T(8,128)(2,1)S(1)}, u32[]{:S(2)}, u32[]{:S(2)}) collective-permute-start(bf16[48,1024]{1,0:T(8,128)(2,1)S(1)} %get-tuple-element.434), channel_id=1, source_target_pairs={{0,8},{2,10},{4,12},{6,14},{8,0},{10,2},{12,4},{14,6},{16,24},{18,... | collective-permute-start | bytes 294920 | tf_op jit(solution)/shard_map/ppermute | solution.py:757
  413.9 16.0 %project_down.1 = bf16[1024,1024]{1,0:T(8,128)(2,1)} custom-call(s32[6]{0:T(128)} %stack.19.s.refs_0_, f32[1024,1024]{1,0:T(8,128)} %get-tuple-element.433.middle_ref, f32[1,1024]{1,0:T(1,128)} %bitcast.53, bf16[1024,1024]{1,0:T(8,128)(2,1)} %get-tuple-element.277.refs_0_, bf16[1024,1024]{1,0:T(8,128)(2,1)} %get-tuple-element.278.refs_1_, ...), custom_call_target="tpu_custom_call" | custom-call | flops 300000000 | tf_op jit(solution)/shard_map/project_down/pallas_call | solution.py:729
  429.9 12.8 %collective-permute-done.36 = bf16[48,1024]{1,0:T(8,128)(2,1)S(1)} collective-permute-done((bf16[48,1024]{1,0:T(8,128)(2,1)S(1)}, bf16[48,1024]{1,0:T(8,128)(2,1)S(1)}, u32[]{:S(2)}, u32[]{:S(2)}) %collective-permute-start.36) | collective-permute-done | bytes 98336 | tf_op jit(solution)/shard_map/ppermute | solution.py:757
  444.6 5.5 %collective-permute-start.42 = (bf16[48,1024]{1,0:T(8,128)(2,1)S(1)}, bf16[48,1024]{1,0:T(8,128)(2,1)S(1)}, u32[]{:S(2)}, u32[]{:S(2)}) collective-permute-start(bf16[48,1024]{1,0:T(8,128)(2,1)S(1)} %add_convert_fusion.29), channel_id=1, source_target_pairs={{0,8},{2,10},{4,12},{6,14},{8,0},{10,2},{12,4},{14,6},{16,24},{18,... | collective-permute-start | bytes 294920 | tf_op jit(solution)/shard_map/ppermute | solution.py:757
  454.1 6.5 %spread.2 = f32[2048,1024]{1,0:T(8,128)} custom-call(s32[6]{0:T(128)} %stack.19.s.refs_0_, bf16[2048,1024]{1,0:T(8,128)(2,1)} %all-gather.3.cloned.1.call-done.refs_0_.refs_1_.refs_2_.refs_3_, bf16[2048,1024]{1,0:T(8,128)(2,1)} %all-gather.3.cloned.1.call-done.refs_0_.refs_1_.refs_2_.refs_3_, ...), custom_call_target="tpu_custom_call" | custom-call | flops 80000000 | tf_op jit(solution)/shard_map/spread/pallas_call | solution.py:889
  463.1 6.5 %spread.3 = f32[1024,2048]{1,0:T(8,128)} custom-call(s32[6]{0:T(128)} %stack.19.s.refs_0_, bf16[2048,1024]{1,0:T(8,128)(2,1)} %all-gather.5.cloned.1.call-done.refs_0_.refs_1_.refs_2_.refs_3_, bf16[2048,1024]{1,0:T(8,128)(2,1)} %all-gather.5.cloned.1.call-done.refs_0_.refs_1_.refs_2_.refs_3_, ...), custom_call_target="tpu_custom_call" | custom-call | flops 80000000 | tf_op jit(solution)/shard_map/spread/pallas_call | solution.py:889
  469.6 4.3 collective-permute-done.49
  475.3 3.3 collective-permute-done.50
  480.6 4.0 collective-permute-done.51
  486.8 6.6 %spread_joined.1 = (f32[1024,512]{1,0:T(8,128)}, f32[1024,512]{1,0:T(8,128)}, f32[1024,512]{1,0:T(8,128)}, f32[512,1024]{1,0:T(8,128)}) custom-call(s32[6]{0:T(128)} %stack.19.s.refs_0_, bf16[640,1024]{1,0:T(8,128)(2,1)} %copy-done.12, bf16[640,1024]{1,0:T(8,128)(2,1)} %copy-done.34, bf16[384,1024]{1,0:T(8,128)(2,1)} %copy-done.16, bf16[384,1024]{1,0:T(8,128)(2,1)} %copy-done.40), custom_call_target="tpu_custom_call" | custom-call | flops 80000000 | tf_op jit(solution)/shard_map/spread_joined/pallas_call | solution.py:926
  (270 shorter events, 104.4 us)
Async XLA Ops:
  7.2 446.9 %all-gather.3.cloned.1.call-start = ((), (), s32[]{:S(2)}) async-start(), calls=%async_computation | async-start | bytes 4456448 | tf_op jit(solution)/shard_map/all_gather | solution.py:1119
  7.2 19.8 %collective-permute-start.3 = (s32[8,16,3]{1,0,2:T(8,128)}, s32[8,16,3]{1,0,2:T(8,128)S(1)}, u32[]{:S(2)}, u32[]{:S(2)}) collective-permute-start(s32[8,16,3]{1,0,2:T(8,128)} %param.29), channel_id=1, source_target_pairs={{0,1},{1,0},{2,3},{3,2},{4,5},{5,4},{6,7},{7,6},{8,9},{9,8},{10,11... | collective-permute-start | bytes 4616 | tf_op jit(solution)/shard_map/ppermute | solution.py:757
  14.8 36.2 %collective-permute-start = (bf16[1024,768]{1,0:T(8,128)(2,1)}, bf16[1024,768]{1,0:T(8,128)(2,1)}, u32[]{:S(2)}, u32[]{:S(2)}) collective-permute-start(bf16[1024,768]{1,0:T(8,128)(2,1)} %pad_maximum_fusion.2.refs_8_), channel_id=1, source_target_pairs={{0,1},{1,0},{2,3},{3,2},{4,5},{5,4},{6,7},{7,6},{8,9},{9,8},{10,11... | collective-permute-start | bytes 4718600 | tf_op jit(solution)/shard_map/ppermute | solution.py:757
  51.0 16.0 %collective-permute-start.1 = (bf16[1024,768]{1,0:T(8,128)(2,1)}, bf16[1024,768]{1,0:T(8,128)(2,1)}, u32[]{:S(2)}, u32[]{:S(2)}) collective-permute-start(bf16[1024,768]{1,0:T(8,128)(2,1)} %collective-permute-done.refs_10_), channel_id=1, source_target_pairs={{0,2},{2,0},{4,6},{6,4},{8,10},{10,8},{12,14},{14,12},{16,18},{18,... | collective-permute-start | bytes 4718600 | tf_op jit(solution)/shard_map/ppermute | solution.py:757
  51.0 16.0 %collective-permute-start.2 = (bf16[256,1024]{1,0:T(8,128)(2,1)S(1)}, bf16[256,1024]{1,0:T(8,128)(2,1)}, u32[]{:S(2)}, u32[]{:S(2)}) collective-permute-start(bf16[256,1024]{1,0:T(8,128)(2,1)S(1)} %copy-done.44), channel_id=1, source_target_pairs={{0,1},{1,0},{2,3},{3,2},{4,5},{5,4},{6,7},{7,6},{8,9},{9,8},{10,11... | collective-permute-start | bytes 1572872 | tf_op jit(solution)/shard_map/ppermute | solution.py:757
  67.0 26.8 %collective-permute-start.5 = (bf16[1024,512]{1,0:T(8,128)(2,1)}, bf16[1024,512]{1,0:T(8,128)(2,1)S(1)}, u32[]{:S(2)}, u32[]{:S(2)}) collective-permute-start(bf16[1024,512]{1,0:T(8,128)(2,1)} %constant_dynamic-slice_fusion.2), channel_id=1, source_target_pairs={{0,1},{1,0},{2,3},{3,2},{4,5},{5,4},{6,7},{7,6},{8,9},{9,8},{10,11... | collective-permute-start | bytes 3145736 | tf_op jit(solution)/shard_map/ppermute | solution.py:757
  68.7 16.2 %collective-permute-start.4 = (bf16[256,1024]{1,0:T(8,128)(2,1)}, bf16[256,1024]{1,0:T(8,128)(2,1)S(1)}, u32[]{:S(2)}, u32[]{:S(2)}) collective-permute-start(bf16[256,1024]{1,0:T(8,128)(2,1)} %collective-permute-done.2.refs_6_.refs_14_), channel_id=1, source_target_pairs={{0,2},{2,0},{4,6},{6,4},{8,10},{10,8},{12,14},{14,12},{16,18},{18,... | collective-permute-start | bytes 1572872 | tf_op jit(solution)/shard_map/ppermute | solution.py:757
  93.8 25.7 %collective-permute-start.6 = (bf16[1024,512]{1,0:T(8,128)(2,1)S(1)}, bf16[1024,512]{1,0:T(8,128)(2,1)}, u32[]{:S(2)}, u32[]{:S(2)}) collective-permute-start(bf16[1024,512]{1,0:T(8,128)(2,1)S(1)} %collective-permute-done.5.refs_4_.refs_8_), channel_id=1, source_target_pairs={{0,4},{2,6},{4,0},{6,2},{8,12},{10,14},{12,8},{14,10},{16,20},{18,... | collective-permute-start | bytes 3145736 | tf_op jit(solution)/shard_map/ppermute | solution.py:757
  95.4 48.0 %collective-permute-start.7 = (bf16[1024,1024]{1,0:T(8,128)(2,1)}, bf16[1024,1024]{1,0:T(8,128)(2,1)S(1)}, u32[]{:S(2)}, u32[]{:S(2)}) collective-permute-start(bf16[1024,1024]{1,0:T(8,128)(2,1)} %constant_dynamic-slice_fusion.1), channel_id=1, source_target_pairs={{0,1},{1,0},{2,3},{3,2},{4,5},{5,4},{6,7},{7,6},{8,9},{9,8},{10,11... | collective-permute-start | bytes 6291464 | tf_op jit(solution)/shard_map/ppermute | solution.py:757
  119.6 23.8 %collective-permute-start.8 = (bf16[1024,512]{1,0:T(8,128)(2,1)S(1)}, bf16[1024,512]{1,0:T(8,128)(2,1)S(1)}, u32[]{:S(2)}, u32[]{:S(2)}) collective-permute-start(bf16[1024,512]{1,0:T(8,128)(2,1)S(1)} %collective-permute-done.5.refs_4_.refs_8_), channel_id=1, source_target_pairs={{0,2},{2,0},{4,6},{6,4},{8,10},{10,8},{12,14},{14,12},{16,18},{18,... | collective-permute-start | bytes 3145736 | tf_op jit(solution)/shard_map/ppermute | solution.py:757
  119.6 24.8 %collective-permute-start.9 = (bf16[1024,512]{1,0:T(8,128)(2,1)}, bf16[1024,512]{1,0:T(8,128)(2,1)S(1)}, u32[]{:S(2)}, u32[]{:S(2)}) collective-permute-start(bf16[1024,512]{1,0:T(8,128)(2,1)} %collective-permute-done.6.refs_5_.refs_9_), channel_id=1, source_target_pairs={{0,2},{2,0},{4,6},{6,4},{8,10},{10,8},{12,14},{14,12},{16,18},{18,... | collective-permute-start | bytes 3145736 | tf_op jit(solution)/shard_map/ppermute | solution.py:757
  145.4 15.8 %collective-permute-start.10 = (bf16[1024,1024]{1,0:T(8,128)(2,1)S(1)}, bf16[1024,1024]{1,0:T(8,128)(2,1)S(1)}, u32[]{:S(2)}, u32[]{:S(2)}) collective-permute-start(bf16[1024,1024]{1,0:T(8,128)(2,1)S(1)} %collective-permute-done.7.refs_6_), channel_id=1, source_target_pairs={{0,2},{2,0},{4,6},{6,4},{8,10},{10,8},{12,14},{14,12},{16,18},{18,... | collective-permute-start | bytes 6291464 | tf_op jit(solution)/shard_map/ppermute | solution.py:757
  145.4 15.8 %collective-permute-start.11 = (bf16[1024,1024]{1,0:T(8,128)(2,1)}, bf16[1024,1024]{1,0:T(8,128)(2,1)S(1)}, u32[]{:S(2)}, u32[]{:S(2)}) collective-permute-start(bf16[1024,1024]{1,0:T(8,128)(2,1)} %convolution_convert_fusion.5), channel_id=1, source_target_pairs={{0,2},{2,0},{4,6},{6,4},{8,10},{10,8},{12,14},{14,12},{16,18},{18,... | collective-permute-start | bytes 6291464 | tf_op jit(solution)/shard_map/ppermute | solution.py:757
  145.9 15.3 %collective-permute-start.12 = (bf16[1024,1024]{1,0:T(8,128)(2,1)}, bf16[1024,1024]{1,0:T(8,128)(2,1)}, u32[]{:S(2)}, u32[]{:S(2)}) collective-permute-start(bf16[1024,1024]{1,0:T(8,128)(2,1)} %convolution_convert_fusion.3), channel_id=1, source_target_pairs={{0,2},{2,0},{4,6},{6,4},{8,10},{10,8},{12,14},{14,12},{16,18},{18,... | collective-permute-start | bytes 6291464 | tf_op jit(solution)/shard_map/ppermute | solution.py:757
  183.8 14.2 %collective-permute-start.15 = (bf16[1024,1024]{1,0:T(8,128)(2,1)}, bf16[1024,1024]{1,0:T(8,128)(2,1)}, u32[]{:S(2)}, u32[]{:S(2)}) collective-permute-start(bf16[1024,1024]{1,0:T(8,128)(2,1)} %convolution_convert_fusion.1), channel_id=1, source_target_pairs={{0,2},{2,0},{4,6},{6,4},{8,10},{10,8},{12,14},{14,12},{16,18},{18,... | collective-permute-start | bytes 6291464 | tf_op jit(solution)/shard_map/ppermute | solution.py:757
  202.6 47.9 %collective-permute-start.18 = (bf16[1024,1024]{1,0:T(8,128)(2,1)}, bf16[1024,1024]{1,0:T(8,128)(2,1)}, u32[]{:S(2)}, u32[]{:S(2)}) collective-permute-start(bf16[1024,1024]{1,0:T(8,128)(2,1)} %pad_maximum_fusion.1), channel_id=1, source_target_pairs={{0,8},{2,10},{4,12},{6,14},{8,0},{10,2},{12,4},{14,6},{16,24},{18,... | collective-permute-start | bytes 6291464 | tf_op jit(solution)/shard_map/ppermute | solution.py:757
  204.3 47.6 %collective-permute-start.17 = (bf16[1024,1024]{1,0:T(8,128)(2,1)}, bf16[1024,1024]{1,0:T(8,128)(2,1)}, u32[]{:S(2)}, u32[]{:S(2)}) collective-permute-start(bf16[1024,1024]{1,0:T(8,128)(2,1)} %add_convert_fusion), channel_id=1, source_target_pairs={{0,1},{1,0},{2,3},{3,2},{4,5},{5,4},{6,7},{7,6},{8,9},{9,8},{10,11... | collective-permute-start | bytes 6291464 | tf_op jit(solution)/shard_map/ppermute | solution.py:757
  236.9 11.1 %collective-permute-start.16 = (bf16[640,1024]{1,0:T(8,128)(2,1)}, bf16[640,1024]{1,0:T(8,128)(2,1)S(1)}, u32[]{:S(2)}, u32[]{:S(2)}) collective-permute-start(bf16[640,1024]{1,0:T(8,128)(2,1)} %get-tuple-element.329), channel_id=1, source_target_pairs={{0,2},{2,0},{4,6},{6,4},{8,10},{10,8},{12,14},{14,12},{16,18},{18,... | collective-permute-start | bytes 3932168 | tf_op jit(solution)/shard_map/ppermute | solution.py:757
  259.0 11.6 %collective-permute-start.19 = (bf16[640,1024]{1,0:T(8,128)(2,1)}, bf16[640,1024]{1,0:T(8,128)(2,1)}, u32[]{:S(2)}, u32[]{:S(2)}) collective-permute-start(bf16[640,1024]{1,0:T(8,128)(2,1)} %get-tuple-element.344), channel_id=1, source_target_pairs={{0,2},{2,0},{4,6},{6,4},{8,10},{10,8},{12,14},{14,12},{16,18},{18,... | collective-permute-start | bytes 3932168 | tf_op jit(solution)/shard_map/ppermute | solution.py:757
  259.0 25.8 %collective-permute-start.20 = (bf16[512,1024]{1,0:T(8,128)(2,1)}, bf16[512,1024]{1,0:T(8,128)(2,1)S(1)}, u32[]{:S(2)}, u32[]{:S(2)}) collective-permute-start(bf16[512,1024]{1,0:T(8,128)(2,1)} %get-tuple-element.349), channel_id=1, source_target_pairs={{0,4},{2,6},{4,0},{6,2},{8,12},{10,14},{12,8},{14,10},{16,20},{18,... | collective-permute-start | bytes 3145736 | tf_op jit(solution)/shard_map/ppermute | solution.py:757
  259.5 25.6 %collective-permute-start.21 = (bf16[512,1024]{1,0:T(8,128)(2,1)}, bf16[512,1024]{1,0:T(8,128)(2,1)}, u32[]{:S(2)}, u32[]{:S(2)}) collective-permute-start(bf16[512,1024]{1,0:T(8,128)(2,1)} %get-tuple-element.350), channel_id=1, source_target_pairs={{0,1},{1,0},{2,3},{3,2},{4,5},{5,4},{6,7},{7,6},{8,9},{9,8},{10,11... | collective-permute-start | bytes 3145736 | tf_op jit(solution)/shard_map/ppermute | solution.py:757
  288.6 13.7 %collective-permute-start.22 = (bf16[256,1024]{1,0:T(8,128)(2,1)S(1)}, bf16[256,1024]{1,0:T(8,128)(2,1)S(1)}, u32[]{:S(2)}, u32[]{:S(2)}) collective-permute-start(bf16[256,1024]{1,0:T(8,128)(2,1)S(1)} %get-tuple-element.359), channel_id=1, source_target_pairs={{0,8},{2,10},{4,12},{6,14},{8,0},{10,2},{12,4},{14,6},{16,24},{18,... | collective-permute-start | bytes 1572872 | tf_op jit(solution)/shard_map/ppermute | solution.py:757
  289.2 13.6 %collective-permute-start.23 = (bf16[256,1024]{1,0:T(8,128)(2,1)}, bf16[256,1024]{1,0:T(8,128)(2,1)S(1)}, u32[]{:S(2)}, u32[]{:S(2)}) collective-permute-start(bf16[256,1024]{1,0:T(8,128)(2,1)} %get-tuple-element.360), channel_id=1, source_target_pairs={{0,4},{2,6},{4,0},{6,2},{8,12},{10,14},{12,8},{14,10},{16,20},{18,... | collective-permute-start | bytes 1572872 | tf_op jit(solution)/shard_map/ppermute | solution.py:757
  304.0 15.3 %collective-permute-start.24 = (bf16[384,1024]{1,0:T(8,128)(2,1)S(1)}, bf16[384,1024]{1,0:T(8,128)(2,1)S(1)}, u32[]{:S(2)}, u32[]{:S(2)}) collective-permute-start(bf16[384,1024]{1,0:T(8,128)(2,1)S(1)} %copy-done.58), channel_id=1, source_target_pairs={{0,2},{2,0},{4,6},{6,4},{8,10},{10,8},{12,14},{14,12},{16,18},{18,... | collective-permute-start | bytes 2359304 | tf_op jit(solution)/shard_map/ppermute | solution.py:757
  304.0 15.2 %collective-permute-start.25 = (bf16[128,1024]{1,0:T(8,128)(2,1)S(1)}, bf16[128,1024]{1,0:T(8,128)(2,1)S(1)}, u32[]{:S(2)}, u32[]{:S(2)}) collective-permute-start(bf16[128,1024]{1,0:T(8,128)(2,1)S(1)} %get-tuple-element.370), channel_id=1, source_target_pairs={{0,16},{2,18},{4,20},{6,22},{8,24},{10,26},{12,28},{14,30},{16,0},... | collective-permute-start | bytes 786440 | tf_op jit(solution)/shard_map/ppermute | solution.py:757
  320.2 140.5 %all-gather.5.cloned.1.call-start = ((), (), s32[]{:S(2)}) async-start(), calls=%async_computation.1 | async-start | bytes 4456448 | tf_op jit(solution)/shard_map/all_gather | solution.py:1124
  320.2 30.6 %collective-permute-start.28 = (bf16[640,1024]{1,0:T(8,128)(2,1)}, bf16[640,1024]{1,0:T(8,128)(2,1)S(1)}, u32[]{:S(2)}, u32[]{:S(2)}) collective-permute-start(bf16[640,1024]{1,0:T(8,128)(2,1)} %get-tuple-element.383), channel_id=1, source_target_pairs={{0,1},{1,0},{2,3},{3,2},{4,5},{5,4},{6,7},{7,6},{8,9},{9,8},{10,11... | collective-permute-start | bytes 3932168 | tf_op jit(solution)/shard_map/ppermute | solution.py:757
  320.8 30.0 %collective-permute-start.26 = (bf16[384,1024]{1,0:T(8,128)(2,1)}, bf16[384,1024]{1,0:T(8,128)(2,1)S(1)}, u32[]{:S(2)}, u32[]{:S(2)}) collective-permute-start(bf16[384,1024]{1,0:T(8,128)(2,1)} %get-tuple-element.381), channel_id=1, source_target_pairs={{0,2},{2,0},{4,6},{6,4},{8,10},{10,8},{12,14},{14,12},{16,18},{18,... | collective-permute-start | bytes 2359304 | tf_op jit(solution)/shard_map/ppermute | solution.py:757
  320.8 23.7 %collective-permute-start.27 = (bf16[128,1024]{1,0:T(8,128)(2,1)S(1)}, bf16[128,1024]{1,0:T(8,128)(2,1)S(1)}, u32[]{:S(2)}, u32[]{:S(2)}) collective-permute-start(bf16[128,1024]{1,0:T(8,128)(2,1)S(1)} %copy-done.47), channel_id=1, source_target_pairs={{0,16},{2,18},{4,20},{6,22},{8,24},{10,26},{12,28},{14,30},{16,0},... | collective-permute-start | bytes 786440 | tf_op jit(solution)/shard_map/ppermute | solution.py:757
  353.9 22.1 %collective-permute-start.29 = (bf16[384,1024]{1,0:T(8,128)(2,1)}, bf16[384,1024]{1,0:T(8,128)(2,1)S(1)}, u32[]{:S(2)}, u32[]{:S(2)}) collective-permute-start(bf16[384,1024]{1,0:T(8,128)(2,1)} %get-tuple-element.394), channel_id=1, source_target_pairs={{0,1},{1,0},{2,3},{3,2},{4,5},{5,4},{6,7},{7,6},{8,9},{9,8},{10,11... | collective-permute-start | bytes 2359304 | tf_op jit(solution)/shard_map/ppermute | solution.py:757
  354.5 21.5 %collective-permute-start.30 = (bf16[320,1024]{1,0:T(8,128)(2,1)}, bf16[320,1024]{1,0:T(8,128)(2,1)}, u32[]{:S(2)}, u32[]{:S(2)}) collective-permute-start(bf16[320,1024]{1,0:T(8,128)(2,1)} %get-tuple-element.395), channel_id=1, source_target_pairs={{0,4},{2,6},{4,0},{6,2},{8,12},{10,14},{12,8},{14,10},{16,20},{18,... | collective-permute-start | bytes 1966088 | tf_op jit(solution)/shard_map/ppermute | solution.py:757
  377.9 20.9 %collective-permute-start.31 = (bf16[192,1024]{1,0:T(8,128)(2,1)S(1)}, bf16[192,1024]{1,0:T(8,128)(2,1)S(1)}, u32[]{:S(2)}, u32[]{:S(2)}) collective-permute-start(bf16[192,1024]{1,0:T(8,128)(2,1)S(1)} %get-tuple-element.410), channel_id=1, source_target_pairs={{0,4},{2,6},{4,0},{6,2},{8,12},{10,14},{12,8},{14,10},{16,20},{18,... | collective-permute-start | bytes 1179656 | tf_op jit(solution)/shard_map/ppermute | solution.py:757
  378.2 20.6 %collective-permute-start.32 = (bf16[80,1024]{1,0:T(8,128)(2,1)S(1)}, bf16[80,1024]{1,0:T(8,128)(2,1)S(1)}, u32[]{:S(2)}, u32[]{:S(2)}) collective-permute-start(bf16[80,1024]{1,0:T(8,128)(2,1)S(1)} %get-tuple-element.411), channel_id=1, source_target_pairs={{0,8},{2,10},{4,12},{6,14},{8,0},{10,2},{12,4},{14,6},{16,24},{18,... | collective-permute-start | bytes 491528 | tf_op jit(solution)/shard_map/ppermute | solution.py:757
  380.0 18.8 %collective-permute-start.33 = (bf16[80,1024]{1,0:T(8,128)(2,1)S(1)}, bf16[80,1024]{1,0:T(8,128)(2,1)S(1)}, u32[]{:S(2)}, u32[]{:S(2)}) collective-permute-start(bf16[80,1024]{1,0:T(8,128)(2,1)S(1)} %get-tuple-element.412), channel_id=1, source_target_pairs={{0,16},{2,18},{4,20},{6,22},{8,24},{10,26},{12,28},{14,30},{16,0},... | collective-permute-start | bytes 491528 | tf_op jit(solution)/shard_map/ppermute | solution.py:757
  382.5 16.3 %collective-permute-start.34 = (bf16[80,1024]{1,0:T(8,128)(2,1)S(1)}, bf16[80,1024]{1,0:T(8,128)(2,1)S(1)}, u32[]{:S(2)}, u32[]{:S(2)}) collective-permute-start(bf16[80,1024]{1,0:T(8,128)(2,1)S(1)} %get-tuple-element.413), channel_id=1, source_target_pairs={{0,24},{2,26},{4,28},{6,30},{8,16},{10,18},{12,20},{14,22},{16,8},... | collective-permute-start | bytes 491528 | tf_op jit(solution)/shard_map/ppermute | solution.py:757
  399.1 12.6 %collective-permute-start.35 = (bf16[48,1024]{1,0:T(8,128)(2,1)S(1)}, bf16[48,1024]{1,0:T(8,128)(2,1)S(1)}, u32[]{:S(2)}, u32[]{:S(2)}) collective-permute-start(bf16[48,1024]{1,0:T(8,128)(2,1)S(1)} %get-tuple-element.434), channel_id=1, source_target_pairs={{0,8},{2,10},{4,12},{6,14},{8,0},{10,2},{12,4},{14,6},{16,24},{18,... | collective-permute-start | bytes 294920 | tf_op jit(solution)/shard_map/ppermute | solution.py:757
  406.1 36.6 %collective-permute-start.38 = (bf16[80,1024]{1,0:T(8,128)(2,1)S(1)}, bf16[80,1024]{1,0:T(8,128)(2,1)S(1)}, u32[]{:S(2)}, u32[]{:S(2)}) collective-permute-start(bf16[80,1024]{1,0:T(8,128)(2,1)S(1)} %add_convert_fusion.24), channel_id=1, source_target_pairs={{0,8},{2,10},{4,12},{6,14},{8,0},{10,2},{12,4},{14,6},{16,24},{18,... | collective-permute-start | bytes 491528 | tf_op jit(solution)/shard_map/ppermute | solution.py:757
  406.1 36.5 %collective-permute-start.39 = (bf16[80,1024]{1,0:T(8,128)(2,1)S(1)}, bf16[80,1024]{1,0:T(8,128)(2,1)S(1)}, u32[]{:S(2)}, u32[]{:S(2)}) collective-permute-start(bf16[80,1024]{1,0:T(8,128)(2,1)S(1)} %add_convert_fusion.24), channel_id=1, source_target_pairs={{0,16},{2,18},{4,20},{6,22},{8,24},{10,26},{12,28},{14,30},{16,0},... | collective-permute-start | bytes 491528 | tf_op jit(solution)/shard_map/ppermute | solution.py:757
  408.7 34.0 %collective-permute-start.40 = (bf16[80,1024]{1,0:T(8,128)(2,1)S(1)}, bf16[80,1024]{1,0:T(8,128)(2,1)S(1)}, u32[]{:S(2)}, u32[]{:S(2)}) collective-permute-start(bf16[80,1024]{1,0:T(8,128)(2,1)S(1)} %add_convert_fusion.24), channel_id=1, source_target_pairs={{0,24},{2,26},{4,28},{6,30},{8,16},{10,18},{12,20},{14,22},{16,8},... | collective-permute-start | bytes 491528 | tf_op jit(solution)/shard_map/ppermute | solution.py:757
  411.7 31.0 %collective-permute-start.36 = (bf16[48,1024]{1,0:T(8,128)(2,1)S(1)}, bf16[48,1024]{1,0:T(8,128)(2,1)S(1)}, u32[]{:S(2)}, u32[]{:S(2)}) collective-permute-start(bf16[48,1024]{1,0:T(8,128)(2,1)S(1)} %get-tuple-element.435), channel_id=1, source_target_pairs={{0,16},{2,18},{4,20},{6,22},{8,24},{10,26},{12,28},{14,30},{16,0},... | collective-permute-start | bytes 294920 | tf_op jit(solution)/shard_map/ppermute | solution.py:757
  411.7 31.0 %collective-permute-start.37 = (bf16[48,1024]{1,0:T(8,128)(2,1)S(1)}, bf16[48,1024]{1,0:T(8,128)(2,1)S(1)}, u32[]{:S(2)}, u32[]{:S(2)}) collective-permute-start(bf16[48,1024]{1,0:T(8,128)(2,1)S(1)} %get-tuple-element.436), channel_id=1, source_target_pairs={{0,24},{2,26},{4,28},{6,30},{8,16},{10,18},{12,20},{14,22},{16,8},... | collective-permute-start | bytes 294920 | tf_op jit(solution)/shard_map/ppermute | solution.py:757
  442.8 17.9 %collective-permute-start.45 = (bf16[320,1024]{1,0:T(8,128)(2,1)S(1)}, bf16[320,1024]{1,0:T(8,128)(2,1)S(1)}, u32[]{:S(2)}, u32[]{:S(2)}) collective-permute-start(bf16[320,1024]{1,0:T(8,128)(2,1)S(1)} %pad_maximum_fusion.6), channel_id=1, source_target_pairs={{0,4},{2,6},{4,0},{6,2},{8,12},{10,14},{12,8},{14,10},{16,20},{18,... | collective-permute-start | bytes 1966088 | tf_op jit(solution)/shard_map/ppermute | solution.py:757
  444.6 16.1 %collective-permute-start.42 = (bf16[48,1024]{1,0:T(8,128)(2,1)S(1)}, bf16[48,1024]{1,0:T(8,128)(2,1)S(1)}, u32[]{:S(2)}, u32[]{:S(2)}) collective-permute-start(bf16[48,1024]{1,0:T(8,128)(2,1)S(1)} %add_convert_fusion.29), channel_id=1, source_target_pairs={{0,8},{2,10},{4,12},{6,14},{8,0},{10,2},{12,4},{14,6},{16,24},{18,... | collective-permute-start | bytes 294920 | tf_op jit(solution)/shard_map/ppermute | solution.py:757
  450.1 10.5 %collective-permute-start.43 = (bf16[48,1024]{1,0:T(8,128)(2,1)S(1)}, bf16[48,1024]{1,0:T(8,128)(2,1)S(1)}, u32[]{:S(2)}, u32[]{:S(2)}) collective-permute-start(bf16[48,1024]{1,0:T(8,128)(2,1)S(1)} %add_convert_fusion.29), channel_id=1, source_target_pairs={{0,16},{2,18},{4,20},{6,22},{8,24},{10,26},{12,28},{14,30},{16,0},... | collective-permute-start | bytes 294920 | tf_op jit(solution)/shard_map/ppermute | solution.py:757
  460.9 13.0 %collective-permute-start.47 = (bf16[640,1024]{1,0:T(8,128)(2,1)S(1)}, bf16[640,1024]{1,0:T(8,128)(2,1)S(1)}, u32[]{:S(2)}, u32[]{:S(2)}) collective-permute-start(bf16[640,1024]{1,0:T(8,128)(2,1)S(1)} %pad_maximum_fusion.4.one_a), channel_id=1, source_target_pairs={{0,2},{2,0},{4,6},{6,4},{8,10},{10,8},{12,14},{14,12},{16,18},{18,... | collective-permute-start | bytes 3932168 | tf_op jit(solution)/shard_map/ppermute | solution.py:757
  461.0 12.9 %collective-permute-start.48 = (bf16[192,1024]{1,0:T(8,128)(2,1)S(1)}, bf16[192,1024]{1,0:T(8,128)(2,1)S(1)}, u32[]{:S(2)}, u32[]{:S(2)}) collective-permute-start(bf16[192,1024]{1,0:T(8,128)(2,1)S(1)} %pad_maximum_fusion.7), channel_id=1, source_target_pairs={{0,4},{2,6},{4,0},{6,2},{8,12},{10,14},{12,8},{14,10},{16,20},{18,... | collective-permute-start | bytes 1179656 | tf_op jit(solution)/shard_map/ppermute | solution.py:757
  461.2 12.7 %collective-permute-start.49 = (f32[9,1024]{1,0:T(8,128)S(1)}, f32[9,1024]{1,0:T(8,128)S(1)}, u32[]{:S(2)}, u32[]{:S(2)}) collective-permute-start(f32[9,1024]{1,0:T(8,128)S(1)} %add.347), channel_id=1, source_target_pairs={{0,4},{2,6},{4,0},{6,2},{8,12},{10,14},{12,8},{14,10},{16,20},{18,... | collective-permute-start | bytes 110600 | tf_op jit(solution)/shard_map/ppermute | solution.py:757
  474.0 11.9 %collective-permute-start.52 = (bf16[384,1024]{1,0:T(8,128)(2,1)S(1)}, bf16[384,1024]{1,0:T(8,128)(2,1)S(1)}, u32[]{:S(2)}, u32[]{:S(2)}) collective-permute-start(bf16[384,1024]{1,0:T(8,128)(2,1)S(1)} %pad_maximum_fusion.5.two_a), channel_id=1, source_target_pairs={{0,2},{2,0},{4,6},{6,4},{8,10},{10,8},{12,14},{14,12},{16,18},{18,... | collective-permute-start | bytes 2359304 | tf_op jit(solution)/shard_map/ppermute | solution.py:757
  (66 other events, 456.3 us)
Sparse Core Ops, SparseCore 0:
  320.3 58.8 all-gather.2
  381.3 66.6 all-gather.4
